TPU v7x, 32 devices: a whole 2x2x4 slice. The times are simulated.
32 devices in a mesh: rep: 4 (over x, core), shard: 8 (over z, y).
Axes of the slice: x: 2, y: 2, z: 4, core: 2. Of those that a mesh axis runs over, the one named last changes fastest.
Arguments:
- tokens: bfloat16 [8192, 768], P(('rep', 'shard')), may hold values from -6 to 6
- letters: bfloat16 [8192, 8, 768], P(('rep', 'shard')), may hold values from -6 to 6
- lengths: int32 [32], P(('rep', 'shard')), may hold values from 64 to 256, as said below
- counts: int32 [8192], P(('rep', 'shard')), may hold values from 1 to 8, as said below
- cot_token: bfloat16 [8192, 768], P(('rep', 'shard')), may hold values from -6 to 6
- cot_letter: bfloat16 [8192, 768], P(('rep', 'shard')), may hold values from -6 to 6
- project_weight: bfloat16 [768, 2304], P('shard'), may hold values from -0.21875 to 0.21875
- project_bias: bfloat16 [1536], P('shard'), may hold values from -1.75 to 1.75
- output_weight: bfloat16 [768, 768], P('shard'), may hold values from -1.5 to 1.5
- output_bias: bfloat16 [768], P('shard'), may hold values from -1.75 to 1.75
- first_gain: bfloat16 [768], P('shard'), may hold values from 0.5 to 1.5
- first_shift: bfloat16 [768], P('shard'), may hold values from -1.75 to 1.75
- up_weight: bfloat16 [768, 3072], P('shard'), may hold values from -0.21875 to 0.21875
- up_bias: bfloat16 [3072], P('shard'), may hold values from -1.75 to 1.75
- down_weight: bfloat16 [3072, 768], P('shard'), may hold values from -0.109375 to 0.109375
- down_bias: bfloat16 [768], P('shard'), may hold values from -1.75 to 1.75
- second_gain: bfloat16 [768], P('shard'), may hold values from 0.5 to 1.5
- second_shift: bfloat16 [768], P('shard'), may hold values from -1.75 to 1.75
- gates_input: bfloat16 [2, 768, 1152], P(None, 'shard'), may hold values from -0.21875 to 0.21875
- gates_hidden: bfloat16 [2, 384, 1152], P(None, 'shard'), may hold values from -0.3125 to 0.3125
- shift_input: bfloat16 [2, 1152], P(None, 'shard'), may hold values from -1.75 to 1.75
- shift_hidden: bfloat16 [2, 1152], P(None, 'shard'), may hold values from -1.75 to 1.75
- token_mixer: bfloat16 [768, 768], P('shard'), may hold values from -0.21875 to 0.21875
- token_offset: bfloat16 [768], P('shard'), may hold values from -1.75 to 1.75
- letter_mixer: bfloat16 [768, 768], P('shard'), may hold values from -0.21875 to 0.21875
- letter_offset: bfloat16 [768], P('shard'), may hold values from -1.75 to 1.75
- window_kernel: bfloat16 [3, 1536, 1536], P(None, 'shard'), may hold values from -0.09375 to 0.09375
- window_offset: bfloat16 [1536], P('shard'), may hold values from -1.75 to 1.75
- third_gain: bfloat16 [768], P('shard'), may hold values from 0.5 to 1.5
- third_shift: bfloat16 [768], P('shard'), may hold values from -1.75 to 1.75
- fourth_gain: bfloat16 [768], P('shard'), may hold values from 0.5 to 1.5
- fourth_shift: bfloat16 [768], P('shard'), may hold values from -1.75 to 1.75
Outputs:
- token_out: bfloat16 [8192, 768], P(('rep', 'shard'))
- letter_out: bfloat16 [8192, 768], P(('rep', 'shard'))
- tokens_grad: bfloat16 [8192, 768], P(('rep', 'shard'))
- letters_grad: bfloat16 [8192, 8, 768], P(('rep', 'shard'))
- project_weight_grad: float32 [768, 2304], P('shard')
- project_bias_grad: float32 [1536], P('shard')
- output_weight_grad: float32 [768, 768], P('shard')
- output_bias_grad: float32 [768], P('shard')
- first_gain_grad: float32 [768], P('shard')
- first_shift_grad: float32 [768], P('shard')
- up_weight_grad: float32 [768, 3072], P('shard')
- up_bias_grad: float32 [3072], P('shard')
- down_weight_grad: float32 [3072, 768], P('shard')
- down_bias_grad: float32 [768], P('shard')
- second_gain_grad: float32 [768], P('shard')
- second_shift_grad: float32 [768], P('shard')
- gates_input_grad: float32 [2, 768, 1152], P(None, 'shard')
- gates_hidden_grad: float32 [2, 384, 1152], P(None, 'shard')
- shift_input_grad: float32 [2, 1152], P(None, 'shard')
- shift_hidden_grad: float32 [2, 1152], P(None, 'shard')
- token_mixer_grad: float32 [768, 768], P('shard')
- token_offset_grad: float32 [768], P('shard')
- letter_mixer_grad: float32 [768, 768], P('shard')
- letter_offset_grad: float32 [768], P('shard')
- window_kernel_grad: float32 [3, 1536, 1536], P(None, 'shard')
- window_offset_grad: float32 [1536], P('shard')
- third_gain_grad: float32 [768], P('shard')
- third_shift_grad: float32 [768], P('shard')
- fourth_gain_grad: float32 [768], P('shard')
- fourth_shift_grad: float32 [768], P('shard')
Inputs may be any that keep to these rules, and one draw needn't show every extreme that they name: `lengths`: each sequence has at least 64 valid tokens, the first ones of its slots; the first sequence is full. `counts`: A token's characters fill its first slots; the first token of all has 8. Counts are given for padded tokens too.
All inputs are finite; a program needn't handle non-finite values.
Results may differ from a plain program's by a relative error of at most 0.023.
Values may be sent and summed in bfloat16 or wider, within the bound.
No kernel may reach another device: no remote copies, remote signals or barrier semaphores. Data moves between devices by JAX's collectives and lax.ppermute only.
A program may use at most 256 MiB of HBM per device.

v0:
```python
import jax
import jax.numpy as jnp
from jax import lax
from jax.experimental import pallas as pl
from jax.experimental.pallas import tpu as pltpu
from jax.sharding import PartitionSpec as P


HEADS = 12


EPS = 1e-05


def product(left, right):
    return jnp.dot(left, right, preferred_element_type=jnp.float32)


def left_product(left, right):
    return lax.dot_general(
        left, right, (((0,), (0,)), ((), ())), preferred_element_type=jnp.float32
    )


def right_product(left, right):
    return lax.dot_general(
        left, right, (((1,), (1,)), ((), ())), preferred_element_type=jnp.float32
    )


def column_sum(values):
    return jnp.sum(values.astype(jnp.float32), axis=0)


def normalize(values, gain, shift):
    center = jnp.mean(values, axis=-1, keepdims=True)
    centered = values - center
    spread = jnp.mean(centered * centered, axis=-1, keepdims=True)
    return centered * lax.rsqrt(spread + EPS) * gain + shift


def gelu_and_slope(values):
    below = 0.5 + 0.5 * lax.erf(values * (0.5**0.5))
    density = jnp.exp(-0.5 * values * values) * ((2.0 * jnp.pi) ** -0.5)
    return values * below, below + values * density


def logistic(values):
    return 0.5 + 0.5 * jnp.tanh(0.5 * values)


def recurrent_forward(slots, gin, ghid, sin, shid, counts):
    letter_slots, rows, width = slots.shape
    hidden = ghid.shape[0]
    gates = 3 * hidden
    last_slot = letter_slots - 1

    def body(
        ahead_ref,
        behind_ref,
        gin_ref,
        ghid_ref,
        sin_ref,
        shid_ref,
        counts_ref,
        gates_ahead,
        gates_behind,
        prev_ahead,
        prev_behind,
        last_ref,
        state_ref,
    ):
        step = pl.program_id(0)

        @pl.when(step == 0)
        def _():
            state_ref[...] = jnp.zeros_like(state_ref)

        counts_in = counts_ref[...]
        work = (
            (0, ahead_ref, step, gates_ahead, prev_ahead),
            (1, behind_ref, last_slot - step, gates_behind, prev_behind),
        )
        for at, slot_ref, slot, gates_ref, prev_ref in work:
            columns = slice(at * gates, (at + 1) * gates)
            own = slice(at * hidden, (at + 1) * hidden)
            state = state_ref[:, own]
            state_low = state.astype(jnp.bfloat16)
            prev_ref[0] = state_low
            inputs = product(slot_ref[0], gin_ref[:, columns]) + sin_ref[:, columns]
            turned = product(state_low, ghid_ref[:, columns]) + shid_ref[:, columns]
            reset = logistic(inputs[:, :hidden] + turned[:, :hidden])
            update = logistic(
                inputs[:, hidden : 2 * hidden] + turned[:, hidden : 2 * hidden]
            )
            turned_new = turned[:, 2 * hidden :]
            fresh = jnp.tanh(inputs[:, 2 * hidden :] + reset * turned_new)
            gates_ref[0, :, :hidden] = reset.astype(jnp.bfloat16)
            gates_ref[0, :, hidden : 2 * hidden] = update.astype(jnp.bfloat16)
            gates_ref[0, :, 2 * hidden : 3 * hidden] = fresh.astype(jnp.bfloat16)
            gates_ref[0, :, 3 * hidden :] = turned_new.astype(jnp.bfloat16)
            moved = (1.0 - update) * fresh + update * state
            state_ref[:, own] = jnp.where(slot < counts_in, moved, state)

        @pl.when(step == last_slot)
        def _():
            last_ref[...] = state_ref[...]

    ahead = lambda i: (i, 0, 0)
    behind = lambda i: (last_slot - i, 0, 0)
    fixed = lambda i: (0, 0)
    low = jnp.bfloat16
    return pl.pallas_call(
        body,
        grid=(letter_slots,),
        in_specs=[
            pl.BlockSpec((1, rows, width), ahead),
            pl.BlockSpec((1, rows, width), behind),
            pl.BlockSpec(gin.shape, fixed),
            pl.BlockSpec(ghid.shape, fixed),
            pl.BlockSpec((1, 2 * gates), fixed),
            pl.BlockSpec((1, 2 * gates), fixed),
            pl.BlockSpec((rows, 1), fixed),
        ],
        out_specs=[
            pl.BlockSpec((1, rows, 4 * hidden), ahead),
            pl.BlockSpec((1, rows, 4 * hidden), behind),
            pl.BlockSpec((1, rows, hidden), ahead),
            pl.BlockSpec((1, rows, hidden), behind),
            pl.BlockSpec((rows, 2 * hidden), fixed),
        ],
        out_shape=[
            jax.ShapeDtypeStruct((letter_slots, rows, 4 * hidden), low),
            jax.ShapeDtypeStruct((letter_slots, rows, 4 * hidden), low),
            jax.ShapeDtypeStruct((letter_slots, rows, hidden), low),
            jax.ShapeDtypeStruct((letter_slots, rows, hidden), low),
            jax.ShapeDtypeStruct((rows, 2 * hidden), jnp.float32),
        ],
        scratch_shapes=[pltpu.VMEM((rows, 2 * hidden), jnp.float32)],
        name="recurrent_forward",
    )(slots, slots, gin, ghid, sin, shid, counts)


def recurrent_backward(saved_gates, saved_states, ghid, counts, delta):
    letter_slots, rows, _ = saved_gates[0].shape
    hidden = ghid.shape[0]
    gates = 3 * hidden
    last_slot = letter_slots - 1

    def body(
        gates_ahead,
        gates_behind,
        prev_ahead,
        prev_behind,
        ghid_ref,
        counts_ref,
        delta_ref,
        inputs_ahead,
        inputs_behind,
        turned_ahead,
        turned_behind,
        inputs_sum,
        turned_sum,
        carry_ref,
    ):
        step = pl.program_id(0)

        @pl.when(step == 0)
        def _():
            carry_ref[...] = delta_ref[...]
            inputs_sum[...] = jnp.zeros_like(inputs_sum)
            turned_sum[...] = jnp.zeros_like(turned_sum)

        counts_in = counts_ref[...]
        work = (
            (0, last_slot - step, gates_ahead, prev_ahead, inputs_ahead, turned_ahead),
            (1, step, gates_behind, prev_behind, inputs_behind, turned_behind),
        )
        for at, slot, gates_ref, prev_ref, inputs_ref, turned_ref in work:
            start = at * gates
            own = slice(at * hidden, (at + 1) * hidden)
            reset = gates_ref[0, :, :hidden].astype(jnp.float32)
            update = gates_ref[0, :, hidden : 2 * hidden].astype(jnp.float32)
            fresh = gates_ref[0, :, 2 * hidden : 3 * hidden].astype(jnp.float32)
            turned_new = gates_ref[0, :, 3 * hidden :].astype(jnp.float32)
            state = prev_ref[0].astype(jnp.float32)
            carry = carry_ref[:, own]
            active = slot < counts_in
            moved = jnp.where(active, carry, 0.0)
            delta_fresh = moved * (1.0 - update) * (1.0 - fresh * fresh)
            delta_update = moved * (state - fresh) * update * (1.0 - update)
            delta_reset = delta_fresh * turned_new * reset * (1.0 - reset)
            low_reset = delta_reset.astype(jnp.bfloat16)
            low_update = delta_update.astype(jnp.bfloat16)
            low_fresh = delta_fresh.astype(jnp.bfloat16)
            low_turned = (delta_fresh * reset).astype(jnp.bfloat16)
            inputs_ref[0, :, :hidden] = low_reset
            inputs_ref[0, :, hidden : 2 * hidden] = low_update
            inputs_ref[0, :, 2 * hidden :] = low_fresh
            turned_ref[0, :, :hidden] = low_reset
            turned_ref[0, :, hidden : 2 * hidden] = low_update
            turned_ref[0, :, 2 * hidden :] = low_turned
            through = right_product(turned_ref[0], ghid_ref[:, start : start + gates])
            carry_ref[:, own] = jnp.where(active, moved * update, carry) + through
            sums = [
                jnp.sum(part.astype(jnp.float32), axis=0, keepdims=True)
                for part in (low_reset, low_update, low_fresh, low_turned)
            ]
            for place_at, (first, second) in enumerate(
                ((sums[0], sums[0]), (sums[1], sums[1]), (sums[2], sums[3]))
            ):
                columns = slice(start + place_at * hidden, start + (place_at + 1) * hidden)
                inputs_sum[:, columns] += first
                turned_sum[:, columns] += second

    ahead = lambda i: (last_slot - i, 0, 0)
    behind = lambda i: (i, 0, 0)
    fixed = lambda i: (0, 0)
    low = jnp.bfloat16
    return pl.pallas_call(
        body,
        grid=(letter_slots,),
        in_specs=[
            pl.BlockSpec((1, rows, 4 * hidden), ahead),
            pl.BlockSpec((1, rows, 4 * hidden), behind),
            pl.BlockSpec((1, rows, hidden), ahead),
            pl.BlockSpec((1, rows, hidden), behind),
            pl.BlockSpec(ghid.shape, fixed),
            pl.BlockSpec((rows, 1), fixed),
            pl.BlockSpec((rows, 2 * hidden), fixed),
        ],
        out_specs=[
            pl.BlockSpec((1, rows, gates), ahead),
            pl.BlockSpec((1, rows, gates), behind),
            pl.BlockSpec((1, rows, gates), ahead),
            pl.BlockSpec((1, rows, gates), behind),
            pl.BlockSpec((1, 2 * gates), fixed),
            pl.BlockSpec((1, 2 * gates), fixed),
        ],
        out_shape=[
            jax.ShapeDtypeStruct((letter_slots, rows, gates), low),
            jax.ShapeDtypeStruct((letter_slots, rows, gates), low),
            jax.ShapeDtypeStruct((letter_slots, rows, gates), low),
            jax.ShapeDtypeStruct((letter_slots, rows, gates), low),
            jax.ShapeDtypeStruct((1, 2 * gates), jnp.float32),
            jax.ShapeDtypeStruct((1, 2 * gates), jnp.float32),
        ],
        scratch_shapes=[pltpu.VMEM((rows, 2 * hidden), jnp.float32)],
        name="recurrent_backward",
    )(*saved_gates, *saved_states, ghid, counts, delta)


DEPTH_SIZE = 4


def exchange(value, axis, pairs):
    return lax.ppermute(value, axis, pairs)


class Place:
    def __init__(self):
        self.rep_size = lax.axis_size("rep")
        self.shard_size = lax.axis_size("shard")
        self.depth = DEPTH_SIZE
        self.height = self.shard_size // DEPTH_SIZE
        rep_at = lax.axis_index("rep")
        shard_at = lax.axis_index("shard")
        self.shard_at = shard_at
        self.core = rep_at % 2
        self.side = (rep_at // 2) % 2
        self.row = shard_at % self.height
        self.layer = shard_at // self.height
        self.coords = jnp.stack([self.layer, self.row, self.side, self.core]).astype(jnp.int32)

    def over_core(self, value):
        return exchange(value, "rep", [(i, i ^ 1) for i in range(self.rep_size)])

    def over_side(self, value):
        return exchange(value, "rep", [(i, i ^ 2) for i in range(self.rep_size)])

    def over_far(self, value, step):
        return exchange(value, "rep", [(i, (i + 4 * step) % self.rep_size) for i in range(self.rep_size)]
        )

    def over_row(self, value, step):
        return exchange(value, "shard", [(i, i ^ step) for i in range(self.shard_size)])

    def over_layer(self, value, step):
        return exchange(value, "shard", [(i, i ^ (step * self.height)) for i in range(self.shard_size)]
        )


def put_together(place, parts, rows, half, split):
    depth = place.depth
    flat = [part for group in parts for inner in group for part in inner]
    slots = [
        (core_slot, side_slot, row_slot)
        for core_slot in range(2)
        for side_slot in range(len(parts[0]))
        for row_slot in range(len(parts[0][0]))
    ]
    height = place.height
    pieces = 2 if split else 1
    part_rows = [r // pieces for r in rows]
    starts = [sum(part_rows[:i]) for i in range(len(rows))]

    def body(coords_ref, *refs):
        ins = refs[: len(flat)]
        outs = refs[len(flat) : len(flat) + len(rows)]
        sems = refs[-1]
        layer, row, side, core = (coords_ref[i] for i in range(4))
        copies = []
        for at, (core_slot, side_slot, row_slot) in enumerate(slots):
            for layer_slot in range(depth):
                block = (layer ^ layer_slot) * height + (row ^ row_slot)
                if split:
                    block = block * 2 + (side ^ side_slot)
                column = pl.multiple_of((core ^ core_slot) * half, 128)
                for out_ref, start, count in zip(outs, starts, part_rows):
                    copies.append(
                        pltpu.make_async_copy(
                            ins[at].at[layer_slot, pl.ds(start, count), :],
                            out_ref.at[block, :, pl.ds(column, half)],
                            sems.at[len(copies)],
                        )
                    )
        for copy in copies:
            copy.start()
        for copy in copies:
            copy.wait()

    blocks = depth * height * pieces
    whole = pl.pallas_call(
        body,
        out_shape=[
            jax.ShapeDtypeStruct((blocks, count, 2 * half), flat[0].dtype) for count in part_rows
        ],
        in_specs=[pl.BlockSpec(memory_space=pltpu.SMEM)]
        + [pl.BlockSpec(memory_space=pl.ANY)] * len(flat),
        out_specs=[pl.BlockSpec(memory_space=pltpu.VMEM)] * len(rows),
        scratch_shapes=[pltpu.SemaphoreType.DMA((len(flat) * depth * len(rows),))],
        name="put_together",
    )(place.coords, *flat)
    return [w.reshape(r * place.shard_size, 2 * half) for w, r in zip(whole, rows)]


def gathered(place, shards_in, split, after=None):
    half = shards_in[0].shape[1] // 2
    pieces = []
    for shard in shards_in:
        part_rows = shard.shape[0] // 2 if split else shard.shape[0]
        top = place.side * part_rows if split else 0
        pieces.append(lax.dynamic_slice(shard, (top, place.core * half), (part_rows, half)))
    piece = pieces[0] if len(pieces) == 1 else jnp.concatenate(pieces, axis=0)
    if after is not None:
        piece = hold(piece, after)
    layers = jnp.stack([piece] + [place.over_layer(piece, step) for step in range(1, place.depth)])
    column = [layers] + [place.over_row(layers, step) for step in range(1, place.height)]
    sides = [column]
    if split:
        sides.append([place.over_side(part) for part in column])
    cores = [
        sides,
        [[place.over_core(part) for part in group] for group in sides],
    ]
    return put_together(place, cores, [shard.shape[0] for shard in shards_in], half, split), piece, layers


def hold(value, *others):
    return lax.optimization_barrier((value, *others))[0]


def pick(value, at, axis):
    return lax.dynamic_index_in_dim(value, at, axis, keepdims=False)


def widen(value):
    return value.astype(jnp.float32)


def narrow(value):
    return value.astype(jnp.bfloat16)


def core_sum(place, inputs, delta):
    half = delta.shape[1] // 2

    def half_of(at):
        return left_product(inputs, lax.dynamic_slice_in_dim(delta, at * half, half, axis=1))

    sent = half_of(1 - place.core)
    other = place.over_core(narrow(sent))
    return narrow(half_of(place.core) + widen(other))


def core_sum_of_pair(place, first, second):
    first, second = narrow(first), narrow(second)
    other = place.over_core(jnp.where(place.core == 0, second, first))
    return narrow(widen(jnp.where(place.core == 0, first, second)) + widen(other))


def summed(place, helds, split):
    half = helds[0].shape[1]
    pieces = 2 if split else 1
    parts = [h.shape[0] // place.shard_size // pieces for h in helds]
    blocks = [h.reshape(place.shard_size, pieces, p, half) for h, p in zip(helds, parts)]
    if split:
        kept = []
        for block in blocks:
            other = place.over_side(pick(block, 1 - place.side, 1))
            kept.append(narrow(widen(pick(block, place.side, 1)) + widen(other)))
    else:
        kept = [block[:, 0] for block in blocks]
    shape = (place.depth, place.height)
    kept = [k.reshape(shape + k.shape[1:]) for k in kept]

    def stacked(values):
        return values[0] if len(values) == 1 else jnp.concatenate(values, axis=-2)

    total = widen(stacked([pick(k, place.row, 1) for k in kept]))
    for step in range(1, place.height):
        sent = stacked([pick(k, place.row ^ step, 1) for k in kept])
        total = total + widen(place.over_row(sent, step))
    held = narrow(total)
    total = widen(pick(held, place.layer, 0))
    for step in range(1, place.depth):
        sent = pick(held, place.layer ^ step, 0)
        total = total + widen(place.over_layer(sent, step))
    return narrow(total), parts, split


def shared(place, pending, after=None):
    held, parts, split = pending
    pieces = 2 if split else 1
    if after is not None:
        held = hold(held, after)
    total = widen(held)
    for step in range(1, place.rep_size // 4):
        total = total + widen(place.over_far(held, step))
    held = narrow(total)
    other = place.over_side(held)
    if split:
        low_side = jnp.where(place.side == 0, held, other)
        high_side = jnp.where(place.side == 0, other, held)
        rows, start = [], 0
        for p in parts:
            rows += [low_side[start : start + p], high_side[start : start + p]]
            start += p
        held = jnp.concatenate(rows, axis=0)
    else:
        held = narrow(widen(held) + widen(other))
    other = place.over_core(held)
    first = jnp.where(place.core == 0, held, other)
    last = jnp.where(place.core == 0, other, held)
    results, start = [], 0
    for p in parts:
        own = slice(start, start + p * pieces)
        results.append(widen(jnp.concatenate([first[own], last[own]], axis=1)))
        start += p * pieces
    return results


def gathered_vectors(place, vectors, after):
    flat = [v.reshape(-1) for v in vectors]
    flat[0] = hold(flat[0], after)
    packed = jnp.concatenate(flat)[None, :]
    layers = jnp.concatenate(
        [packed] + [place.over_layer(packed, step) for step in range(1, place.depth)], axis=0
    )
    slots = jnp.stack(
        [layers] + [place.over_row(layers, step) for step in range(1, place.height)], axis=1
    ).reshape(place.shard_size, -1)
    order = jnp.arange(place.shard_size)
    slot_of = ((order // place.height) ^ place.layer) * place.height + (
        (order % place.height) ^ place.row
    )
    ordered = jnp.take(slots, slot_of, axis=0, mode="clip").astype(jnp.float32)
    whole, start = [], 0
    for v in vectors:
        width = v.size
        part = ordered[:, start : start + width]
        if v.ndim == 1:
            whole.append(part.reshape(-1))
        else:
            lead, inner = v.shape
            whole.append(
                part.reshape(place.shard_size, lead, inner).transpose(1, 0, 2).reshape(lead, -1)
            )
        start += width
    return whole


def owned_vectors(place, vectors):
    count = place.shard_size
    rows = []
    for v in vectors:
        if v.ndim == 1:
            rows.append(v.reshape(count, -1))
        else:
            lead = v.shape[0]
            rows.append(v.reshape(lead, count, -1).transpose(1, 0, 2).reshape(count, -1))
    total = jnp.concatenate(rows, axis=1)
    total = total + place.over_core(total)
    total = total + place.over_side(total)
    base = total
    for step in range(1, place.rep_size // 4):
        total = total + place.over_far(base, step)
    span = 1
    while span < place.height:
        total = total + place.over_row(total, span)
        span *= 2
    span = 1
    while span < place.depth:
        total = total + place.over_layer(total, span)
        span *= 2
    own = lax.dynamic_index_in_dim(total, place.shard_at, 0, keepdims=False)
    parts, start = [], 0
    for v in vectors:
        width = v.size // count
        part = own[start : start + width]
        parts.append(part if v.ndim == 1 else part.reshape(v.shape[0], -1))
        start += width
    return parts


def shards(
    tokens,
    letters,
    lengths,
    counts,
    cot_token,
    cot_letter,
    project_weight,
    project_bias,
    output_weight,
    output_bias,
    first_gain,
    first_shift,
    up_weight,
    up_bias,
    down_weight,
    down_bias,
    second_gain,
    second_shift,
    gates_input,
    gates_hidden,
    shift_input,
    shift_hidden,
    token_mixer,
    token_offset,
    letter_mixer,
    letter_offset,
    window_kernel,
    window_offset,
    third_gain,
    third_shift,
    fourth_gain,
    fourth_shift,
):
    place = Place()
    seq_rows, model_width = tokens.shape
    letter_slots = letters.shape[1]
    head_width = model_width // HEADS
    score_scale = float(head_width) ** (-0.5)
    row_valid = jnp.arange(seq_rows) < lengths[0]
    row_mask = row_valid.astype(jnp.float32)[:, None]
    key_valid = row_valid[None, None, :]
    letter_flat = letters.transpose(1, 0, 2).reshape(letter_slots * seq_rows, model_width)

    side_by_side = lambda w: jnp.concatenate([w[i] for i in range(w.shape[0])], axis=1)
    (full_gin, full_project), first_piece, first_layers = gathered(
        place, (side_by_side(gates_input), project_weight), True
    )
    (full_ghid,), _, second_layers = gathered(place, (side_by_side(gates_hidden),), False)
    window = side_by_side(window_kernel)
    window_half = window.shape[1] // 2
    (kernel_one,), _, third_layers = gathered(place, (window[:, :window_half],), True, first_layers)
    (full_output, full_down), _, fourth_layers = gathered(
        place, (output_weight, down_weight), False, second_layers
    )
    (full_up,), _, fifth_layers = gathered(place, (up_weight,), False, third_layers)
    (kernel_two,), _, _ = gathered(place, (window[:, window_half:],), True, fourth_layers)
    (full_tmix, full_lmix), _, _ = gathered(place, (token_mixer, letter_mixer), False, fifth_layers)
    (
        full_pbias,
        full_obias,
        gain_one,
        shift_one,
        full_ubias,
        full_dbias,
        gain_two,
        shift_two,
        full_sin,
        full_shid,
        full_toff,
        full_loff,
        full_koff,
        gain_three,
        shift_three,
        gain_four,
        shift_four,
    ) = gathered_vectors(
        place,
        (
            project_bias,
            output_bias,
            first_gain,
            first_shift,
            up_bias,
            down_bias,
            second_gain,
            second_shift,
            shift_input,
            shift_hidden,
            token_offset,
            letter_offset,
            window_offset,
            third_gain,
            third_shift,
            fourth_gain,
            fourth_shift,
        ),
        first_piece,
    )

    bias_full = jnp.concatenate(
        [full_pbias[:model_width], jnp.zeros((model_width,), jnp.float32), full_pbias[model_width:]]
    )
    mixed = (product(tokens, full_project) + bias_full).astype(jnp.bfloat16)
    queries = mixed[:, :model_width].reshape(seq_rows, HEADS, head_width)
    key_rows = mixed[:, model_width : 2 * model_width].reshape(seq_rows, HEADS, head_width)
    value_rows = mixed[:, 2 * model_width :].reshape(seq_rows, HEADS, head_width)

    def masked_scores_of(query_part, key_part):
        raw_scores = (
            jnp.einsum("qhd,khd->hqk", query_part, key_part, preferred_element_type=jnp.float32)
            * score_scale
        )
        return jnp.where(key_valid, raw_scores, -1e30)

    masked_scores = masked_scores_of(queries, key_rows)
    row_peak = jnp.max(masked_scores, axis=-1, keepdims=True)
    log_total = row_peak + jnp.log(
        jnp.sum(jnp.exp(masked_scores - row_peak), axis=-1, keepdims=True)
    )
    probabilities = jnp.exp(masked_scores - log_total)
    probs_low = probabilities.astype(jnp.bfloat16)
    context = jnp.einsum("hqk,khd->qhd", probs_low, value_rows, preferred_element_type=jnp.float32)
    context = (
        context
        .astype(jnp.bfloat16)
        .reshape(seq_rows, model_width)
    )
    attended = product(context, full_output) + full_obias
    residual_one = tokens.astype(jnp.float32) + attended
    first = normalize(residual_one, gain_one, shift_one)
    first_low = first.astype(jnp.bfloat16)
    upper = product(first_low, full_up)
    upper = upper + full_ubias
    activated, slope_upper = gelu_and_slope(upper)
    activated = activated.astype(jnp.bfloat16)
    residual_two = first + product(activated, full_down) + full_dbias
    second = normalize(residual_two, gain_two, shift_two)
    hidden_width = full_ghid.shape[0]
    gates_width = 3 * hidden_width
    counts_column = counts.reshape(-1, 1)
    gates_ahead, gates_behind, prev_ahead, prev_behind, pooled = recurrent_forward(
        letter_flat.reshape(letter_slots, seq_rows, model_width),
        full_gin,
        full_ghid,
        full_sin.reshape(1, -1),
        full_shid.reshape(1, -1),
        counts_column,
    )
    second_low = second.astype(jnp.bfloat16)
    pooled_low = pooled.astype(jnp.bfloat16)
    token_side = product(second_low, full_tmix) + full_toff
    letter_side = product(pooled_low, full_lmix) + full_loff
    joined = (jnp.concatenate([token_side, letter_side], axis=-1) * row_mask).astype(jnp.bfloat16)
    joined_width = joined.shape[1]
    taps_one = product(joined, kernel_one)
    taps_two = product(joined, kernel_two)
    rest = window_half - joined_width
    convolved = (
        jnp.pad(taps_one[:-1, :joined_width], ((1, 0), (0, 0)))
        + jnp.concatenate([taps_one[:, joined_width:], taps_two[:, :rest]], axis=1)
        + jnp.pad(taps_two[1:, rest:], ((0, 1), (0, 0)))
        + full_koff
    )
    widened, slope_conv = gelu_and_slope(convolved)
    residual_three = second + widened[:, :model_width]
    residual_four = pooled + widened[:, model_width:]
    token_out = normalize(residual_three, gain_three, shift_three) * row_mask
    letter_out = normalize(residual_four, gain_four, shift_four) * row_mask

    out_token_delta = cot_token.astype(jnp.float32) * row_mask
    out_letter_delta = cot_letter.astype(jnp.float32) * row_mask
    _, pull_three = jax.vjp(normalize, residual_three, gain_three, shift_three)
    delta_three, delta_gain_three, delta_shift_three = pull_three(out_token_delta)
    _, pull_four = jax.vjp(normalize, residual_four, gain_four, shift_four)
    delta_four, delta_gain_four, delta_shift_four = pull_four(out_letter_delta)
    delta_conv = (jnp.concatenate([delta_three, delta_four], axis=-1) * slope_conv).astype(
        jnp.bfloat16
    )
    delta_koff = column_sum(delta_conv)
    delta_taps = jnp.concatenate(
        [
            jnp.pad(delta_conv[1:], ((0, 1), (0, 0))),
            delta_conv,
            jnp.pad(delta_conv[:-1], ((1, 0), (0, 0))),
        ],
        axis=1,
    )
    taps_low, taps_high = delta_taps[:, :window_half], delta_taps[:, window_half:]
    one_sum = core_sum(place, joined, taps_low)
    two_sum = core_sum(place, joined, taps_high)
    one_pending = summed(place, (one_sum,), True)
    two_pending = summed(place, (two_sum,), True)
    delta_joined = right_product(taps_low, kernel_one) + right_product(taps_high, kernel_two)
    delta_joined = delta_joined * row_mask
    delta_tside = delta_joined[:, :model_width].astype(jnp.bfloat16)
    delta_lside = delta_joined[:, model_width:].astype(jnp.bfloat16)
    tmix_sum = core_sum(place, second_low, delta_tside)
    delta_toff = column_sum(delta_tside)
    lmix_sum = core_sum(place, pooled_low, delta_lside)
    delta_loff = column_sum(delta_lside)
    delta_second = delta_three + right_product(delta_tside, full_tmix)
    delta_pooled = delta_four + right_product(delta_lside, full_lmix)

    inputs_ahead, inputs_behind, turned_ahead, turned_behind, sin_delta, shid_delta = (
        recurrent_backward(
            (gates_ahead, gates_behind),
            (prev_ahead, prev_behind),
            full_ghid,
            counts_column,
            delta_pooled,
        )
    )
    flat_rows = lambda v: v.reshape(letter_slots * seq_rows, -1)
    inputs_ahead, inputs_behind = flat_rows(inputs_ahead), flat_rows(inputs_behind)
    gin_sum = core_sum_of_pair(
        place, left_product(letter_flat, inputs_ahead), left_product(letter_flat, inputs_behind)
    )
    ghid_sum = core_sum_of_pair(
        place,
        left_product(flat_rows(prev_ahead), flat_rows(turned_ahead)),
        left_product(flat_rows(prev_behind), flat_rows(turned_behind)),
    )
    letters_delta = right_product(inputs_ahead, full_gin[:, :gates_width]) + right_product(
        inputs_behind, full_gin[:, gates_width:]
    )
    letters_grad = (
        letters_delta.astype(jnp.bfloat16)
        .reshape(letter_slots, seq_rows, model_width)
        .transpose(1, 0, 2)
    )
    sin_delta = sin_delta.reshape(2, -1)
    shid_delta = shid_delta.reshape(2, -1)
    in_pair = lambda v: jnp.stack([v[:, :gates_width], v[:, gates_width:]])
    ghid_pending = summed(place, (ghid_sum,), False)
    gin_pending = summed(place, (gin_sum,), True)
    delta_second = hold(delta_second, letters_delta)
    _, pull_two = jax.vjp(normalize, residual_two, gain_two, shift_two)
    delta_two, delta_gain_two, delta_shift_two = pull_two(delta_second)
    delta_lowered = delta_two.astype(jnp.bfloat16)
    down_sum = core_sum(place, activated, delta_lowered)
    down_pending = summed(place, (tmix_sum, lmix_sum, down_sum), False)
    delta_dbias = column_sum(delta_lowered)
    delta_activated = right_product(delta_lowered, full_down)
    delta_upper = (delta_activated * slope_upper).astype(jnp.bfloat16)
    up_sum = core_sum(place, first_low, delta_upper)
    up_pending = summed(place, (up_sum,), False)
    delta_ubias = column_sum(delta_upper)
    delta_first = right_product(delta_upper, full_up)
    delta_first = delta_two + delta_first
    _, pull_one = jax.vjp(normalize, residual_one, gain_one, shift_one)
    delta_one, delta_gain_one, delta_shift_one = pull_one(delta_first)
    delta_attended = delta_one.astype(jnp.bfloat16)
    output_sum = core_sum(place, context, delta_attended)
    output_pending = summed(place, (output_sum,), False)
    delta_obias = column_sum(delta_attended)
    delta_context = right_product(delta_attended, full_output)
    delta_context = (
        delta_context
        .astype(jnp.bfloat16)
        .reshape(seq_rows, HEADS, head_width)
    )
    delta_values = jnp.einsum(
        "hqk,qhd->khd",
        probs_low,
        delta_context,
        preferred_element_type=jnp.float32,
    )
    delta_probs = jnp.einsum(
        "qhd,khd->hqk", delta_context, value_rows, preferred_element_type=jnp.float32
    )
    delta_scores = (
        probabilities * (delta_probs - jnp.sum(probabilities * delta_probs, axis=-1, keepdims=True))
    ).astype(jnp.bfloat16)
    delta_queries = jnp.einsum(
        "hqk,khd->qhd", delta_scores, key_rows, preferred_element_type=jnp.float32
    )
    delta_keys = jnp.einsum(
        "hqk,qhd->khd", delta_scores, queries, preferred_element_type=jnp.float32
    )
    delta_queries = delta_queries * score_scale
    delta_keys = delta_keys * score_scale
    delta_mixed = jnp.concatenate(
        [
            delta_queries.reshape(seq_rows, model_width),
            delta_keys.reshape(seq_rows, model_width),
            delta_values.reshape(seq_rows, model_width),
        ],
        axis=-1,
    ).astype(jnp.bfloat16)
    project_sum = core_sum(place, tokens, delta_mixed)
    project_pending = summed(place, (project_sum,), True)
    (ghid_grad,) = shared(place, ghid_pending, delta_context)
    (kernel_one_grad,) = shared(place, one_pending, delta_context)
    (kernel_two_grad,) = shared(place, two_pending, delta_mixed)
    (gin_grad,) = shared(place, gin_pending, delta_mixed)
    tmix_grad, lmix_grad, down_grad = shared(place, down_pending, delta_mixed)
    (up_grad,) = shared(place, up_pending, delta_mixed)
    (output_grad,) = shared(place, output_pending, delta_mixed)
    (project_grad,) = shared(place, project_pending)
    ghid_grad, gin_grad = in_pair(ghid_grad), in_pair(gin_grad)
    kernel_grad = jnp.concatenate([kernel_one_grad, kernel_two_grad], axis=1)
    delta_mixed_sum = column_sum(delta_mixed)
    delta_pbias = jnp.concatenate(
        [delta_mixed_sum[:model_width], delta_mixed_sum[2 * model_width :]]
    )
    tokens_grad = right_product(delta_mixed, full_project)
    tokens_grad = (delta_one + tokens_grad).astype(jnp.bfloat16)
    (
        pbias_grad,
        obias_grad,
        gain_one_grad,
        shift_one_grad,
        ubias_grad,
        dbias_grad,
        gain_two_grad,
        shift_two_grad,
        sin_grad,
        shid_grad,
        toff_grad,
        loff_grad,
        koff_grad,
        gain_three_grad,
        shift_three_grad,
        gain_four_grad,
        shift_four_grad,
    ) = owned_vectors(
        place,
        (
            delta_pbias,
            delta_obias,
            delta_gain_one,
            delta_shift_one,
            delta_ubias,
            delta_dbias,
            delta_gain_two,
            delta_shift_two,
            sin_delta,
            shid_delta,
            delta_toff,
            delta_loff,
            delta_koff,
            delta_gain_three,
            delta_shift_three,
            delta_gain_four,
            delta_shift_four,
        ),
    )
    taps_grad = jnp.stack(
        [kernel_grad[:, t * joined_width : (t + 1) * joined_width] for t in range(3)]
    )
    return (
        token_out.astype(jnp.bfloat16),
        letter_out.astype(jnp.bfloat16),
        tokens_grad,
        letters_grad,
        project_grad,
        pbias_grad,
        output_grad,
        obias_grad,
        gain_one_grad,
        shift_one_grad,
        up_grad,
        ubias_grad,
        down_grad,
        dbias_grad,
        gain_two_grad,
        shift_two_grad,
        gin_grad,
        ghid_grad,
        sin_grad,
        shid_grad,
        tmix_grad,
        toff_grad,
        lmix_grad,
        loff_grad,
        taps_grad,
        koff_grad,
        gain_three_grad,
        shift_three_grad,
        gain_four_grad,
        shift_four_grad,
    )


def solution(mesh):
    placed = (
        P(("rep", "shard"), None),
        P(("rep", "shard"), None, None),
        P(("rep", "shard")),
        P(("rep", "shard")),
        P(("rep", "shard"), None),
        P(("rep", "shard"), None),
        P("shard", None),
        P("shard"),
        P("shard", None),
        P("shard"),
        P("shard"),
        P("shard"),
        P("shard", None),
        P("shard"),
        P("shard", None),
        P("shard"),
        P("shard"),
        P("shard"),
        P(None, "shard", None),
        P(None, "shard", None),
        P(None, "shard"),
        P(None, "shard"),
        P("shard", None),
        P("shard"),
        P("shard", None),
        P("shard"),
        P(None, "shard", None),
        P("shard"),
        P("shard"),
        P("shard"),
        P("shard"),
        P("shard"),
    )
    return jax.shard_map(
        shards,
        mesh=mesh,
        in_specs=placed,
        out_specs=(
            P(("rep", "shard"), None),
            P(("rep", "shard"), None),
            P(("rep", "shard"), None),
            P(("rep", "shard"), None, None),
            P("shard", None),
            P("shard"),
            P("shard", None),
            P("shard"),
            P("shard"),
            P("shard"),
            P("shard", None),
            P("shard"),
            P("shard", None),
            P("shard"),
            P("shard"),
            P("shard"),
            P(None, "shard", None),
            P(None, "shard", None),
            P(None, "shard"),
            P(None, "shard"),
            P("shard", None),
            P("shard"),
            P("shard", None),
            P("shard"),
            P(None, "shard", None),
            P("shard"),
            P("shard"),
            P("shard"),
            P("shard"),
            P("shard"),
        ),
        check_vma=False,
    )
```

profile of v0, /device:TPU:0, one launch (start us, length us, event | category | flops | bytes accessed | tf_op | source)
XLA Modules:
  0.0 858.5 jit_solution(1266069986247467900)
XLA Ops:
  2.7 4.1 collective-permute-start.15
  25.3 5.0 collective-permute-done.2
  30.3 13.0 %collective-permute-done.1 = bf16[96,1152]{1,0:T(8,128)(2,1)S(1)} collective-permute-done((bf16[96,1152]{1,0:T(8,128)(2,1)S(1)}, bf16[96,1152]{1,0:T(8,128)(2,1)S(1)}, u32[]{:S(2)}, u32[]{:S(2)}) %collective-permute-start.1) | collective-permute-done | bytes 221216 | tf_op jit(solution)/shard_map/ppermute | solution.py:257
  47.5 3.5 collective-permute-start.19
  56.3 14.9 %collective-permute-start.23 = (bf16[96,1152]{1,0:T(8,128)(2,1)S(1)}, bf16[96,1152]{1,0:T(8,128)(2,1)S(1)}, u32[]{:S(2)}, u32[]{:S(2)}) collective-permute-start(bf16[96,1152]{1,0:T(8,128)(2,1)S(1)} %get-tuple-element.65), channel_id=1, source_target_pairs={{0,2},{1,3},{2,0},{3,1},{4,6},{5,7},{6,4},{7,5},{8,10},{9,11},{10,... | collective-permute-start | bytes 663560 | tf_op jit(solution)/shard_map/ppermute | solution.py:257
  72.2 22.9 %collective-permute-done.24 = bf16[96,1152]{1,0:T(8,128)(2,1)S(1)} collective-permute-done((bf16[96,1152]{1,0:T(8,128)(2,1)S(1)}, bf16[96,1152]{1,0:T(8,128)(2,1)S(1)}, u32[]{:S(2)}, u32[]{:S(2)}) %collective-permute-start.24) | collective-permute-done | bytes 221216 | tf_op jit(solution)/shard_map/ppermute | solution.py:257
  103.4 4.3 collective-permute-done.38.refs_1_
  110.8 17.7 %collective-permute-done.27 = bf16[96,1536]{1,0:T(8,128)(2,1)S(1)} collective-permute-done((bf16[96,1536]{1,0:T(8,128)(2,1)S(1)}, bf16[96,1536]{1,0:T(8,128)(2,1)S(1)}, u32[]{:S(2)}, u32[]{:S(2)}) %collective-permute-start.27) | collective-permute-done | bytes 294944 | tf_op jit(solution)/shard_map/ppermute | solution.py:257
  133.1 12.7 %collective-permute-done.49 = bf16[96,1152]{1,0:T(8,128)(2,1)S(1)} collective-permute-done((bf16[96,1152]{1,0:T(8,128)(2,1)S(1)}, bf16[96,1152]{1,0:T(8,128)(2,1)S(1)}, u32[]{:S(2)}, u32[]{:S(2)}) %collective-permute-start.49) | collective-permute-done | bytes 221216 | tf_op jit(solution)/shard_map/ppermute | solution.py:257
  146.7 9.3 %collective-permute-done.33 = bf16[192,384]{1,0:T(8,128)(2,1)S(1)} collective-permute-done((bf16[192,384]{1,0:T(8,128)(2,1)S(1)}, bf16[192,384]{1,0:T(8,128)(2,1)S(1)}, u32[]{:S(2)}, u32[]{:S(2)}) %collective-permute-start.33) | collective-permute-done | bytes 147488 | tf_op jit(solution)/shard_map/ppermute | solution.py:257
  155.9 5.8 collective-permute-done.32
  165.1 3.5 collective-permute-done.3.refs_1_
  169.4 14.5 %collective-permute-done.42.refs_2_ = bf16[4,96,1152]{2,1,0:T(8,128)(2,1)S(1)} collective-permute-done((bf16[4,96,1152]{2,1,0:T(8,128)(2,1)S(1)}, bf16[4,96,1152]{2,1,0:T(8,128)(2,1)S(1)}, u32[]{:S(2)}, u32[]{:S(2)}) %collective-permute-start.42) | collective-permute-done | bytes 884768 | tf_op jit(solution)/shard_map/ppermute | solution.py:257
  188.2 11.9 %collective-permute-done.35.refs_1_ = bf16[4,192,384]{2,1,0:T(8,128)(2,1)S(1)} collective-permute-done((bf16[4,192,384]{2,1,0:T(8,128)(2,1)S(1)}, bf16[4,192,384]{2,1,0:T(8,128)(2,1)S(1)}, u32[]{:S(2)}, u32[]{:S(2)}) %collective-permute-start.35) | collective-permute-done | bytes 589856 | tf_op jit(solution)/shard_map/ppermute | solution.py:257
  203.1 3.4 collective-permute-done.52.refs_2_
  207.6 36.3 %collective-permute-done.51.refs_1_ = bf16[4,96,1152]{2,1,0:T(8,128)(2,1)} collective-permute-done((bf16[4,96,1152]{2,1,0:T(8,128)(2,1)S(1)}, bf16[4,96,1152]{2,1,0:T(8,128)(2,1)}, u32[]{:S(2)}, u32[]{:S(2)}) %collective-permute-start.51) | collective-permute-done | bytes 884768 | tf_op jit(solution)/shard_map/ppermute | solution.py:257
  246.7 4.2 copy.142
  267.6 3.5 put_together.11
  271.2 4.1 put_together.10
  275.3 7.4 put_together.7
  283.7 3.3 fusion.2
  289.3 15.7 %collective-permute-done.53.refs_3_ = bf16[4,96,1152]{2,1,0:T(8,128)(2,1)} collective-permute-done((bf16[4,96,1152]{2,1,0:T(8,128)(2,1)}, bf16[4,96,1152]{2,1,0:T(8,128)(2,1)}, u32[]{:S(2)}, u32[]{:S(2)}) %collective-permute-start.53) | collective-permute-done | bytes 884768 | tf_op jit(solution)/shard_map/ppermute | solution.py:257
  307.2 20.7 %recurrent_forward.1 = (bf16[8,256,1536]{2,1,0:T(8,128)(2,1)}, bf16[8,256,1536]{2,1,0:T(8,128)(2,1)}, bf16[8,256,384]{2,1,0:T(8,128)(2,1)}, bf16[8,256,384]{2,1,0:T(8,128)(2,1)}, f32[256,768]{1,0:T(8,128)}) custom-call(bf16[8,256,768]{2,1,0:T(8,128)(2,1)} %bitcast.400, bf16[8,256,768]{2,1,0:T(8,128)(2,1)} %bitcast.401, bf16[768,2304]{1,0:T(8,128)(2,1)} %bitcast.441, ...), custom_call_target="tpu_custom_call" | custom-call | tf_op jit(solution)/shard_map/recurrent_forward/pallas_call | solution.py:113
  333.3 5.2 put_together.9
  338.5 7.0 put_together.12
  345.6 7.0 put_together.13
  352.6 6.1 put_together.8
  361.1 5.9 multiply_convert_fusion.1
  393.1 3.0 convolution_convert_fusion.1
  396.2 3.0 convolution_convert_fusion
  399.2 16.8 %recurrent_backward.1 = (bf16[8,256,1152]{2,1,0:T(8,128)(2,1)}, bf16[8,256,1152]{2,1,0:T(8,128)(2,1)}, bf16[8,256,1152]{2,1,0:T(8,128)(2,1)}, bf16[8,256,1152]{2...) custom-call(bf16[8,256,1536]{2,1,0:T(8,128)(2,1)} %get-tuple-element.74.gates_ahead, ...), custom_call_target="tpu_custom_call" | custom-call | tf_op jit(solution)/shard_map/recurrent_backward/pallas_call | solution.py:220
  416.0 9.5 %fusion.6 = bf16[1152,768]{0,1:T(8,128)(2,1)} fusion(bf16[8,256,1152]{2,1,0:T(8,128)(2,1)} %get-tuple-element.78, bf16[8,256,768]{2,0,1:T(8,128)(2,1)} %bitcast.453), kind=kOutput, calls=%fused_computation.30 | convolution fusion | flops 3624763392 | bytes 9633792 | tf_op jit(solution)/shard_map/dot_general | solution.py:20
  425.5 6.3 fusion.7
  431.8 4.3 fusion.23
  436.2 5.7 convolution_add_fusion.2
  474.7 5.5 fusion.13
  481.3 6.6 broadcast_select_fusion
  524.6 3.4 copy.141
  551.7 3.1 collective-permute-done.74
  564.0 4.0 collective-permute-done.105
  571.5 3.8 collective-permute-done.107
  587.3 15.7 %collective-permute-done.95 = bf16[8,48,1152]{2,1,0:T(8,128)(2,1)S(1)} collective-permute-done((bf16[8,48,1152]{2,1,0:T(8,128)(2,1)S(1)}, bf16[8,48,1152]{2,1,0:T(8,128)(2,1)S(1)}, u32[]{:S(2)}, u32[]{:S(2)}) %collective-permute-start.95) | collective-permute-done | bytes 884768 | tf_op jit(solution)/shard_map/ppermute | solution.py:257
  605.2 15.9 %collective-permute-done.59 = bf16[8,48,1152]{2,1,0:T(8,128)(2,1)S(1)} collective-permute-done((bf16[8,48,1152]{2,1,0:T(8,128)(2,1)S(1)}, bf16[8,48,1152]{2,1,0:T(8,128)(2,1)S(1)}, u32[]{:S(2)}, u32[]{:S(2)}) %collective-permute-start.59) | collective-permute-done | bytes 884768 | tf_op jit(solution)/shard_map/ppermute | solution.py:257
  626.8 6.2 collective-permute-done.60
  637.7 4.6 collective-permute-done.98
  642.8 3.6 collective-permute-start.79
  648.1 4.2 collective-permute-start.100
  652.4 3.8 collective-permute-done.100
  657.2 3.7 collective-permute-done.64
  661.6 3.2 add_convert_fusion
  665.0 8.3 collective-permute-done.79
  675.4 3.0 collective-permute-start.80
  682.6 6.6 collective-permute-done.80
  689.2 6.3 collective-permute-done.81
  696.8 8.4 collective-permute-done.88
  713.0 3.7 collective-permute-done.89
  718.4 6.3 collective-permute-done.91
  724.7 17.0 %collective-permute-done.90 = bf16[576,384]{1,0:T(8,128)(2,1)S(1)} collective-permute-done((bf16[576,384]{1,0:T(8,128)(2,1)S(1)}, bf16[576,384]{1,0:T(8,128)(2,1)S(1)}, u32[]{:S(2)}, u32[]{:S(2)}) %collective-permute-start.90) | collective-permute-done | bytes 442400 | tf_op jit(solution)/shard_map/ppermute | solution.py:257
  743.1 20.5 %collective-permute-done.92 = bf16[576,384]{1,0:T(8,128)(2,1)S(1)} collective-permute-done((bf16[576,384]{1,0:T(8,128)(2,1)S(1)}, bf16[576,384]{1,0:T(8,128)(2,1)S(1)}, u32[]{:S(2)}, u32[]{:S(2)}) %collective-permute-start.92) | collective-permute-done | bytes 442400 | tf_op jit(solution)/shard_map/ppermute | solution.py:257
  770.1 35.3 %collective-permute-done.111 = bf16[4,96,1152]{2,1,0:T(8,128)(2,1)S(1)} collective-permute-done((bf16[4,96,1152]{2,1,0:T(8,128)(2,1)S(1)}, bf16[4,96,1152]{2,1,0:T(8,128)(2,1)S(1)}, u32[]{:S(2)}, u32[]{:S(2)}) %collective-permute-start.111) | collective-permute-done | bytes 884768 | tf_op jit(solution)/shard_map/ppermute | solution.py:257
  812.4 6.8 collective-permute-done.112
  819.1 20.2 %collective-permute-done.113 = bf16[96,1152]{1,0:T(8,128)(2,1)S(1)} collective-permute-done((bf16[96,1152]{1,0:T(8,128)(2,1)S(1)}, bf16[96,1152]{1,0:T(8,128)(2,1)S(1)}, u32[]{:S(2)}, u32[]{:S(2)}) %collective-permute-start.113) | collective-permute-done | bytes 221216 | tf_op jit(solution)/shard_map/ppermute | solution.py:257
  840.4 6.7 collective-permute-done.121
  848.6 4.7 collective-permute-done.123
  (845 shorter events, 290.9 us)
Async XLA Ops:
  2.7 43.8 %collective-permute-start.15 = (bf16[48,1152]{1,0:T(8,128)(2,1)}, bf16[48,1152]{1,0:T(8,128)(2,1)}, u32[]{:S(2)}, u32[]{:S(2)}) collective-permute-start(bf16[48,1152]{1,0:T(8,128)(2,1)} %fusion.123), channel_id=1, source_target_pairs={{0,4},{1,5},{2,6},{3,7},{4,0},{5,1},{6,2},{7,3},{8,12},{9,13},{10,... | collective-permute-start | bytes 331784 | tf_op jit(solution)/shard_map/ppermute | solution.py:257
  6.7 39.7 %collective-permute-start.14 = (bf16[48,1152]{1,0:T(8,128)(2,1)}, bf16[48,1152]{1,0:T(8,128)(2,1)}, u32[]{:S(2)}, u32[]{:S(2)}) collective-permute-start(bf16[48,1152]{1,0:T(8,128)(2,1)} %fusion.123), channel_id=1, source_target_pairs={{0,2},{1,3},{2,0},{3,1},{4,6},{5,7},{6,4},{7,5},{8,10},{9,11},{10,... | collective-permute-start | bytes 331784 | tf_op jit(solution)/shard_map/ppermute | solution.py:257
  20.2 23.2 %collective-permute-start.1 = (bf16[96,1152]{1,0:T(8,128)(2,1)S(1)}, bf16[96,1152]{1,0:T(8,128)(2,1)S(1)}, u32[]{:S(2)}, u32[]{:S(2)}) collective-permute-start(bf16[96,1152]{1,0:T(8,128)(2,1)S(1)} %copy-done.93), channel_id=1, source_target_pairs={{0,4},{1,5},{2,6},{3,7},{4,0},{5,1},{6,2},{7,3},{8,12},{9,13},{10,... | collective-permute-start | bytes 663560 | tf_op jit(solution)/shard_map/ppermute | solution.py:257
  21.5 24.3 %collective-permute-start = (bf16[96,1152]{1,0:T(8,128)(2,1)S(1)}, bf16[96,1152]{1,0:T(8,128)(2,1)S(1)}, u32[]{:S(2)}, u32[]{:S(2)}) collective-permute-start(bf16[96,1152]{1,0:T(8,128)(2,1)S(1)} %copy-done.93), channel_id=1, source_target_pairs={{0,2},{1,3},{2,0},{3,1},{4,6},{5,7},{6,4},{7,5},{8,10},{9,11},{10,... | collective-permute-start | bytes 663560 | tf_op jit(solution)/shard_map/ppermute | solution.py:257
  47.5 49.2 %collective-permute-start.19 = (bf16[480,384]{1,0:T(8,128)(2,1)S(1)}, bf16[480,384]{1,0:T(8,128)(2,1)S(1)}, u32[]{:S(2)}, u32[]{:S(2)}) collective-permute-start(bf16[480,384]{1,0:T(8,128)(2,1)S(1)} %pad_maximum_fusion.15), channel_id=1, source_target_pairs={{0,6},{1,7},{2,4},{3,5},{4,2},{5,3},{6,0},{7,1},{8,14},{9,15},{10,... | collective-permute-start | bytes 1105928 | tf_op jit(solution)/shard_map/ppermute | solution.py:257
  51.1 47.2 %collective-permute-start.18 = (bf16[480,384]{1,0:T(8,128)(2,1)S(1)}, bf16[480,384]{1,0:T(8,128)(2,1)S(1)}, u32[]{:S(2)}, u32[]{:S(2)}) collective-permute-start(bf16[480,384]{1,0:T(8,128)(2,1)S(1)} %pad_maximum_fusion.15), channel_id=1, source_target_pairs={{0,4},{1,5},{2,6},{3,7},{4,0},{5,1},{6,2},{7,3},{8,12},{9,13},{10,... | collective-permute-start | bytes 1105928 | tf_op jit(solution)/shard_map/ppermute | solution.py:257
  51.1 47.2 %collective-permute-start.17 = (bf16[480,384]{1,0:T(8,128)(2,1)S(1)}, bf16[480,384]{1,0:T(8,128)(2,1)S(1)}, u32[]{:S(2)}, u32[]{:S(2)}) collective-permute-start(bf16[480,384]{1,0:T(8,128)(2,1)S(1)} %pad_maximum_fusion.15), channel_id=1, source_target_pairs={{0,2},{1,3},{2,0},{3,1},{4,6},{5,7},{6,4},{7,5},{8,10},{9,11},{10,... | collective-permute-start | bytes 1105928 | tf_op jit(solution)/shard_map/ppermute | solution.py:257
  52.0 43.1 %collective-permute-start.24 = (bf16[96,1152]{1,0:T(8,128)(2,1)S(1)}, bf16[96,1152]{1,0:T(8,128)(2,1)S(1)}, u32[]{:S(2)}, u32[]{:S(2)}) collective-permute-start(bf16[96,1152]{1,0:T(8,128)(2,1)S(1)} %get-tuple-element.65), channel_id=1, source_target_pairs={{0,4},{1,5},{2,6},{3,7},{4,0},{5,1},{6,2},{7,3},{8,12},{9,13},{10,... | collective-permute-start | bytes 663560 | tf_op jit(solution)/shard_map/ppermute | solution.py:257
  56.3 38.8 %collective-permute-start.23 = (bf16[96,1152]{1,0:T(8,128)(2,1)S(1)}, bf16[96,1152]{1,0:T(8,128)(2,1)S(1)}, u32[]{:S(2)}, u32[]{:S(2)}) collective-permute-start(bf16[96,1152]{1,0:T(8,128)(2,1)S(1)} %get-tuple-element.65), channel_id=1, source_target_pairs={{0,2},{1,3},{2,0},{3,1},{4,6},{5,7},{6,4},{7,5},{8,10},{9,11},{10,... | collective-permute-start | bytes 663560 | tf_op jit(solution)/shard_map/ppermute | solution.py:257
  98.3 30.2 %collective-permute-start.27 = (bf16[96,1536]{1,0:T(8,128)(2,1)S(1)}, bf16[96,1536]{1,0:T(8,128)(2,1)S(1)}, u32[]{:S(2)}, u32[]{:S(2)}) collective-permute-start(bf16[96,1536]{1,0:T(8,128)(2,1)S(1)} %constant_dynamic-slice_fusion.3), channel_id=1, source_target_pairs={{0,4},{1,5},{2,6},{3,7},{4,0},{5,1},{6,2},{7,3},{8,12},{9,13},{10,... | collective-permute-start | bytes 884744 | tf_op jit(solution)/shard_map/ppermute | solution.py:257
  98.3 30.2 %collective-permute-start.26 = (bf16[96,1536]{1,0:T(8,128)(2,1)S(1)}, bf16[96,1536]{1,0:T(8,128)(2,1)S(1)}, u32[]{:S(2)}, u32[]{:S(2)}) collective-permute-start(bf16[96,1536]{1,0:T(8,128)(2,1)S(1)} %constant_dynamic-slice_fusion.3), channel_id=1, source_target_pairs={{0,2},{1,3},{2,0},{3,1},{4,6},{5,7},{6,4},{7,5},{8,10},{9,11},{10,... | collective-permute-start | bytes 884744 | tf_op jit(solution)/shard_map/ppermute | solution.py:257
  102.6 60.7 %collective-permute-start.6 = (bf16[4,96,1152]{2,1,0:T(8,128)(2,1)S(1)}, bf16[4,96,1152]{2,1,0:T(8,128)(2,1)S(1)}, u32[]{:S(2)}, u32[]{:S(2)}) collective-permute-start(bf16[4,96,1152]{2,1,0:T(8,128)(2,1)S(1)} %pad_maximum_fusion.6.refs_0_), channel_id=1, source_target_pairs={{0,8},{8,0},{16,24},{24,16},{1,9},{9,1},{17,25},{25,17},{2,10},{10... | collective-permute-start | bytes 2654216 | tf_op jit(solution)/shard_map/ppermute | solution.py:257
  107.7 56.3 %collective-permute-start.4 = (bf16[4,96,1152]{2,1,0:T(8,128)(2,1)S(1)}, bf16[4,96,1152]{2,1,0:T(8,128)(2,1)S(1)}, u32[]{:S(2)}, u32[]{:S(2)}) collective-permute-start(bf16[4,96,1152]{2,1,0:T(8,128)(2,1)S(1)} %pad_maximum_fusion.6.refs_0_), channel_id=1, source_target_pairs={{0,16},{8,24},{16,0},{24,8},{1,17},{9,25},{17,1},{25,9},{2,18},{10... | collective-permute-start | bytes 2654216 | tf_op jit(solution)/shard_map/ppermute | solution.py:257
  109.2 22.4 %collective-permute-start.50 = (bf16[96,1152]{1,0:T(8,128)(2,1)S(1)}, bf16[96,1152]{1,0:T(8,128)(2,1)S(1)}, u32[]{:S(2)}, u32[]{:S(2)}) collective-permute-start(bf16[96,1152]{1,0:T(8,128)(2,1)S(1)} %get-tuple-element.73), channel_id=1, source_target_pairs={{0,6},{1,7},{2,4},{3,5},{4,2},{5,3},{6,0},{7,1},{8,14},{9,15},{10,... | collective-permute-start | bytes 663560 | tf_op jit(solution)/shard_map/ppermute | solution.py:257
  128.5 17.4 %collective-permute-start.49 = (bf16[96,1152]{1,0:T(8,128)(2,1)S(1)}, bf16[96,1152]{1,0:T(8,128)(2,1)S(1)}, u32[]{:S(2)}, u32[]{:S(2)}) collective-permute-start(bf16[96,1152]{1,0:T(8,128)(2,1)S(1)} %get-tuple-element.73), channel_id=1, source_target_pairs={{0,4},{1,5},{2,6},{3,7},{4,0},{5,1},{6,2},{7,3},{8,12},{9,13},{10,... | collective-permute-start | bytes 663560 | tf_op jit(solution)/shard_map/ppermute | solution.py:257
  145.9 22.7 %collective-permute-start.3 = (bf16[4,96,1152]{2,1,0:T(8,128)(2,1)S(1)}, bf16[4,96,1152]{2,1,0:T(8,128)(2,1)}, u32[]{:S(2)}, u32[]{:S(2)}) collective-permute-start(bf16[4,96,1152]{2,1,0:T(8,128)(2,1)S(1)} %pad_maximum_fusion.6.refs_0_), channel_id=1, source_target_pairs={{0,1},{1,0},{2,3},{3,2},{4,5},{5,4},{6,7},{7,6},{8,9},{9,8},{10,11... | collective-permute-start | bytes 2654216 | tf_op jit(solution)/shard_map/ppermute | solution.py:257
  161.8 22.1 %collective-permute-start.42 = (bf16[4,96,1152]{2,1,0:T(8,128)(2,1)S(1)}, bf16[4,96,1152]{2,1,0:T(8,128)(2,1)S(1)}, u32[]{:S(2)}, u32[]{:S(2)}) collective-permute-start(bf16[4,96,1152]{2,1,0:T(8,128)(2,1)S(1)} %pad_maximum_fusion.7.refs_0_), channel_id=1, source_target_pairs={{0,16},{8,24},{16,0},{24,8},{1,17},{9,25},{17,1},{25,9},{2,18},{10... | collective-permute-start | bytes 2654216 | tf_op jit(solution)/shard_map/ppermute | solution.py:257
  163.3 24.1 %collective-permute-start.41 = (bf16[4,96,1152]{2,1,0:T(8,128)(2,1)S(1)}, bf16[4,96,1152]{2,1,0:T(8,128)(2,1)S(1)}, u32[]{:S(2)}, u32[]{:S(2)}) collective-permute-start(bf16[4,96,1152]{2,1,0:T(8,128)(2,1)S(1)} %pad_maximum_fusion.7.refs_0_), channel_id=1, source_target_pairs={{0,1},{1,0},{2,3},{3,2},{4,5},{5,4},{6,7},{7,6},{8,9},{9,8},{10,11... | collective-permute-start | bytes 2654216 | tf_op jit(solution)/shard_map/ppermute | solution.py:257
  164.0 23.4 %collective-permute-start.36 = (bf16[4,192,384]{2,1,0:T(8,128)(2,1)S(1)}, bf16[4,192,384]{2,1,0:T(8,128)(2,1)S(1)}, u32[]{:S(2)}, u32[]{:S(2)}) collective-permute-start(bf16[4,192,384]{2,1,0:T(8,128)(2,1)S(1)} %pad_maximum_fusion.10.refs_0_), channel_id=1, source_target_pairs={{0,8},{8,0},{16,24},{24,16},{1,9},{9,1},{17,25},{25,17},{2,10},{10... | collective-permute-start | bytes 1769480 | tf_op jit(solution)/shard_map/ppermute | solution.py:257
  168.6 32.2 %collective-permute-start.54 = (bf16[4,96,1152]{2,1,0:T(8,128)(2,1)S(1)}, bf16[4,96,1152]{2,1,0:T(8,128)(2,1)}, u32[]{:S(2)}, u32[]{:S(2)}) collective-permute-start(bf16[4,96,1152]{2,1,0:T(8,128)(2,1)S(1)} %pad_maximum_fusion.8.refs_0_), channel_id=1, source_target_pairs={{0,8},{8,0},{16,24},{24,16},{1,9},{9,1},{17,25},{25,17},{2,10},{10... | collective-permute-start | bytes 2654216 | tf_op jit(solution)/shard_map/ppermute | solution.py:257
  168.6 31.5 %collective-permute-start.35 = (bf16[4,192,384]{2,1,0:T(8,128)(2,1)S(1)}, bf16[4,192,384]{2,1,0:T(8,128)(2,1)S(1)}, u32[]{:S(2)}, u32[]{:S(2)}) collective-permute-start(bf16[4,192,384]{2,1,0:T(8,128)(2,1)S(1)} %pad_maximum_fusion.10.refs_0_), channel_id=1, source_target_pairs={{0,1},{1,0},{2,3},{3,2},{4,5},{5,4},{6,7},{7,6},{8,9},{9,8},{10,11... | collective-permute-start | bytes 1769480 | tf_op jit(solution)/shard_map/ppermute | solution.py:257
  183.8 22.6 %collective-permute-start.52 = (bf16[4,96,1152]{2,1,0:T(8,128)(2,1)S(1)}, bf16[4,96,1152]{2,1,0:T(8,128)(2,1)}, u32[]{:S(2)}, u32[]{:S(2)}) collective-permute-start(bf16[4,96,1152]{2,1,0:T(8,128)(2,1)S(1)} %pad_maximum_fusion.8.refs_0_), channel_id=1, source_target_pairs={{0,16},{8,24},{16,0},{24,8},{1,17},{9,25},{17,1},{25,9},{2,18},{10... | collective-permute-start | bytes 2654216 | tf_op jit(solution)/shard_map/ppermute | solution.py:257
  187.5 63.5 %collective-permute-start.30 = (bf16[4,96,1536]{2,1,0:T(8,128)(2,1)S(1)}, bf16[4,96,1536]{2,1,0:T(8,128)(2,1)}, u32[]{:S(2)}, u32[]{:S(2)}) collective-permute-start(bf16[4,96,1536]{2,1,0:T(8,128)(2,1)S(1)} %pad_maximum_fusion.4.refs_0_), channel_id=1, source_target_pairs={{0,8},{8,0},{16,24},{24,16},{1,9},{9,1},{17,25},{25,17},{2,10},{10... | collective-permute-start | bytes 3538952 | tf_op jit(solution)/shard_map/ppermute | solution.py:257
  187.5 63.6 %collective-permute-start.29 = (bf16[4,96,1536]{2,1,0:T(8,128)(2,1)S(1)}, bf16[4,96,1536]{2,1,0:T(8,128)(2,1)}, u32[]{:S(2)}, u32[]{:S(2)}) collective-permute-start(bf16[4,96,1536]{2,1,0:T(8,128)(2,1)S(1)} %pad_maximum_fusion.4.refs_0_), channel_id=1, source_target_pairs={{0,1},{1,0},{2,3},{3,2},{4,5},{5,4},{6,7},{7,6},{8,9},{9,8},{10,11... | collective-permute-start | bytes 3538952 | tf_op jit(solution)/shard_map/ppermute | solution.py:257
  200.1 43.9 %collective-permute-start.51 = (bf16[4,96,1152]{2,1,0:T(8,128)(2,1)S(1)}, bf16[4,96,1152]{2,1,0:T(8,128)(2,1)}, u32[]{:S(2)}, u32[]{:S(2)}) collective-permute-start(bf16[4,96,1152]{2,1,0:T(8,128)(2,1)S(1)} %pad_maximum_fusion.8.refs_0_), channel_id=1, source_target_pairs={{0,1},{1,0},{2,3},{3,2},{4,5},{5,4},{6,7},{7,6},{8,9},{9,8},{10,11... | collective-permute-start | bytes 2654216 | tf_op jit(solution)/shard_map/ppermute | solution.py:257
  200.9 50.6 %collective-permute-start.5 = (bf16[4,96,1152]{2,1,0:T(8,128)(2,1)}, bf16[4,96,1152]{2,1,0:T(8,128)(2,1)S(1)}, u32[]{:S(2)}, u32[]{:S(2)}) collective-permute-start(bf16[4,96,1152]{2,1,0:T(8,128)(2,1)} %collective-permute-done.3.refs_1_), channel_id=1, source_target_pairs={{0,16},{8,24},{16,0},{24,8},{1,17},{9,25},{17,1},{25,9},{2,18},{10... | collective-permute-start | bytes 2654216 | tf_op jit(solution)/shard_map/ppermute | solution.py:257
  206.4 46.1 %collective-permute-start.8 = (bf16[4,96,1152]{2,1,0:T(8,128)(2,1)}, bf16[4,96,1152]{2,1,0:T(8,128)(2,1)}, u32[]{:S(2)}, u32[]{:S(2)}) collective-permute-start(bf16[4,96,1152]{2,1,0:T(8,128)(2,1)} %copy-done.77), channel_id=1, source_target_pairs={{0,8},{8,0},{16,24},{24,16},{1,9},{9,1},{17,25},{25,17},{2,10},{10... | collective-permute-start | bytes 2654216 | tf_op jit(solution)/shard_map/ppermute | solution.py:257
  244.0 38.7 %collective-permute-start.20 = (bf16[4,480,384]{2,1,0:T(8,128)(2,1)}, bf16[4,480,384]{2,1,0:T(8,128)(2,1)}, u32[]{:S(2)}, u32[]{:S(2)}) collective-permute-start(bf16[4,480,384]{2,1,0:T(8,128)(2,1)} %pad_maximum_fusion.2.refs_0_), channel_id=1, source_target_pairs={{0,1},{1,0},{2,3},{3,2},{4,5},{5,4},{6,7},{7,6},{8,9},{9,8},{10,11... | collective-permute-start | bytes 4423688 | tf_op jit(solution)/shard_map/ppermute | solution.py:257
  252.5 31.0 %collective-permute-start.43 = (bf16[4,96,1152]{2,1,0:T(8,128)(2,1)}, bf16[4,96,1152]{2,1,0:T(8,128)(2,1)}, u32[]{:S(2)}, u32[]{:S(2)}) collective-permute-start(bf16[4,96,1152]{2,1,0:T(8,128)(2,1)} %copy-done.86), channel_id=1, source_target_pairs={{0,16},{8,24},{16,0},{24,8},{1,17},{9,25},{17,1},{25,9},{2,18},{10... | collective-permute-start | bytes 2654216 | tf_op jit(solution)/shard_map/ppermute | solution.py:257
  255.7 31.8 %collective-permute-start.45 = (bf16[4,96,1152]{2,1,0:T(8,128)(2,1)}, bf16[4,96,1152]{2,1,0:T(8,128)(2,1)}, u32[]{:S(2)}, u32[]{:S(2)}) collective-permute-start(bf16[4,96,1152]{2,1,0:T(8,128)(2,1)} %copy-done.86), channel_id=1, source_target_pairs={{0,8},{8,0},{16,24},{24,16},{1,9},{9,1},{17,25},{25,17},{2,10},{10... | collective-permute-start | bytes 2654216 | tf_op jit(solution)/shard_map/ppermute | solution.py:257
  255.8 31.2 %collective-permute-start.46 = (bf16[4,96,1152]{2,1,0:T(8,128)(2,1)}, bf16[4,96,1152]{2,1,0:T(8,128)(2,1)}, u32[]{:S(2)}, u32[]{:S(2)}) collective-permute-start(bf16[4,96,1152]{2,1,0:T(8,128)(2,1)} %copy-done.85), channel_id=1, source_target_pairs={{0,8},{8,0},{16,24},{24,16},{1,9},{9,1},{17,25},{25,17},{2,10},{10... | collective-permute-start | bytes 2654216 | tf_op jit(solution)/shard_map/ppermute | solution.py:257
  256.4 49.1 %collective-permute-start.31 = (bf16[4,96,1536]{2,1,0:T(8,128)(2,1)}, bf16[4,96,1536]{2,1,0:T(8,128)(2,1)}, u32[]{:S(2)}, u32[]{:S(2)}) collective-permute-start(bf16[4,96,1536]{2,1,0:T(8,128)(2,1)} %collective-permute-done.29.refs_1_), channel_id=1, source_target_pairs={{0,8},{8,0},{16,24},{24,16},{1,9},{9,1},{17,25},{25,17},{2,10},{10... | collective-permute-start | bytes 3538952 | tf_op jit(solution)/shard_map/ppermute | solution.py:257
  282.7 22.3 %collective-permute-start.53 = (bf16[4,96,1152]{2,1,0:T(8,128)(2,1)}, bf16[4,96,1152]{2,1,0:T(8,128)(2,1)}, u32[]{:S(2)}, u32[]{:S(2)}) collective-permute-start(bf16[4,96,1152]{2,1,0:T(8,128)(2,1)} %collective-permute-done.51.refs_1_), channel_id=1, source_target_pairs={{0,16},{8,24},{16,0},{24,8},{1,17},{9,25},{17,1},{25,9},{2,18},{10... | collective-permute-start | bytes 2654216 | tf_op jit(solution)/shard_map/ppermute | solution.py:257
  283.6 21.4 %collective-permute-start.47 = (bf16[4,96,1152]{2,1,0:T(8,128)(2,1)}, bf16[4,96,1152]{2,1,0:T(8,128)(2,1)}, u32[]{:S(2)}, u32[]{:S(2)}) collective-permute-start(bf16[4,96,1152]{2,1,0:T(8,128)(2,1)} %collective-permute-done.43.refs_3_), channel_id=1, source_target_pairs={{0,8},{8,0},{16,24},{24,16},{1,9},{9,1},{17,25},{25,17},{2,10},{10... | collective-permute-start | bytes 2654216 | tf_op jit(solution)/shard_map/ppermute | solution.py:257
  287.0 65.6 %collective-permute-start.21 = (bf16[4,480,384]{2,1,0:T(8,128)(2,1)}, bf16[4,480,384]{2,1,0:T(8,128)(2,1)}, u32[]{:S(2)}, u32[]{:S(2)}) collective-permute-start(bf16[4,480,384]{2,1,0:T(8,128)(2,1)} %pad_maximum_fusion.2.refs_0_), channel_id=1, source_target_pairs={{0,8},{8,0},{16,24},{24,16},{1,9},{9,1},{17,25},{25,17},{2,10},{10... | collective-permute-start | bytes 4423688 | tf_op jit(solution)/shard_map/ppermute | solution.py:257
  287.5 65.1 %collective-permute-start.22 = (bf16[4,480,384]{2,1,0:T(8,128)(2,1)}, bf16[4,480,384]{2,1,0:T(8,128)(2,1)}, u32[]{:S(2)}, u32[]{:S(2)}) collective-permute-start(bf16[4,480,384]{2,1,0:T(8,128)(2,1)} %collective-permute-done.20.refs_1_), channel_id=1, source_target_pairs={{0,8},{8,0},{16,24},{24,16},{1,9},{9,1},{17,25},{25,17},{2,10},{10... | collective-permute-start | bytes 4423688 | tf_op jit(solution)/shard_map/ppermute | solution.py:257
  305.0 40.6 %collective-permute-start.55 = (bf16[4,96,1152]{2,1,0:T(8,128)(2,1)}, bf16[4,96,1152]{2,1,0:T(8,128)(2,1)}, u32[]{:S(2)}, u32[]{:S(2)}) collective-permute-start(bf16[4,96,1152]{2,1,0:T(8,128)(2,1)} %collective-permute-done.51.refs_1_), channel_id=1, source_target_pairs={{0,8},{8,0},{16,24},{24,16},{1,9},{9,1},{17,25},{25,17},{2,10},{10... | collective-permute-start | bytes 2654216 | tf_op jit(solution)/shard_map/ppermute | solution.py:257
  305.0 40.6 %collective-permute-start.56 = (bf16[4,96,1152]{2,1,0:T(8,128)(2,1)}, bf16[4,96,1152]{2,1,0:T(8,128)(2,1)}, u32[]{:S(2)}, u32[]{:S(2)}) collective-permute-start(bf16[4,96,1152]{2,1,0:T(8,128)(2,1)} %collective-permute-done.52.refs_2_), channel_id=1, source_target_pairs={{0,8},{8,0},{16,24},{24,16},{1,9},{9,1},{17,25},{25,17},{2,10},{10... | collective-permute-start | bytes 2654216 | tf_op jit(solution)/shard_map/ppermute | solution.py:257
  305.5 40.1 %collective-permute-start.57 = (bf16[4,96,1152]{2,1,0:T(8,128)(2,1)}, bf16[4,96,1152]{2,1,0:T(8,128)(2,1)}, u32[]{:S(2)}, u32[]{:S(2)}) collective-permute-start(bf16[4,96,1152]{2,1,0:T(8,128)(2,1)} %collective-permute-done.53.refs_3_), channel_id=1, source_target_pairs={{0,8},{8,0},{16,24},{24,16},{1,9},{9,1},{17,25},{25,17},{2,10},{10... | collective-permute-start | bytes 2654216 | tf_op jit(solution)/shard_map/ppermute | solution.py:257
  487.9 51.9 %collective-permute-start.102 = (bf16[384,1152]{1,0:T(8,128)(2,1)}, bf16[384,1152]{1,0:T(8,128)(2,1)}, u32[]{:S(2)}, u32[]{:S(2)}) collective-permute-start(bf16[384,1152]{1,0:T(8,128)(2,1)} %get-tuple-element.270), channel_id=1, source_target_pairs={{0,8},{8,0},{16,24},{24,16},{1,9},{9,1},{17,25},{25,17},{2,10},{10... | collective-permute-start | bytes 2654216 | tf_op jit(solution)/shard_map/ppermute | solution.py:257
  519.7 18.5 %collective-permute-start.85 = (bf16[768,384]{1,0:T(8,128)(2,1)}, bf16[768,384]{1,0:T(8,128)(2,1)}, u32[]{:S(2)}, u32[]{:S(2)}) collective-permute-start(bf16[768,384]{1,0:T(8,128)(2,1)} %convolution_convert_fusion.6), channel_id=1, source_target_pairs={{0,8},{8,0},{16,24},{24,16},{1,9},{9,1},{17,25},{25,17},{2,10},{10... | collective-permute-start | bytes 1769480 | tf_op jit(solution)/shard_map/ppermute | solution.py:257
  520.2 140.8 %collective-permute-start.117 = (bf16[1536,1152]{1,0:T(8,128)(2,1)}, bf16[1536,1152]{1,0:T(8,128)(2,1)}, u32[]{:S(2)}, u32[]{:S(2)}) collective-permute-start(bf16[1536,1152]{1,0:T(8,128)(2,1)} %convolution_convert_fusion), channel_id=1, source_target_pairs={{0,8},{8,0},{16,24},{24,16},{1,9},{9,1},{17,25},{25,17},{2,10},{10... | collective-permute-start | bytes 10616840 | tf_op jit(solution)/shard_map/ppermute | solution.py:257
  549.0 28.8 %collective-permute-start.94 = (bf16[768,1152]{1,0:T(8,128)(2,1)S(1)}, bf16[768,1152]{1,0:T(8,128)(2,1)S(1)}, u32[]{:S(2)}, u32[]{:S(2)}) collective-permute-start(bf16[768,1152]{1,0:T(8,128)(2,1)S(1)} %copy-done.57), channel_id=1, source_target_pairs={{0,8},{8,0},{16,24},{24,16},{1,9},{9,1},{17,25},{25,17},{2,10},{10... | collective-permute-start | bytes 5308424 | tf_op jit(solution)/shard_map/ppermute | solution.py:257
  562.2 22.7 %collective-permute-start.78 = (bf16[768,1536]{1,0:T(8,128)(2,1)S(1)}, bf16[768,1536]{1,0:T(8,128)(2,1)S(1)}, u32[]{:S(2)}, u32[]{:S(2)}) collective-permute-start(bf16[768,1536]{1,0:T(8,128)(2,1)S(1)} %copy-done.55), channel_id=1, source_target_pairs={{0,8},{8,0},{16,24},{24,16},{1,9},{9,1},{17,25},{25,17},{2,10},{10... | collective-permute-start | bytes 7077896 | tf_op jit(solution)/shard_map/ppermute | solution.py:257
  564.0 18.6 %collective-permute-start.87 = (bf16[3072,384]{1,0:T(8,128)(2,1)S(1)}, bf16[3072,384]{1,0:T(8,128)(2,1)S(1)}, u32[]{:S(2)}, u32[]{:S(2)}) collective-permute-start(bf16[3072,384]{1,0:T(8,128)(2,1)S(1)} %copy-done.22), channel_id=1, source_target_pairs={{0,8},{8,0},{16,24},{24,16},{1,9},{9,1},{17,25},{25,17},{2,10},{10... | collective-permute-start | bytes 7077896 | tf_op jit(solution)/shard_map/ppermute | solution.py:257
  577.8 103.3 %collective-permute-start.109 = (bf16[1536,1152]{1,0:T(8,128)(2,1)S(1)}, bf16[1536,1152]{1,0:T(8,128)(2,1)S(1)}, u32[]{:S(2)}, u32[]{:S(2)}) collective-permute-start(bf16[1536,1152]{1,0:T(8,128)(2,1)S(1)} %copy-done.14), channel_id=1, source_target_pairs={{0,8},{8,0},{16,24},{24,16},{1,9},{9,1},{17,25},{25,17},{2,10},{10... | collective-permute-start | bytes 10616840 | tf_op jit(solution)/shard_map/ppermute | solution.py:257
  580.5 22.5 %collective-permute-start.95 = (bf16[8,48,1152]{2,1,0:T(8,128)(2,1)S(1)}, bf16[8,48,1152]{2,1,0:T(8,128)(2,1)S(1)}, u32[]{:S(2)}, u32[]{:S(2)}) collective-permute-start(bf16[8,48,1152]{2,1,0:T(8,128)(2,1)S(1)} %dynamic-slice_bitcast_fusion.7), channel_id=1, source_target_pairs={{0,16},{8,24},{16,0},{24,8},{1,17},{9,25},{17,1},{25,9},{2,18},{10... | collective-permute-start | bytes 2654216 | tf_op jit(solution)/shard_map/ppermute | solution.py:257
  582.5 38.6 %collective-permute-start.59 = (bf16[8,48,1152]{2,1,0:T(8,128)(2,1)S(1)}, bf16[8,48,1152]{2,1,0:T(8,128)(2,1)S(1)}, u32[]{:S(2)}, u32[]{:S(2)}) collective-permute-start(bf16[8,48,1152]{2,1,0:T(8,128)(2,1)S(1)} %dynamic-slice_bitcast_fusion.8), channel_id=1, source_target_pairs={{0,16},{8,24},{16,0},{24,8},{1,17},{9,25},{17,1},{25,9},{2,18},{10... | collective-permute-start | bytes 2654216 | tf_op jit(solution)/shard_map/ppermute | solution.py:257
  603.3 20.1 %collective-permute-start.96 = (bf16[4,48,1152]{2,1,0:T(8,128)(2,1)S(1)}, bf16[4,48,1152]{2,1,0:T(8,128)(2,1)S(1)}, u32[]{:S(2)}, u32[]{:S(2)}) collective-permute-start(bf16[4,48,1152]{2,1,0:T(8,128)(2,1)S(1)} %dynamic-slice_bitcast_fusion.10), channel_id=1, source_target_pairs={{0,1},{1,0},{2,3},{3,2},{4,5},{5,4},{6,7},{7,6},{8,9},{9,8},{10,11... | collective-permute-start | bytes 1327112 | tf_op jit(solution)/shard_map/ppermute | solution.py:257
  642.8 30.5 %collective-permute-start.79 = (bf16[4,96,1536]{2,1,0:T(8,128)(2,1)S(1)}, bf16[4,96,1536]{2,1,0:T(8,128)(2,1)S(1)}, u32[]{:S(2)}, u32[]{:S(2)}) collective-permute-start(bf16[4,96,1536]{2,1,0:T(8,128)(2,1)S(1)} %dynamic-slice_bitcast_fusion.4), channel_id=1, source_target_pairs={{0,1},{1,0},{2,3},{3,2},{4,5},{5,4},{6,7},{7,6},{8,9},{9,8},{10,11... | collective-permute-start | bytes 3538952 | tf_op jit(solution)/shard_map/ppermute | solution.py:257
  646.5 58.7 %collective-permute-start.88 = (bf16[4,576,384]{2,1,0:T(8,128)(2,1)S(1)}, bf16[4,576,384]{2,1,0:T(8,128)(2,1)S(1)}, u32[]{:S(2)}, u32[]{:S(2)}) collective-permute-start(bf16[4,576,384]{2,1,0:T(8,128)(2,1)S(1)} %pad_maximum_fusion.1), channel_id=1, source_target_pairs={{0,1},{1,0},{2,3},{3,2},{4,5},{5,4},{6,7},{7,6},{8,9},{9,8},{10,11... | collective-permute-start | bytes 5308424 | tf_op jit(solution)/shard_map/ppermute | solution.py:257
  661.0 17.6 %collective-permute-start.65 = (bf16[96,1152]{1,0:T(8,128)(2,1)S(1)}, bf16[96,1152]{1,0:T(8,128)(2,1)S(1)}, u32[]{:S(2)}, u32[]{:S(2)}) collective-permute-start(bf16[96,1152]{1,0:T(8,128)(2,1)S(1)} %pad_maximum_fusion.17), channel_id=1, source_target_pairs={{0,8},{8,0},{16,24},{24,16},{1,9},{9,1},{17,25},{25,17},{2,10},{10... | collective-permute-start | bytes 663560 | tf_op jit(solution)/shard_map/ppermute | solution.py:257
  673.3 90.6 %collective-permute-start.118 = (bf16[8,96,1152]{2,1,0:T(8,128)(2,1)S(1)}, bf16[8,96,1152]{2,1,0:T(8,128)(2,1)S(1)}, u32[]{:S(2)}, u32[]{:S(2)}) collective-permute-start(bf16[8,96,1152]{2,1,0:T(8,128)(2,1)S(1)} %dynamic-slice_bitcast_fusion), channel_id=1, source_target_pairs={{0,16},{8,24},{16,0},{24,8},{1,17},{9,25},{17,1},{25,9},{2,18},{10... | collective-permute-start | bytes 5308424 | tf_op jit(solution)/shard_map/ppermute | solution.py:257
  705.9 18.8 %collective-permute-start.91 = (bf16[576,384]{1,0:T(8,128)(2,1)S(1)}, bf16[576,384]{1,0:T(8,128)(2,1)S(1)}, u32[]{:S(2)}, u32[]{:S(2)}) collective-permute-start(bf16[576,384]{1,0:T(8,128)(2,1)S(1)} %get-tuple-element.139), channel_id=1, source_target_pairs={{0,6},{1,7},{2,4},{3,5},{4,2},{5,3},{6,0},{7,1},{8,14},{9,15},{10,... | collective-permute-start | bytes 1327112 | tf_op jit(solution)/shard_map/ppermute | solution.py:257
  708.1 33.6 %collective-permute-start.90 = (bf16[576,384]{1,0:T(8,128)(2,1)S(1)}, bf16[576,384]{1,0:T(8,128)(2,1)S(1)}, u32[]{:S(2)}, u32[]{:S(2)}) collective-permute-start(bf16[576,384]{1,0:T(8,128)(2,1)S(1)} %get-tuple-element.140), channel_id=1, source_target_pairs={{0,4},{1,5},{2,6},{3,7},{4,0},{5,1},{6,2},{7,3},{8,12},{9,13},{10,... | collective-permute-start | bytes 1327112 | tf_op jit(solution)/shard_map/ppermute | solution.py:257
  712.0 30.0 %collective-permute-start.84 = (bf16[96,1536]{1,0:T(8,128)(2,1)S(1)}, bf16[96,1536]{1,0:T(8,128)(2,1)S(1)}, u32[]{:S(2)}, u32[]{:S(2)}) collective-permute-start(bf16[96,1536]{1,0:T(8,128)(2,1)S(1)} %add_convert_fusion.13), channel_id=1, source_target_pairs={{0,8},{8,0},{16,24},{24,16},{1,9},{9,1},{17,25},{25,17},{2,10},{10... | collective-permute-start | bytes 884744 | tf_op jit(solution)/shard_map/ppermute | solution.py:257
  716.8 48.9 %collective-permute-start.110 = (bf16[8,96,1152]{2,1,0:T(8,128)(2,1)S(1)}, bf16[8,96,1152]{2,1,0:T(8,128)(2,1)S(1)}, u32[]{:S(2)}, u32[]{:S(2)}) collective-permute-start(bf16[8,96,1152]{2,1,0:T(8,128)(2,1)S(1)} %dynamic-slice_bitcast_fusion.1), channel_id=1, source_target_pairs={{0,16},{8,24},{16,0},{24,8},{1,17},{9,25},{17,1},{25,9},{2,18},{10... | collective-permute-start | bytes 5308424 | tf_op jit(solution)/shard_map/ppermute | solution.py:257
  741.9 21.8 %collective-permute-start.92 = (bf16[576,384]{1,0:T(8,128)(2,1)S(1)}, bf16[576,384]{1,0:T(8,128)(2,1)S(1)}, u32[]{:S(2)}, u32[]{:S(2)}) collective-permute-start(bf16[576,384]{1,0:T(8,128)(2,1)S(1)} %fusion.52), channel_id=1, source_target_pairs={{0,16},{8,24},{16,0},{24,8},{1,17},{9,25},{17,1},{25,9},{2,18},{10... | collective-permute-start | bytes 1327112 | tf_op jit(solution)/shard_map/ppermute | solution.py:257
  764.4 44.9 %collective-permute-start.119 = (bf16[4,96,1152]{2,1,0:T(8,128)(2,1)S(1)}, bf16[4,96,1152]{2,1,0:T(8,128)(2,1)S(1)}, u32[]{:S(2)}, u32[]{:S(2)}) collective-permute-start(bf16[4,96,1152]{2,1,0:T(8,128)(2,1)S(1)} %dynamic-slice_bitcast_fusion.5), channel_id=1, source_target_pairs={{0,1},{1,0},{2,3},{3,2},{4,5},{5,4},{6,7},{7,6},{8,9},{9,8},{10,11... | collective-permute-start | bytes 2654216 | tf_op jit(solution)/shard_map/ppermute | solution.py:257
  766.2 39.2 %collective-permute-start.111 = (bf16[4,96,1152]{2,1,0:T(8,128)(2,1)S(1)}, bf16[4,96,1152]{2,1,0:T(8,128)(2,1)S(1)}, u32[]{:S(2)}, u32[]{:S(2)}) collective-permute-start(bf16[4,96,1152]{2,1,0:T(8,128)(2,1)S(1)} %dynamic-slice_bitcast_fusion.6), channel_id=1, source_target_pairs={{0,1},{1,0},{2,3},{3,2},{4,5},{5,4},{6,7},{7,6},{8,9},{9,8},{10,11... | collective-permute-start | bytes 2654216 | tf_op jit(solution)/shard_map/ppermute | solution.py:257
  807.6 31.7 %collective-permute-start.113 = (bf16[96,1152]{1,0:T(8,128)(2,1)S(1)}, bf16[96,1152]{1,0:T(8,128)(2,1)S(1)}, u32[]{:S(2)}, u32[]{:S(2)}) collective-permute-start(bf16[96,1152]{1,0:T(8,128)(2,1)S(1)} %get-tuple-element.156), channel_id=1, source_target_pairs={{0,4},{1,5},{2,6},{3,7},{4,0},{5,1},{6,2},{7,3},{8,12},{9,13},{10,... | collective-permute-start | bytes 663560 | tf_op jit(solution)/shard_map/ppermute | solution.py:257
  809.6 30.8 %collective-permute-start.120 = (bf16[96,1152]{1,0:T(8,128)(2,1)S(1)}, bf16[96,1152]{1,0:T(8,128)(2,1)S(1)}, u32[]{:S(2)}, u32[]{:S(2)}) collective-permute-start(bf16[96,1152]{1,0:T(8,128)(2,1)S(1)} %get-tuple-element.159), channel_id=1, source_target_pairs={{0,2},{1,3},{2,0},{3,1},{4,6},{5,7},{6,4},{7,5},{8,10},{9,11},{10,... | collective-permute-start | bytes 663560 | tf_op jit(solution)/shard_map/ppermute | solution.py:257
  810.7 29.8 %collective-permute-start.122 = (bf16[96,1152]{1,0:T(8,128)(2,1)S(1)}, bf16[96,1152]{1,0:T(8,128)(2,1)S(1)}, u32[]{:S(2)}, u32[]{:S(2)}) collective-permute-start(bf16[96,1152]{1,0:T(8,128)(2,1)S(1)} %get-tuple-element.160), channel_id=1, source_target_pairs={{0,6},{1,7},{2,4},{3,5},{4,2},{5,3},{6,0},{7,1},{8,14},{9,15},{10,... | collective-permute-start | bytes 663560 | tf_op jit(solution)/shard_map/ppermute | solution.py:257
  819.1 28.0 %collective-permute-start.121 = (bf16[96,1152]{1,0:T(8,128)(2,1)S(1)}, bf16[96,1152]{1,0:T(8,128)(2,1)S(1)}, u32[]{:S(2)}, u32[]{:S(2)}) collective-permute-start(bf16[96,1152]{1,0:T(8,128)(2,1)S(1)} %get-tuple-element.161), channel_id=1, source_target_pairs={{0,4},{1,5},{2,6},{3,7},{4,0},{5,1},{6,2},{7,3},{8,12},{9,13},{10,... | collective-permute-start | bytes 663560 | tf_op jit(solution)/shard_map/ppermute | solution.py:257
  (242 other events, 2754.0 us)
where the time goes:
time: 869 us; the launch traced here: 859 us
  waiting for transfers between devices  418 us (48%)
  starting transfers between devices  133 us (15%)
  matrix products  108 us (12%)
  Pallas kernels  77.8 us (9%)
  local copies, waits for them, and re-layouts  70.1 us (8%)
  other arithmetic  45.8 us (5%)
    ppermute x125, waiting for transfers between devices, exchange(): return lax.ppermute(value, axis, pairs)  418 us
    ppermute x125, starting transfers between devices, exchange(): return lax.ppermute(value, axis, pairs)  133 us
    dot_general x20, matrix products, left_product(): lax.dot_general(left, right, (((0,), (0,)), ((), ())), preferred_element_...  56.4 us
    pallas_call x7, Pallas kernels, put_together(): pl.pallas_call(body, out_shape=[jax.ShapeDtypeStruct((blocks, count, 2 *...  40.3 us
    dot_general x10, matrix products, right_product(): lax.dot_general(left, right, (((1,), (1,)), ((), ())), preferred_element_...  25.4 us
    pallas_call x1, Pallas kernels, recurrent_forward(): pl.pallas_call(body, grid=(letter_slots,), in_specs=[pl.BlockSpec((1, row...  20.7 us
    dot_general x8, matrix products, product(): return jnp.dot(left, right, preferred_element_type=jnp.float32)  20 us
  transfers between devices with their start and end apart: 125, of which 54 were waited for; matrix products, arithmetic and copies ran while one was open for 12% of the time, Pallas kernels for 6%

commit v1 on v0

--- a/solution.py
+++ b/solution.py
@@ -10,6 +10,10 @@
 
 
 EPS = 1e-05
+
+SHARD = "shard"
+REP = "rep"
+BOTH = (REP, SHARD)
 
 
 def product(left, right):
@@ -137,7 +141,7 @@
             jax.ShapeDtypeStruct((rows, 2 * hidden), jnp.float32),
         ],
         scratch_shapes=[pltpu.VMEM((rows, 2 * hidden), jnp.float32)],
-        name="recurrent_forward",
+        name="recurrent",
     )(slots, slots, gin, ghid, sin, shid, counts)
 
 
@@ -246,7 +250,7 @@
             jax.ShapeDtypeStruct((1, 2 * gates), jnp.float32),
         ],
         scratch_shapes=[pltpu.VMEM((rows, 2 * hidden), jnp.float32)],
-        name="recurrent_backward",
+        name="recurrent_back",
     )(*saved_gates, *saved_states, ghid, counts, delta)
 
 
@@ -259,12 +263,12 @@
 
 class Place:
     def __init__(self):
-        self.rep_size = lax.axis_size("rep")
-        self.shard_size = lax.axis_size("shard")
+        self.rep_size = lax.axis_size(REP)
+        self.shard_size = lax.axis_size(SHARD)
         self.depth = DEPTH_SIZE
         self.height = self.shard_size // DEPTH_SIZE
-        rep_at = lax.axis_index("rep")
-        shard_at = lax.axis_index("shard")
+        rep_at = lax.axis_index(REP)
+        shard_at = lax.axis_index(SHARD)
         self.shard_at = shard_at
         self.core = rep_at % 2
         self.side = (rep_at // 2) % 2
@@ -273,20 +277,20 @@
         self.coords = jnp.stack([self.layer, self.row, self.side, self.core]).astype(jnp.int32)
 
     def over_core(self, value):
-        return exchange(value, "rep", [(i, i ^ 1) for i in range(self.rep_size)])
+        return exchange(value, REP, [(i, i ^ 1) for i in range(self.rep_size)])
 
     def over_side(self, value):
-        return exchange(value, "rep", [(i, i ^ 2) for i in range(self.rep_size)])
+        return exchange(value, REP, [(i, i ^ 2) for i in range(self.rep_size)])
 
     def over_far(self, value, step):
-        return exchange(value, "rep", [(i, (i + 4 * step) % self.rep_size) for i in range(self.rep_size)]
+        return exchange(value, REP, [(i, (i + 4 * step) % self.rep_size) for i in range(self.rep_size)]
         )
 
     def over_row(self, value, step):
-        return exchange(value, "shard", [(i, i ^ step) for i in range(self.shard_size)])
+        return exchange(value, SHARD, [(i, i ^ step) for i in range(self.shard_size)])
 
     def over_layer(self, value, step):
-        return exchange(value, "shard", [(i, i ^ (step * self.height)) for i in range(self.shard_size)]
+        return exchange(value, SHARD, [(i, i ^ (step * self.height)) for i in range(self.shard_size)]
         )
 
 
@@ -344,7 +348,7 @@
     return [w.reshape(r * place.shard_size, 2 * half) for w, r in zip(whole, rows)]
 
 
-def gathered(place, shards_in, split, after=None):
+def gathered(place, shards_in, split):
     half = shards_in[0].shape[1] // 2
     pieces = []
     for shard in shards_in:
@@ -352,8 +356,6 @@
         top = place.side * part_rows if split else 0
         pieces.append(lax.dynamic_slice(shard, (top, place.core * half), (part_rows, half)))
     piece = pieces[0] if len(pieces) == 1 else jnp.concatenate(pieces, axis=0)
-    if after is not None:
-        piece = hold(piece, after)
     layers = jnp.stack([piece] + [place.over_layer(piece, step) for step in range(1, place.depth)])
     column = [layers] + [place.over_row(layers, step) for step in range(1, place.height)]
     sides = [column]
@@ -363,7 +365,8 @@
         sides,
         [[place.over_core(part) for part in group] for group in sides],
     ]
-    return put_together(place, cores, [shard.shape[0] for shard in shards_in], half, split), piece, layers
+    whole = put_together(place, cores, [shard.shape[0] for shard in shards_in], half, split)
+    return whole, piece
 
 
 def hold(value, *others):
@@ -568,19 +571,17 @@
     letter_flat = letters.transpose(1, 0, 2).reshape(letter_slots * seq_rows, model_width)
 
     side_by_side = lambda w: jnp.concatenate([w[i] for i in range(w.shape[0])], axis=1)
-    (full_gin, full_project), first_piece, first_layers = gathered(
+    (full_gin, full_project), first_piece = gathered(
         place, (side_by_side(gates_input), project_weight), True
     )
-    (full_ghid,), _, second_layers = gathered(place, (side_by_side(gates_hidden),), False)
+    (full_ghid,), _ = gathered(place, (side_by_side(gates_hidden),), False)
     window = side_by_side(window_kernel)
     window_half = window.shape[1] // 2
-    (kernel_one,), _, third_layers = gathered(place, (window[:, :window_half],), True, first_layers)
-    (full_output, full_down), _, fourth_layers = gathered(
-        place, (output_weight, down_weight), False, second_layers
-    )
-    (full_up,), _, fifth_layers = gathered(place, (up_weight,), False, third_layers)
-    (kernel_two,), _, _ = gathered(place, (window[:, window_half:],), True, fourth_layers)
-    (full_tmix, full_lmix), _, _ = gathered(place, (token_mixer, letter_mixer), False, fifth_layers)
+    (kernel_one,), _ = gathered(place, (window[:, :window_half],), True)
+    (full_output, full_down), _ = gathered(place, (output_weight, down_weight), False)
+    (full_up,), _ = gathered(place, (up_weight,), False)
+    (kernel_two,), _ = gathered(place, (window[:, window_half:],), True)
+    (full_tmix, full_lmix), _ = gathered(place, (token_mixer, letter_mixer), False)
     (
         full_pbias,
         full_obias,
@@ -817,7 +818,7 @@
     project_pending = summed(place, (project_sum,), True)
     (ghid_grad,) = shared(place, ghid_pending, delta_context)
     (kernel_one_grad,) = shared(place, one_pending, delta_context)
-    (kernel_two_grad,) = shared(place, two_pending, delta_mixed)
+    (kernel_two_grad,) = shared(place, two_pending, delta_context)
     (gin_grad,) = shared(place, gin_pending, delta_mixed)
     tmix_grad, lmix_grad, down_grad = shared(place, down_pending, delta_mixed)
     (up_grad,) = shared(place, up_pending, delta_mixed)
@@ -910,74 +911,74 @@
 
 def solution(mesh):
     placed = (
-        P(("rep", "shard"), None),
-        P(("rep", "shard"), None, None),
-        P(("rep", "shard")),
-        P(("rep", "shard")),
-        P(("rep", "shard"), None),
-        P(("rep", "shard"), None),
-        P("shard", None),
-        P("shard"),
-        P("shard", None),
-        P("shard"),
-        P("shard"),
-        P("shard"),
-        P("shard", None),
-        P("shard"),
-        P("shard", None),
-        P("shard"),
-        P("shard"),
-        P("shard"),
-        P(None, "shard", None),
-        P(None, "shard", None),
-        P(None, "shard"),
-        P(None, "shard"),
-        P("shard", None),
-        P("shard"),
-        P("shard", None),
-        P("shard"),
-        P(None, "shard", None),
-        P("shard"),
-        P("shard"),
-        P("shard"),
-        P("shard"),
-        P("shard"),
+        P(BOTH, None),
+        P(BOTH, None, None),
+        P(BOTH),
+        P(BOTH),
+        P(BOTH, None),
+        P(BOTH, None),
+        P(SHARD, None),
+        P(SHARD),
+        P(SHARD, None),
+        P(SHARD),
+        P(SHARD),
+        P(SHARD),
+        P(SHARD, None),
+        P(SHARD),
+        P(SHARD, None),
+        P(SHARD),
+        P(SHARD),
+        P(SHARD),
+        P(None, SHARD, None),
+        P(None, SHARD, None),
+        P(None, SHARD),
+        P(None, SHARD),
+        P(SHARD, None),
+        P(SHARD),
+        P(SHARD, None),
+        P(SHARD),
+        P(None, SHARD, None),
+        P(SHARD),
+        P(SHARD),
+        P(SHARD),
+        P(SHARD),
+        P(SHARD),
     )
     return jax.shard_map(
         shards,
         mesh=mesh,
         in_specs=placed,
         out_specs=(
-            P(("rep", "shard"), None),
-            P(("rep", "shard"), None),
-            P(("rep", "shard"), None),
-            P(("rep", "shard"), None, None),
-            P("shard", None),
-            P("shard"),
-            P("shard", None),
-            P("shard"),
-            P("shard"),
-            P("shard"),
-            P("shard", None),
-            P("shard"),
-            P("shard", None),
-            P("shard"),
-            P("shard"),
-            P("shard"),
-            P(None, "shard", None),
-            P(None, "shard", None),
-            P(None, "shard"),
-            P(None, "shard"),
-            P("shard", None),
-            P("shard"),
-            P("shard", None),
-            P("shard"),
-            P(None, "shard", None),
-            P("shard"),
-            P("shard"),
-            P("shard"),
-            P("shard"),
-            P("shard"),
+            P(BOTH, None),
+            P(BOTH, None),
+            P(BOTH, None),
+            P(BOTH, None, None),
+            P(SHARD, None),
+            P(SHARD),
+            P(SHARD, None),
+            P(SHARD),
+            P(SHARD),
+            P(SHARD),
+            P(SHARD, None),
+            P(SHARD),
+            P(SHARD, None),
+            P(SHARD),
+            P(SHARD),
+            P(SHARD),
+            P(None, SHARD, None),
+            P(None, SHARD, None),
+            P(None, SHARD),
+            P(None, SHARD),
+            P(SHARD, None),
+            P(SHARD),
+            P(SHARD, None),
+            P(SHARD),
+            P(None, SHARD, None),
+            P(SHARD),
+            P(SHARD),
+            P(SHARD),
+            P(SHARD),
+            P(SHARD),
         ),
         check_vma=False,
     )

time: 869 us -> 914 us (1.052)
  waiting for transfers between devices: 418 us -> 442 us
  starting transfers between devices: 133 us -> 156 us
    ppermute x125, waiting for transfers between devices: 418 us -> 442 us  [exchange(): return lax.ppermute(value, axis, pairs)]
    ppermute x125, starting transfers between devices: 133 us -> 156 us  [exchange(): return lax.ppermute(value, axis, pairs)]
  transfers between devices with their start and end apart: 125 -> 125, of which waited for: 54 -> 55; matrix products, arithmetic and copies ran while one was open for 12% -> 13% of each run, Pallas kernels for 6% -> 6%
where the time goes in v1:
time: 914 us; the launch traced here: 904 us
  waiting for transfers between devices  442 us (48%)
  starting transfers between devices  156 us (17%)
  matrix products  112 us (12%)
  Pallas kernels  78.3 us (9%)
  local copies, waits for them, and re-layouts  66.7 us (7%)
  other arithmetic  42.7 us (5%)
    ppermute x125, waiting for transfers between devices, exchange(): return lax.ppermute(value, axis, pairs)  442 us
    ppermute x125, starting transfers between devices, exchange(): return lax.ppermute(value, axis, pairs)  156 us
    dot_general x20, matrix products, left_product(): lax.dot_general(left, right, (((0,), (0,)), ((), ())), preferred_element_...  55.7 us
    pallas_call x7, Pallas kernels, put_together(): pl.pallas_call(body, out_shape=[jax.ShapeDtypeStruct((blocks, count, 2 *...  40.5 us
    dot_general x10, matrix products, right_product(): lax.dot_general(left, right, (((1,), (1,)), ((), ())), preferred_element_...  28 us
    pallas_call x1, Pallas kernels, recurrent_forward(): pl.pallas_call(body, grid=(letter_slots,), in_specs=[pl.BlockSpec((1, row...  20.9 us
    dot_general x8, matrix products, product(): return jnp.dot(left, right, preferred_element_type=jnp.float32)  18.9 us
  transfers between devices with their start and end apart: 125, of which 55 were waited for; matrix products, arithmetic and copies ran while one was open for 13% of the time, Pallas kernels for 6%

profile of v1, /device:TPU:0, one launch (start us, length us, event | category | flops | bytes accessed | tf_op | source)
XLA Modules:
  0.0 904.2 jit_solution(6624766120277508736)
XLA Ops:
  2.7 4.1 collective-permute-start.27
  22.4 3.6 collective-permute-start.34
  27.0 3.2 collective-permute-start.2
  30.4 11.2 %collective-permute-start.1 = (bf16[96,1152]{1,0:T(8,128)(2,1)S(1)}, bf16[96,1152]{1,0:T(8,128)(2,1)S(1)}, u32[]{:S(2)}, u32[]{:S(2)}) collective-permute-start(bf16[96,1152]{1,0:T(8,128)(2,1)S(1)} %get-tuple-element.211), channel_id=1, source_target_pairs={{0,4},{1,5},{2,6},{3,7},{4,0},{5,1},{6,2},{7,3},{8,12},{9,13},{10,... | collective-permute-start | bytes 663560 | tf_op jit(solution)/shard_map/ppermute | solution.py:261
  44.9 7.2 collective-permute-start.38
  53.2 15.0 %collective-permute-done.1 = bf16[96,1152]{1,0:T(8,128)(2,1)S(1)} collective-permute-done((bf16[96,1152]{1,0:T(8,128)(2,1)S(1)}, bf16[96,1152]{1,0:T(8,128)(2,1)S(1)}, u32[]{:S(2)}, u32[]{:S(2)}) %collective-permute-start.1) | collective-permute-done | bytes 221216 | tf_op jit(solution)/shard_map/ppermute | solution.py:261
  69.9 8.0 collective-permute-done.39
  78.9 12.7 %collective-permute-start.20 = (bf16[96,1536]{1,0:T(8,128)(2,1)S(1)}, bf16[96,1536]{1,0:T(8,128)(2,1)S(1)}, u32[]{:S(2)}, u32[]{:S(2)}) collective-permute-start(bf16[96,1536]{1,0:T(8,128)(2,1)S(1)} %constant_dynamic-slice_fusion.4), channel_id=1, source_target_pairs={{0,2},{1,3},{2,0},{3,1},{4,6},{5,7},{6,4},{7,5},{8,10},{9,11},{10,... | collective-permute-start | bytes 884744 | tf_op jit(solution)/shard_map/ppermute | solution.py:261
  91.7 4.3 collective-permute-done.49
  97.0 17.5 %collective-permute-start.14 = (bf16[480,384]{1,0:T(8,128)(2,1)S(1)}, bf16[480,384]{1,0:T(8,128)(2,1)S(1)}, u32[]{:S(2)}, u32[]{:S(2)}) collective-permute-start(bf16[480,384]{1,0:T(8,128)(2,1)S(1)} %get-tuple-element.198), channel_id=1, source_target_pairs={{0,2},{1,3},{2,0},{3,1},{4,6},{5,7},{6,4},{7,5},{8,10},{9,11},{10,... | collective-permute-start | bytes 1105928 | tf_op jit(solution)/shard_map/ppermute | solution.py:261
  115.6 5.6 collective-permute-done.21
  124.0 19.2 %collective-permute-done.15 = bf16[480,384]{1,0:T(8,128)(2,1)S(1)} collective-permute-done((bf16[480,384]{1,0:T(8,128)(2,1)S(1)}, bf16[480,384]{1,0:T(8,128)(2,1)S(1)}, u32[]{:S(2)}, u32[]{:S(2)}) %collective-permute-start.15) | collective-permute-done | bytes 368672 | tf_op jit(solution)/shard_map/ppermute | solution.py:261
  147.0 9.2 %collective-permute-done.35.refs_1_ = bf16[4,48,1152]{2,1,0:T(8,128)(2,1)S(1)} collective-permute-done((bf16[4,48,1152]{2,1,0:T(8,128)(2,1)S(1)}, bf16[4,48,1152]{2,1,0:T(8,128)(2,1)S(1)}, u32[]{:S(2)}, u32[]{:S(2)}) %collective-permute-start.35) | collective-permute-done | bytes 442400 | tf_op jit(solution)/shard_map/ppermute | solution.py:261
  158.0 9.4 %collective-permute-done.29.refs_1_ = bf16[4,192,384]{2,1,0:T(8,128)(2,1)S(1)} collective-permute-done((bf16[4,192,384]{2,1,0:T(8,128)(2,1)S(1)}, bf16[4,192,384]{2,1,0:T(8,128)(2,1)S(1)}, u32[]{:S(2)}, u32[]{:S(2)}) %collective-permute-start.29) | collective-permute-done | bytes 589856 | tf_op jit(solution)/shard_map/ppermute | solution.py:261
  170.8 15.7 %collective-permute-done.3.refs_1_ = bf16[4,96,1152]{2,1,0:T(8,128)(2,1)} collective-permute-done((bf16[4,96,1152]{2,1,0:T(8,128)(2,1)S(1)}, bf16[4,96,1152]{2,1,0:T(8,128)(2,1)}, u32[]{:S(2)}, u32[]{:S(2)}) %collective-permute-start.3) | collective-permute-done | bytes 884768 | tf_op jit(solution)/shard_map/ppermute | solution.py:261
  193.0 12.4 %collective-permute-done.51.refs_1_ = bf16[4,96,1152]{2,1,0:T(8,128)(2,1)S(1)} collective-permute-done((bf16[4,96,1152]{2,1,0:T(8,128)(2,1)S(1)}, bf16[4,96,1152]{2,1,0:T(8,128)(2,1)S(1)}, u32[]{:S(2)}, u32[]{:S(2)}) %collective-permute-start.51) | collective-permute-done | bytes 884768 | tf_op jit(solution)/shard_map/ppermute | solution.py:261
  210.1 14.2 %collective-permute-done.41.refs_1_ = bf16[4,96,1152]{2,1,0:T(8,128)(2,1)S(1)} collective-permute-done((bf16[4,96,1152]{2,1,0:T(8,128)(2,1)S(1)}, bf16[4,96,1152]{2,1,0:T(8,128)(2,1)S(1)}, u32[]{:S(2)}, u32[]{:S(2)}) %collective-permute-start.41) | collective-permute-done | bytes 884768 | tf_op jit(solution)/shard_map/ppermute | solution.py:261
  229.8 47.4 %collective-permute-done.23.refs_1_ = bf16[4,96,1536]{2,1,0:T(8,128)(2,1)S(1)} collective-permute-done((bf16[4,96,1536]{2,1,0:T(8,128)(2,1)S(1)}, bf16[4,96,1536]{2,1,0:T(8,128)(2,1)S(1)}, u32[]{:S(2)}, u32[]{:S(2)}) %collective-permute-start.23) | collective-permute-done | bytes 1179680 | tf_op jit(solution)/shard_map/ppermute | solution.py:261
  279.3 4.2 copy.142
  290.3 16.4 %collective-permute-done.53.refs_3_ = bf16[4,96,1152]{2,1,0:T(8,128)(2,1)} collective-permute-done((bf16[4,96,1152]{2,1,0:T(8,128)(2,1)}, bf16[4,96,1152]{2,1,0:T(8,128)(2,1)}, u32[]{:S(2)}, u32[]{:S(2)}) %collective-permute-start.53) | collective-permute-done | bytes 884768 | tf_op jit(solution)/shard_map/ppermute | solution.py:261
  307.6 17.2 %collective-permute-done.43.refs_3_ = bf16[4,96,1152]{2,1,0:T(8,128)(2,1)} collective-permute-done((bf16[4,96,1152]{2,1,0:T(8,128)(2,1)}, bf16[4,96,1152]{2,1,0:T(8,128)(2,1)}, u32[]{:S(2)}, u32[]{:S(2)}) %collective-permute-start.43) | collective-permute-done | bytes 884768 | tf_op jit(solution)/shard_map/ppermute | solution.py:261
  334.4 3.5 put_together.11
  338.0 4.1 put_together.10
  342.0 5.2 put_together.9
  347.3 7.5 put_together.7
  354.7 3.3 fusion.2
  359.6 20.9 %recurrent.1 = (bf16[8,256,1536]{2,1,0:T(8,128)(2,1)}, bf16[8,256,1536]{2,1,0:T(8,128)(2,1)}, bf16[8,256,384]{2,1,0:T(8,128)(2,1)}, bf16[8,256,384]{2,1,0:T(8,128)(2,1)}, f32[256,768]{1,0:T(8,128)}) custom-call(bf16[8,256,768]{2,1,0:T(8,128)(2,1)} %bitcast.403, bf16[8,256,768]{2,1,0:T(8,128)(2,1)} %bitcast.404, bf16[768,2304]{1,0:T(8,128)(2,1)} %bitcast.444, ...), custom_call_target="tpu_custom_call" | custom-call | tf_op jit(solution)/shard_map/recurrent/pallas_call | solution.py:117
  380.5 7.0 put_together.13
  387.6 7.0 put_together.12
  400.9 6.3 put_together.8
  409.5 6.3 multiply_convert_fusion.1
  448.8 16.8 %recurrent_back.1 = (bf16[8,256,1152]{2,1,0:T(8,128)(2,1)}, bf16[8,256,1152]{2,1,0:T(8,128)(2,1)}, bf16[8,256,1152]{2,1,0:T(8,128)(2,1)}, bf16[8,256,1152]{2,1,0...) custom-call(bf16[8,256,1536]{2,1,0:T(8,128)(2,1)} %get-tuple-element.64.gates_ahead, ...), custom_call_target="tpu_custom_call" | custom-call | tf_op jit(solution)/shard_map/recurrent_back/pallas_call | solution.py:224
  465.7 9.5 %fusion.6 = bf16[1152,768]{0,1:T(8,128)(2,1)} fusion(bf16[8,256,1152]{2,1,0:T(8,128)(2,1)} %get-tuple-element.68, bf16[8,256,768]{2,0,1:T(8,128)(2,1)} %bitcast.456), kind=kOutput, calls=%fused_computation.30 | convolution fusion | flops 3624763392 | bytes 9633792 | tf_op jit(solution)/shard_map/dot_general | solution.py:24
  475.2 6.2 fusion.7
  481.4 4.3 fusion.23
  485.8 5.7 convolution_add_fusion.2
  520.7 5.6 fusion.13
  528.1 5.9 broadcast_select_fusion
  544.2 4.5 fusion.42
  562.6 3.1 collective-permute-done.69
  568.0 3.4 copy.141
  592.7 3.8 collective-permute-done.75
  608.9 4.7 collective-permute-done.105
  615.4 4.5 collective-permute-done.107
  631.9 15.7 %collective-permute-done.95 = bf16[8,48,1152]{2,1,0:T(8,128)(2,1)S(1)} collective-permute-done((bf16[8,48,1152]{2,1,0:T(8,128)(2,1)S(1)}, bf16[8,48,1152]{2,1,0:T(8,128)(2,1)S(1)}, u32[]{:S(2)}, u32[]{:S(2)}) %collective-permute-start.95) | collective-permute-done | bytes 884768 | tf_op jit(solution)/shard_map/ppermute | solution.py:261
  650.2 15.5 %collective-permute-done.59 = bf16[8,48,1152]{2,1,0:T(8,128)(2,1)S(1)} collective-permute-done((bf16[8,48,1152]{2,1,0:T(8,128)(2,1)S(1)}, bf16[8,48,1152]{2,1,0:T(8,128)(2,1)S(1)}, u32[]{:S(2)}, u32[]{:S(2)}) %collective-permute-start.59) | collective-permute-done | bytes 884768 | tf_op jit(solution)/shard_map/ppermute | solution.py:261
  672.4 5.6 collective-permute-done.60
  682.8 5.4 collective-permute-done.98
  691.6 3.0 collective-permute-done.62
  695.1 5.1 collective-permute-done.100
  700.9 4.1 collective-permute-done.64
  705.1 12.3 %collective-permute-done.79 = bf16[4,96,1536]{2,1,0:T(8,128)(2,1)S(1)} collective-permute-done((bf16[4,96,1536]{2,1,0:T(8,128)(2,1)S(1)}, bf16[4,96,1536]{2,1,0:T(8,128)(2,1)S(1)}, u32[]{:S(2)}, u32[]{:S(2)}) %collective-permute-start.79) | collective-permute-done | bytes 1179680 | tf_op jit(solution)/shard_map/ppermute | solution.py:261
  717.7 3.7 collective-permute-start.80
  726.0 3.2 add_convert_fusion
  731.7 4.8 collective-permute-done.82
  736.5 13.4 %collective-permute-done.81 = bf16[96,1536]{1,0:T(8,128)(2,1)S(1)} collective-permute-done((bf16[96,1536]{1,0:T(8,128)(2,1)S(1)}, bf16[96,1536]{1,0:T(8,128)(2,1)S(1)}, u32[]{:S(2)}, u32[]{:S(2)}) %collective-permute-start.81) | collective-permute-done | bytes 294944 | tf_op jit(solution)/shard_map/ppermute | solution.py:261
  754.2 21.6 %collective-permute-done.83 = bf16[96,1536]{1,0:T(8,128)(2,1)S(1)} collective-permute-done((bf16[96,1536]{1,0:T(8,128)(2,1)S(1)}, bf16[96,1536]{1,0:T(8,128)(2,1)S(1)}, u32[]{:S(2)}, u32[]{:S(2)}) %collective-permute-start.83) | collective-permute-done | bytes 294944 | tf_op jit(solution)/shard_map/ppermute | solution.py:261
  776.5 15.2 %collective-permute-done.90 = bf16[576,384]{1,0:T(8,128)(2,1)S(1)} collective-permute-done((bf16[576,384]{1,0:T(8,128)(2,1)S(1)}, bf16[576,384]{1,0:T(8,128)(2,1)S(1)}, u32[]{:S(2)}, u32[]{:S(2)}) %collective-permute-start.90) | collective-permute-done | bytes 442400 | tf_op jit(solution)/shard_map/ppermute | solution.py:261
  794.9 31.8 %collective-permute-done.92 = bf16[576,384]{1,0:T(8,128)(2,1)S(1)} collective-permute-done((bf16[576,384]{1,0:T(8,128)(2,1)S(1)}, bf16[576,384]{1,0:T(8,128)(2,1)S(1)}, u32[]{:S(2)}, u32[]{:S(2)}) %collective-permute-start.92) | collective-permute-done | bytes 442400 | tf_op jit(solution)/shard_map/ppermute | solution.py:261
  833.2 16.8 %collective-permute-done.119 = bf16[4,96,1152]{2,1,0:T(8,128)(2,1)S(1)} collective-permute-done((bf16[4,96,1152]{2,1,0:T(8,128)(2,1)S(1)}, bf16[4,96,1152]{2,1,0:T(8,128)(2,1)S(1)}, u32[]{:S(2)}, u32[]{:S(2)}) %collective-permute-start.119) | collective-permute-done | bytes 884768 | tf_op jit(solution)/shard_map/ppermute | solution.py:261
  854.2 14.6 %collective-permute-done.111 = bf16[4,96,1152]{2,1,0:T(8,128)(2,1)S(1)} collective-permute-done((bf16[4,96,1152]{2,1,0:T(8,128)(2,1)S(1)}, bf16[4,96,1152]{2,1,0:T(8,128)(2,1)S(1)}, u32[]{:S(2)}, u32[]{:S(2)}) %collective-permute-start.111) | collective-permute-done | bytes 884768 | tf_op jit(solution)/shard_map/ppermute | solution.py:261
  874.0 8.9 collective-permute-done.112
  883.3 9.1 %collective-permute-done.113 = bf16[96,1152]{1,0:T(8,128)(2,1)S(1)} collective-permute-done((bf16[96,1152]{1,0:T(8,128)(2,1)S(1)}, bf16[96,1152]{1,0:T(8,128)(2,1)S(1)}, u32[]{:S(2)}, u32[]{:S(2)}) %collective-permute-start.113) | collective-permute-done | bytes 221216 | tf_op jit(solution)/shard_map/ppermute | solution.py:261
  893.1 5.9 collective-permute-done.115
  (878 shorter events, 276.3 us)
Async XLA Ops:
  2.7 39.0 %collective-permute-start.27 = (bf16[192,384]{1,0:T(8,128)(2,1)}, bf16[192,384]{1,0:T(8,128)(2,1)S(1)}, u32[]{:S(2)}, u32[]{:S(2)}) collective-permute-start(bf16[192,384]{1,0:T(8,128)(2,1)} %get-tuple-element.215), channel_id=1, source_target_pairs={{0,4},{1,5},{2,6},{3,7},{4,0},{5,1},{6,2},{7,3},{8,12},{9,13},{10,... | collective-permute-start | bytes 442376 | tf_op jit(solution)/shard_map/ppermute | solution.py:261
  6.7 35.2 %collective-permute-start.26 = (bf16[192,384]{1,0:T(8,128)(2,1)}, bf16[192,384]{1,0:T(8,128)(2,1)}, u32[]{:S(2)}, u32[]{:S(2)}) collective-permute-start(bf16[192,384]{1,0:T(8,128)(2,1)} %get-tuple-element.215), channel_id=1, source_target_pairs={{0,2},{1,3},{2,0},{3,1},{4,6},{5,7},{6,4},{7,5},{8,10},{9,11},{10,... | collective-permute-start | bytes 442376 | tf_op jit(solution)/shard_map/ppermute | solution.py:261
  27.0 25.1 %collective-permute-start.2 = (bf16[96,1152]{1,0:T(8,128)(2,1)S(1)}, bf16[96,1152]{1,0:T(8,128)(2,1)S(1)}, u32[]{:S(2)}, u32[]{:S(2)}) collective-permute-start(bf16[96,1152]{1,0:T(8,128)(2,1)S(1)} %get-tuple-element.211), channel_id=1, source_target_pairs={{0,6},{1,7},{2,4},{3,5},{4,2},{5,3},{6,0},{7,1},{8,14},{9,15},{10,... | collective-permute-start | bytes 663560 | tf_op jit(solution)/shard_map/ppermute | solution.py:261
  30.4 37.7 %collective-permute-start.1 = (bf16[96,1152]{1,0:T(8,128)(2,1)S(1)}, bf16[96,1152]{1,0:T(8,128)(2,1)S(1)}, u32[]{:S(2)}, u32[]{:S(2)}) collective-permute-start(bf16[96,1152]{1,0:T(8,128)(2,1)S(1)} %get-tuple-element.211), channel_id=1, source_target_pairs={{0,4},{1,5},{2,6},{3,7},{4,0},{5,1},{6,2},{7,3},{8,12},{9,13},{10,... | collective-permute-start | bytes 663560 | tf_op jit(solution)/shard_map/ppermute | solution.py:261
  41.6 26.6 %collective-permute-start = (bf16[96,1152]{1,0:T(8,128)(2,1)S(1)}, bf16[96,1152]{1,0:T(8,128)(2,1)S(1)}, u32[]{:S(2)}, u32[]{:S(2)}) collective-permute-start(bf16[96,1152]{1,0:T(8,128)(2,1)S(1)} %get-tuple-element.211), channel_id=1, source_target_pairs={{0,2},{1,3},{2,0},{3,1},{4,6},{5,7},{6,4},{7,5},{8,10},{9,11},{10,... | collective-permute-start | bytes 663560 | tf_op jit(solution)/shard_map/ppermute | solution.py:261
  42.0 35.9 %collective-permute-start.39 = (bf16[96,1152]{1,0:T(8,128)(2,1)S(1)}, bf16[96,1152]{1,0:T(8,128)(2,1)S(1)}, u32[]{:S(2)}, u32[]{:S(2)}) collective-permute-start(bf16[96,1152]{1,0:T(8,128)(2,1)S(1)} %get-tuple-element.170), channel_id=1, source_target_pairs={{0,4},{1,5},{2,6},{3,7},{4,0},{5,1},{6,2},{7,3},{8,12},{9,13},{10,... | collective-permute-start | bytes 663560 | tf_op jit(solution)/shard_map/ppermute | solution.py:261
  44.9 34.0 %collective-permute-start.38 = (bf16[96,1152]{1,0:T(8,128)(2,1)S(1)}, bf16[96,1152]{1,0:T(8,128)(2,1)S(1)}, u32[]{:S(2)}, u32[]{:S(2)}) collective-permute-start(bf16[96,1152]{1,0:T(8,128)(2,1)S(1)} %get-tuple-element.170), channel_id=1, source_target_pairs={{0,2},{1,3},{2,0},{3,1},{4,6},{5,7},{6,4},{7,5},{8,10},{9,11},{10,... | collective-permute-start | bytes 663560 | tf_op jit(solution)/shard_map/ppermute | solution.py:261
  52.0 26.8 %collective-permute-start.40 = (bf16[96,1152]{1,0:T(8,128)(2,1)S(1)}, bf16[96,1152]{1,0:T(8,128)(2,1)S(1)}, u32[]{:S(2)}, u32[]{:S(2)}) collective-permute-start(bf16[96,1152]{1,0:T(8,128)(2,1)S(1)} %get-tuple-element.170), channel_id=1, source_target_pairs={{0,6},{1,7},{2,4},{3,5},{4,2},{5,3},{6,0},{7,1},{8,14},{9,15},{10,... | collective-permute-start | bytes 663560 | tf_op jit(solution)/shard_map/ppermute | solution.py:261
  68.2 27.8 %collective-permute-start.49 = (bf16[96,1152]{1,0:T(8,128)(2,1)S(1)}, bf16[96,1152]{1,0:T(8,128)(2,1)S(1)}, u32[]{:S(2)}, u32[]{:S(2)}) collective-permute-start(bf16[96,1152]{1,0:T(8,128)(2,1)S(1)} %get-tuple-element.171), channel_id=1, source_target_pairs={{0,4},{1,5},{2,6},{3,7},{4,0},{5,1},{6,2},{7,3},{8,12},{9,13},{10,... | collective-permute-start | bytes 663560 | tf_op jit(solution)/shard_map/ppermute | solution.py:261
  68.2 28.8 %collective-permute-start.48 = (bf16[96,1152]{1,0:T(8,128)(2,1)S(1)}, bf16[96,1152]{1,0:T(8,128)(2,1)S(1)}, u32[]{:S(2)}, u32[]{:S(2)}) collective-permute-start(bf16[96,1152]{1,0:T(8,128)(2,1)S(1)} %get-tuple-element.171), channel_id=1, source_target_pairs={{0,2},{1,3},{2,0},{3,1},{4,6},{5,7},{6,4},{7,5},{8,10},{9,11},{10,... | collective-permute-start | bytes 663560 | tf_op jit(solution)/shard_map/ppermute | solution.py:261
  78.8 42.3 %collective-permute-start.21 = (bf16[96,1536]{1,0:T(8,128)(2,1)S(1)}, bf16[96,1536]{1,0:T(8,128)(2,1)S(1)}, u32[]{:S(2)}, u32[]{:S(2)}) collective-permute-start(bf16[96,1536]{1,0:T(8,128)(2,1)S(1)} %constant_dynamic-slice_fusion.4), channel_id=1, source_target_pairs={{0,4},{1,5},{2,6},{3,7},{4,0},{5,1},{6,2},{7,3},{8,12},{9,13},{10,... | collective-permute-start | bytes 884744 | tf_op jit(solution)/shard_map/ppermute | solution.py:261
  78.9 43.3 %collective-permute-start.20 = (bf16[96,1536]{1,0:T(8,128)(2,1)S(1)}, bf16[96,1536]{1,0:T(8,128)(2,1)S(1)}, u32[]{:S(2)}, u32[]{:S(2)}) collective-permute-start(bf16[96,1536]{1,0:T(8,128)(2,1)S(1)} %constant_dynamic-slice_fusion.4), channel_id=1, source_target_pairs={{0,2},{1,3},{2,0},{3,1},{4,6},{5,7},{6,4},{7,5},{8,10},{9,11},{10,... | collective-permute-start | bytes 884744 | tf_op jit(solution)/shard_map/ppermute | solution.py:261
  95.9 27.5 %collective-permute-start.22 = (bf16[96,1536]{1,0:T(8,128)(2,1)S(1)}, bf16[96,1536]{1,0:T(8,128)(2,1)S(1)}, u32[]{:S(2)}, u32[]{:S(2)}) collective-permute-start(bf16[96,1536]{1,0:T(8,128)(2,1)S(1)} %constant_dynamic-slice_fusion.4), channel_id=1, source_target_pairs={{0,6},{1,7},{2,4},{3,5},{4,2},{5,3},{6,0},{7,1},{8,14},{9,15},{10,... | collective-permute-start | bytes 884744 | tf_op jit(solution)/shard_map/ppermute | solution.py:261
  97.0 46.2 %collective-permute-start.15 = (bf16[480,384]{1,0:T(8,128)(2,1)S(1)}, bf16[480,384]{1,0:T(8,128)(2,1)S(1)}, u32[]{:S(2)}, u32[]{:S(2)}) collective-permute-start(bf16[480,384]{1,0:T(8,128)(2,1)S(1)} %get-tuple-element.198), channel_id=1, source_target_pairs={{0,4},{1,5},{2,6},{3,7},{4,0},{5,1},{6,2},{7,3},{8,12},{9,13},{10,... | collective-permute-start | bytes 1105928 | tf_op jit(solution)/shard_map/ppermute | solution.py:261
  97.0 47.7 %collective-permute-start.14 = (bf16[480,384]{1,0:T(8,128)(2,1)S(1)}, bf16[480,384]{1,0:T(8,128)(2,1)S(1)}, u32[]{:S(2)}, u32[]{:S(2)}) collective-permute-start(bf16[480,384]{1,0:T(8,128)(2,1)S(1)} %get-tuple-element.198), channel_id=1, source_target_pairs={{0,2},{1,3},{2,0},{3,1},{4,6},{5,7},{6,4},{7,5},{8,10},{9,11},{10,... | collective-permute-start | bytes 1105928 | tf_op jit(solution)/shard_map/ppermute | solution.py:261
  121.2 24.2 %collective-permute-start.16 = (bf16[480,384]{1,0:T(8,128)(2,1)S(1)}, bf16[480,384]{1,0:T(8,128)(2,1)S(1)}, u32[]{:S(2)}, u32[]{:S(2)}) collective-permute-start(bf16[480,384]{1,0:T(8,128)(2,1)S(1)} %get-tuple-element.198), channel_id=1, source_target_pairs={{0,6},{1,7},{2,4},{3,5},{4,2},{5,3},{6,0},{7,1},{8,14},{9,15},{10,... | collective-permute-start | bytes 1105928 | tf_op jit(solution)/shard_map/ppermute | solution.py:261
  122.2 23.2 %collective-permute-start.36 = (bf16[4,48,1152]{2,1,0:T(8,128)(2,1)S(1)}, bf16[4,48,1152]{2,1,0:T(8,128)(2,1)S(1)}, u32[]{:S(2)}, u32[]{:S(2)}) collective-permute-start(bf16[4,48,1152]{2,1,0:T(8,128)(2,1)S(1)} %pad_maximum_fusion.11.refs_0_), channel_id=1, source_target_pairs={{0,8},{8,0},{16,24},{24,16},{1,9},{9,1},{17,25},{25,17},{2,10},{10... | collective-permute-start | bytes 1327112 | tf_op jit(solution)/shard_map/ppermute | solution.py:261
  123.4 32.8 %collective-permute-start.30 = (bf16[4,192,384]{2,1,0:T(8,128)(2,1)S(1)}, bf16[4,192,384]{2,1,0:T(8,128)(2,1)S(1)}, u32[]{:S(2)}, u32[]{:S(2)}) collective-permute-start(bf16[4,192,384]{2,1,0:T(8,128)(2,1)S(1)} %pad_maximum_fusion.10.refs_0_), channel_id=1, source_target_pairs={{0,8},{8,0},{16,24},{24,16},{1,9},{9,1},{17,25},{25,17},{2,10},{10... | collective-permute-start | bytes 1769480 | tf_op jit(solution)/shard_map/ppermute | solution.py:261
  144.7 22.7 %collective-permute-start.29 = (bf16[4,192,384]{2,1,0:T(8,128)(2,1)S(1)}, bf16[4,192,384]{2,1,0:T(8,128)(2,1)S(1)}, u32[]{:S(2)}, u32[]{:S(2)}) collective-permute-start(bf16[4,192,384]{2,1,0:T(8,128)(2,1)S(1)} %pad_maximum_fusion.10.refs_0_), channel_id=1, source_target_pairs={{0,1},{1,0},{2,3},{3,2},{4,5},{5,4},{6,7},{7,6},{8,9},{9,8},{10,11... | collective-permute-start | bytes 1769480 | tf_op jit(solution)/shard_map/ppermute | solution.py:261
  145.4 23.8 %collective-permute-start.6 = (bf16[4,96,1152]{2,1,0:T(8,128)(2,1)S(1)}, bf16[4,96,1152]{2,1,0:T(8,128)(2,1)S(1)}, u32[]{:S(2)}, u32[]{:S(2)}) collective-permute-start(bf16[4,96,1152]{2,1,0:T(8,128)(2,1)S(1)} %pad_maximum_fusion.6.refs_0_), channel_id=1, source_target_pairs={{0,8},{8,0},{16,24},{24,16},{1,9},{9,1},{17,25},{25,17},{2,10},{10... | collective-permute-start | bytes 2654216 | tf_op jit(solution)/shard_map/ppermute | solution.py:261
  145.5 25.3 %collective-permute-start.4 = (bf16[4,96,1152]{2,1,0:T(8,128)(2,1)S(1)}, bf16[4,96,1152]{2,1,0:T(8,128)(2,1)}, u32[]{:S(2)}, u32[]{:S(2)}) collective-permute-start(bf16[4,96,1152]{2,1,0:T(8,128)(2,1)S(1)} %pad_maximum_fusion.6.refs_0_), channel_id=1, source_target_pairs={{0,16},{8,24},{16,0},{24,8},{1,17},{9,25},{17,1},{25,9},{2,18},{10... | collective-permute-start | bytes 2654216 | tf_op jit(solution)/shard_map/ppermute | solution.py:261
  156.2 30.3 %collective-permute-start.3 = (bf16[4,96,1152]{2,1,0:T(8,128)(2,1)S(1)}, bf16[4,96,1152]{2,1,0:T(8,128)(2,1)}, u32[]{:S(2)}, u32[]{:S(2)}) collective-permute-start(bf16[4,96,1152]{2,1,0:T(8,128)(2,1)S(1)} %pad_maximum_fusion.6.refs_0_), channel_id=1, source_target_pairs={{0,1},{1,0},{2,3},{3,2},{4,5},{5,4},{6,7},{7,6},{8,9},{9,8},{10,11... | collective-permute-start | bytes 2654216 | tf_op jit(solution)/shard_map/ppermute | solution.py:261
  167.4 22.6 %collective-permute-start.52 = (bf16[4,96,1152]{2,1,0:T(8,128)(2,1)S(1)}, bf16[4,96,1152]{2,1,0:T(8,128)(2,1)S(1)}, u32[]{:S(2)}, u32[]{:S(2)}) collective-permute-start(bf16[4,96,1152]{2,1,0:T(8,128)(2,1)S(1)} %pad_maximum_fusion.8.refs_0_), channel_id=1, source_target_pairs={{0,16},{8,24},{16,0},{24,8},{1,17},{9,25},{17,1},{25,9},{2,18},{10... | collective-permute-start | bytes 2654216 | tf_op jit(solution)/shard_map/ppermute | solution.py:261
  169.2 36.2 %collective-permute-start.51 = (bf16[4,96,1152]{2,1,0:T(8,128)(2,1)S(1)}, bf16[4,96,1152]{2,1,0:T(8,128)(2,1)S(1)}, u32[]{:S(2)}, u32[]{:S(2)}) collective-permute-start(bf16[4,96,1152]{2,1,0:T(8,128)(2,1)S(1)} %pad_maximum_fusion.8.refs_0_), channel_id=1, source_target_pairs={{0,1},{1,0},{2,3},{3,2},{4,5},{5,4},{6,7},{7,6},{8,9},{9,8},{10,11... | collective-permute-start | bytes 2654216 | tf_op jit(solution)/shard_map/ppermute | solution.py:261
  170.8 36.1 %collective-permute-start.44 = (bf16[4,96,1152]{2,1,0:T(8,128)(2,1)S(1)}, bf16[4,96,1152]{2,1,0:T(8,128)(2,1)S(1)}, u32[]{:S(2)}, u32[]{:S(2)}) collective-permute-start(bf16[4,96,1152]{2,1,0:T(8,128)(2,1)S(1)} %pad_maximum_fusion.7.refs_0_), channel_id=1, source_target_pairs={{0,8},{8,0},{16,24},{24,16},{1,9},{9,1},{17,25},{25,17},{2,10},{10... | collective-permute-start | bytes 2654216 | tf_op jit(solution)/shard_map/ppermute | solution.py:261
  186.5 22.1 %collective-permute-start.42 = (bf16[4,96,1152]{2,1,0:T(8,128)(2,1)S(1)}, bf16[4,96,1152]{2,1,0:T(8,128)(2,1)}, u32[]{:S(2)}, u32[]{:S(2)}) collective-permute-start(bf16[4,96,1152]{2,1,0:T(8,128)(2,1)S(1)} %pad_maximum_fusion.7.refs_0_), channel_id=1, source_target_pairs={{0,16},{8,24},{16,0},{24,8},{1,17},{9,25},{17,1},{25,9},{2,18},{10... | collective-permute-start | bytes 2654216 | tf_op jit(solution)/shard_map/ppermute | solution.py:261
  188.2 36.6 %collective-permute-start.24 = (bf16[4,96,1536]{2,1,0:T(8,128)(2,1)S(1)}, bf16[4,96,1536]{2,1,0:T(8,128)(2,1)S(1)}, u32[]{:S(2)}, u32[]{:S(2)}) collective-permute-start(bf16[4,96,1536]{2,1,0:T(8,128)(2,1)S(1)} %pad_maximum_fusion.4.refs_0_), channel_id=1, source_target_pairs={{0,8},{8,0},{16,24},{24,16},{1,9},{9,1},{17,25},{25,17},{2,10},{10... | collective-permute-start | bytes 3538952 | tf_op jit(solution)/shard_map/ppermute | solution.py:261
  190.0 34.3 %collective-permute-start.41 = (bf16[4,96,1152]{2,1,0:T(8,128)(2,1)S(1)}, bf16[4,96,1152]{2,1,0:T(8,128)(2,1)S(1)}, u32[]{:S(2)}, u32[]{:S(2)}) collective-permute-start(bf16[4,96,1152]{2,1,0:T(8,128)(2,1)S(1)} %pad_maximum_fusion.7.refs_0_), channel_id=1, source_target_pairs={{0,1},{1,0},{2,3},{3,2},{4,5},{5,4},{6,7},{7,6},{8,9},{9,8},{10,11... | collective-permute-start | bytes 2654216 | tf_op jit(solution)/shard_map/ppermute | solution.py:261
  205.3 78.1 %collective-permute-start.17 = (bf16[4,480,384]{2,1,0:T(8,128)(2,1)}, bf16[4,480,384]{2,1,0:T(8,128)(2,1)}, u32[]{:S(2)}, u32[]{:S(2)}) collective-permute-start(bf16[4,480,384]{2,1,0:T(8,128)(2,1)} %pad_maximum_fusion.2.refs_0_), channel_id=1, source_target_pairs={{0,1},{1,0},{2,3},{3,2},{4,5},{5,4},{6,7},{7,6},{8,9},{9,8},{10,11... | collective-permute-start | bytes 4423688 | tf_op jit(solution)/shard_map/ppermute | solution.py:261
  208.6 68.6 %collective-permute-start.23 = (bf16[4,96,1536]{2,1,0:T(8,128)(2,1)S(1)}, bf16[4,96,1536]{2,1,0:T(8,128)(2,1)S(1)}, u32[]{:S(2)}, u32[]{:S(2)}) collective-permute-start(bf16[4,96,1536]{2,1,0:T(8,128)(2,1)S(1)} %pad_maximum_fusion.4.refs_0_), channel_id=1, source_target_pairs={{0,1},{1,0},{2,3},{3,2},{4,5},{5,4},{6,7},{7,6},{8,9},{9,8},{10,11... | collective-permute-start | bytes 3538952 | tf_op jit(solution)/shard_map/ppermute | solution.py:261
  224.3 59.6 %collective-permute-start.8 = (bf16[4,96,1152]{2,1,0:T(8,128)(2,1)}, bf16[4,96,1152]{2,1,0:T(8,128)(2,1)}, u32[]{:S(2)}, u32[]{:S(2)}) collective-permute-start(bf16[4,96,1152]{2,1,0:T(8,128)(2,1)} %collective-permute-done.4.refs_2_), channel_id=1, source_target_pairs={{0,8},{8,0},{16,24},{24,16},{1,9},{9,1},{17,25},{25,17},{2,10},{10... | collective-permute-start | bytes 2654216 | tf_op jit(solution)/shard_map/ppermute | solution.py:261
  224.3 61.1 %collective-permute-start.7 = (bf16[4,96,1152]{2,1,0:T(8,128)(2,1)}, bf16[4,96,1152]{2,1,0:T(8,128)(2,1)}, u32[]{:S(2)}, u32[]{:S(2)}) collective-permute-start(bf16[4,96,1152]{2,1,0:T(8,128)(2,1)} %collective-permute-done.3.refs_1_), channel_id=1, source_target_pairs={{0,8},{8,0},{16,24},{24,16},{1,9},{9,1},{17,25},{25,17},{2,10},{10... | collective-permute-start | bytes 2654216 | tf_op jit(solution)/shard_map/ppermute | solution.py:261
  226.4 59.6 %collective-permute-start.5 = (bf16[4,96,1152]{2,1,0:T(8,128)(2,1)}, bf16[4,96,1152]{2,1,0:T(8,128)(2,1)}, u32[]{:S(2)}, u32[]{:S(2)}) collective-permute-start(bf16[4,96,1152]{2,1,0:T(8,128)(2,1)} %collective-permute-done.3.refs_1_), channel_id=1, source_target_pairs={{0,16},{8,24},{16,0},{24,8},{1,17},{9,25},{17,1},{25,9},{2,18},{10... | collective-permute-start | bytes 2654216 | tf_op jit(solution)/shard_map/ppermute | solution.py:261
  277.1 47.7 %collective-permute-start.25 = (bf16[4,96,1536]{2,1,0:T(8,128)(2,1)S(1)}, bf16[4,96,1536]{2,1,0:T(8,128)(2,1)S(1)}, u32[]{:S(2)}, u32[]{:S(2)}) collective-permute-start(bf16[4,96,1536]{2,1,0:T(8,128)(2,1)S(1)} %collective-permute-done.23.refs_1_), channel_id=1, source_target_pairs={{0,8},{8,0},{16,24},{24,16},{1,9},{9,1},{17,25},{25,17},{2,10},{10... | collective-permute-start | bytes 3538952 | tf_op jit(solution)/shard_map/ppermute | solution.py:261
  283.9 22.8 %collective-permute-start.53 = (bf16[4,96,1152]{2,1,0:T(8,128)(2,1)}, bf16[4,96,1152]{2,1,0:T(8,128)(2,1)}, u32[]{:S(2)}, u32[]{:S(2)}) collective-permute-start(bf16[4,96,1152]{2,1,0:T(8,128)(2,1)} %copy-done.91), channel_id=1, source_target_pairs={{0,16},{8,24},{16,0},{24,8},{1,17},{9,25},{17,1},{25,9},{2,18},{10... | collective-permute-start | bytes 2654216 | tf_op jit(solution)/shard_map/ppermute | solution.py:261
  285.4 39.4 %collective-permute-start.43 = (bf16[4,96,1152]{2,1,0:T(8,128)(2,1)}, bf16[4,96,1152]{2,1,0:T(8,128)(2,1)}, u32[]{:S(2)}, u32[]{:S(2)}) collective-permute-start(bf16[4,96,1152]{2,1,0:T(8,128)(2,1)} %copy-done.92), channel_id=1, source_target_pairs={{0,16},{8,24},{16,0},{24,8},{1,17},{9,25},{17,1},{25,9},{2,18},{10... | collective-permute-start | bytes 2654216 | tf_op jit(solution)/shard_map/ppermute | solution.py:261
  286.0 39.4 %collective-permute-start.9 = (bf16[4,96,1152]{2,1,0:T(8,128)(2,1)}, bf16[4,96,1152]{2,1,0:T(8,128)(2,1)S(1)}, u32[]{:S(2)}, u32[]{:S(2)}) collective-permute-start(bf16[4,96,1152]{2,1,0:T(8,128)(2,1)} %collective-permute-done.5.refs_3_), channel_id=1, source_target_pairs={{0,8},{8,0},{16,24},{24,16},{1,9},{9,1},{17,25},{25,17},{2,10},{10... | collective-permute-start | bytes 2654216 | tf_op jit(solution)/shard_map/ppermute | solution.py:261
  289.8 68.2 %collective-permute-start.55 = (bf16[4,96,1152]{2,1,0:T(8,128)(2,1)}, bf16[4,96,1152]{2,1,0:T(8,128)(2,1)}, u32[]{:S(2)}, u32[]{:S(2)}) collective-permute-start(bf16[4,96,1152]{2,1,0:T(8,128)(2,1)} %copy-done.91), channel_id=1, source_target_pairs={{0,8},{8,0},{16,24},{24,16},{1,9},{9,1},{17,25},{25,17},{2,10},{10... | collective-permute-start | bytes 2654216 | tf_op jit(solution)/shard_map/ppermute | solution.py:261
  306.8 51.7 %collective-permute-start.57 = (bf16[4,96,1152]{2,1,0:T(8,128)(2,1)}, bf16[4,96,1152]{2,1,0:T(8,128)(2,1)}, u32[]{:S(2)}, u32[]{:S(2)}) collective-permute-start(bf16[4,96,1152]{2,1,0:T(8,128)(2,1)} %collective-permute-done.53.refs_3_), channel_id=1, source_target_pairs={{0,8},{8,0},{16,24},{24,16},{1,9},{9,1},{17,25},{25,17},{2,10},{10... | collective-permute-start | bytes 2654216 | tf_op jit(solution)/shard_map/ppermute | solution.py:261
  324.9 62.7 %collective-permute-start.45 = (bf16[4,96,1152]{2,1,0:T(8,128)(2,1)}, bf16[4,96,1152]{2,1,0:T(8,128)(2,1)}, u32[]{:S(2)}, u32[]{:S(2)}) collective-permute-start(bf16[4,96,1152]{2,1,0:T(8,128)(2,1)} %copy-done.92), channel_id=1, source_target_pairs={{0,8},{8,0},{16,24},{24,16},{1,9},{9,1},{17,25},{25,17},{2,10},{10... | collective-permute-start | bytes 2654216 | tf_op jit(solution)/shard_map/ppermute | solution.py:261
  324.9 62.7 %collective-permute-start.46 = (bf16[4,96,1152]{2,1,0:T(8,128)(2,1)}, bf16[4,96,1152]{2,1,0:T(8,128)(2,1)}, u32[]{:S(2)}, u32[]{:S(2)}) collective-permute-start(bf16[4,96,1152]{2,1,0:T(8,128)(2,1)} %collective-permute-done.42.refs_2_), channel_id=1, source_target_pairs={{0,8},{8,0},{16,24},{24,16},{1,9},{9,1},{17,25},{25,17},{2,10},{10... | collective-permute-start | bytes 2654216 | tf_op jit(solution)/shard_map/ppermute | solution.py:261
  325.4 62.2 %collective-permute-start.47 = (bf16[4,96,1152]{2,1,0:T(8,128)(2,1)}, bf16[4,96,1152]{2,1,0:T(8,128)(2,1)}, u32[]{:S(2)}, u32[]{:S(2)}) collective-permute-start(bf16[4,96,1152]{2,1,0:T(8,128)(2,1)} %collective-permute-done.43.refs_3_), channel_id=1, source_target_pairs={{0,8},{8,0},{16,24},{24,16},{1,9},{9,1},{17,25},{25,17},{2,10},{10... | collective-permute-start | bytes 2654216 | tf_op jit(solution)/shard_map/ppermute | solution.py:261
  358.1 42.8 %collective-permute-start.18 = (bf16[4,480,384]{2,1,0:T(8,128)(2,1)}, bf16[4,480,384]{2,1,0:T(8,128)(2,1)}, u32[]{:S(2)}, u32[]{:S(2)}) collective-permute-start(bf16[4,480,384]{2,1,0:T(8,128)(2,1)} %pad_maximum_fusion.2.refs_0_), channel_id=1, source_target_pairs={{0,8},{8,0},{16,24},{24,16},{1,9},{9,1},{17,25},{25,17},{2,10},{10... | collective-permute-start | bytes 4423688 | tf_op jit(solution)/shard_map/ppermute | solution.py:261
  358.5 42.4 %collective-permute-start.19 = (bf16[4,480,384]{2,1,0:T(8,128)(2,1)}, bf16[4,480,384]{2,1,0:T(8,128)(2,1)}, u32[]{:S(2)}, u32[]{:S(2)}) collective-permute-start(bf16[4,480,384]{2,1,0:T(8,128)(2,1)} %collective-permute-done.17.refs_1_), channel_id=1, source_target_pairs={{0,8},{8,0},{16,24},{24,16},{1,9},{9,1},{17,25},{25,17},{2,10},{10... | collective-permute-start | bytes 4423688 | tf_op jit(solution)/shard_map/ppermute | solution.py:261
  520.2 61.5 %collective-permute-start.85 = (bf16[768,384]{1,0:T(8,128)(2,1)}, bf16[768,384]{1,0:T(8,128)(2,1)}, u32[]{:S(2)}, u32[]{:S(2)}) collective-permute-start(bf16[768,384]{1,0:T(8,128)(2,1)} %convolution_convert_fusion.6), channel_id=1, source_target_pairs={{0,8},{8,0},{16,24},{24,16},{1,9},{9,1},{17,25},{25,17},{2,10},{10... | collective-permute-start | bytes 1769480 | tf_op jit(solution)/shard_map/ppermute | solution.py:261
  520.5 204.0 %collective-permute-start.117 = (bf16[1536,1152]{1,0:T(8,128)(2,1)}, bf16[1536,1152]{1,0:T(8,128)(2,1)}, u32[]{:S(2)}, u32[]{:S(2)}) collective-permute-start(bf16[1536,1152]{1,0:T(8,128)(2,1)} %convolution_convert_fusion), channel_id=1, source_target_pairs={{0,8},{8,0},{16,24},{24,16},{1,9},{9,1},{17,25},{25,17},{2,10},{10... | collective-permute-start | bytes 10616840 | tf_op jit(solution)/shard_map/ppermute | solution.py:261
  534.0 49.4 %collective-permute-start.102 = (bf16[384,1152]{1,0:T(8,128)(2,1)}, bf16[384,1152]{1,0:T(8,128)(2,1)}, u32[]{:S(2)}, u32[]{:S(2)}) collective-permute-start(bf16[384,1152]{1,0:T(8,128)(2,1)} %get-tuple-element.264), channel_id=1, source_target_pairs={{0,8},{8,0},{16,24},{24,16},{1,9},{9,1},{17,25},{25,17},{2,10},{10... | collective-permute-start | bytes 2654216 | tf_op jit(solution)/shard_map/ppermute | solution.py:261
  592.7 29.8 %collective-permute-start.94 = (bf16[768,1152]{1,0:T(8,128)(2,1)S(1)}, bf16[768,1152]{1,0:T(8,128)(2,1)S(1)}, u32[]{:S(2)}, u32[]{:S(2)}) collective-permute-start(bf16[768,1152]{1,0:T(8,128)(2,1)S(1)} %copy-done.59), channel_id=1, source_target_pairs={{0,8},{8,0},{16,24},{24,16},{1,9},{9,1},{17,25},{25,17},{2,10},{10... | collective-permute-start | bytes 5308424 | tf_op jit(solution)/shard_map/ppermute | solution.py:261
  605.9 23.7 %collective-permute-start.78 = (bf16[768,1536]{1,0:T(8,128)(2,1)S(1)}, bf16[768,1536]{1,0:T(8,128)(2,1)S(1)}, u32[]{:S(2)}, u32[]{:S(2)}) collective-permute-start(bf16[768,1536]{1,0:T(8,128)(2,1)S(1)} %copy-done.58), channel_id=1, source_target_pairs={{0,8},{8,0},{16,24},{24,16},{1,9},{9,1},{17,25},{25,17},{2,10},{10... | collective-permute-start | bytes 7077896 | tf_op jit(solution)/shard_map/ppermute | solution.py:261
  622.5 106.9 %collective-permute-start.109 = (bf16[1536,1152]{1,0:T(8,128)(2,1)S(1)}, bf16[1536,1152]{1,0:T(8,128)(2,1)S(1)}, u32[]{:S(2)}, u32[]{:S(2)}) collective-permute-start(bf16[1536,1152]{1,0:T(8,128)(2,1)S(1)} %copy-done.15), channel_id=1, source_target_pairs={{0,8},{8,0},{16,24},{24,16},{1,9},{9,1},{17,25},{25,17},{2,10},{10... | collective-permute-start | bytes 10616840 | tf_op jit(solution)/shard_map/ppermute | solution.py:261
  625.1 22.5 %collective-permute-start.95 = (bf16[8,48,1152]{2,1,0:T(8,128)(2,1)S(1)}, bf16[8,48,1152]{2,1,0:T(8,128)(2,1)S(1)}, u32[]{:S(2)}, u32[]{:S(2)}) collective-permute-start(bf16[8,48,1152]{2,1,0:T(8,128)(2,1)S(1)} %dynamic-slice_bitcast_fusion.7), channel_id=1, source_target_pairs={{0,16},{8,24},{16,0},{24,8},{1,17},{9,25},{17,1},{25,9},{2,18},{10... | collective-permute-start | bytes 2654216 | tf_op jit(solution)/shard_map/ppermute | solution.py:261
  626.7 39.1 %collective-permute-start.59 = (bf16[8,48,1152]{2,1,0:T(8,128)(2,1)S(1)}, bf16[8,48,1152]{2,1,0:T(8,128)(2,1)S(1)}, u32[]{:S(2)}, u32[]{:S(2)}) collective-permute-start(bf16[8,48,1152]{2,1,0:T(8,128)(2,1)S(1)} %dynamic-slice_bitcast_fusion.8), channel_id=1, source_target_pairs={{0,16},{8,24},{16,0},{24,8},{1,17},{9,25},{17,1},{25,9},{2,18},{10... | collective-permute-start | bytes 2654216 | tf_op jit(solution)/shard_map/ppermute | solution.py:261
  688.3 29.0 %collective-permute-start.79 = (bf16[4,96,1536]{2,1,0:T(8,128)(2,1)S(1)}, bf16[4,96,1536]{2,1,0:T(8,128)(2,1)S(1)}, u32[]{:S(2)}, u32[]{:S(2)}) collective-permute-start(bf16[4,96,1536]{2,1,0:T(8,128)(2,1)S(1)} %dynamic-slice_bitcast_fusion.4), channel_id=1, source_target_pairs={{0,1},{1,0},{2,3},{3,2},{4,5},{5,4},{6,7},{7,6},{8,9},{9,8},{10,11... | collective-permute-start | bytes 3538952 | tf_op jit(solution)/shard_map/ppermute | solution.py:261
  690.5 59.6 %collective-permute-start.88 = (bf16[4,576,384]{2,1,0:T(8,128)(2,1)S(1)}, bf16[4,576,384]{2,1,0:T(8,128)(2,1)S(1)}, u32[]{:S(2)}, u32[]{:S(2)}) collective-permute-start(bf16[4,576,384]{2,1,0:T(8,128)(2,1)S(1)} %pad_maximum_fusion.1), channel_id=1, source_target_pairs={{0,1},{1,0},{2,3},{3,2},{4,5},{5,4},{6,7},{7,6},{8,9},{9,8},{10,11... | collective-permute-start | bytes 5308424 | tf_op jit(solution)/shard_map/ppermute | solution.py:261
  724.5 25.3 %collective-permute-start.81 = (bf16[96,1536]{1,0:T(8,128)(2,1)S(1)}, bf16[96,1536]{1,0:T(8,128)(2,1)S(1)}, u32[]{:S(2)}, u32[]{:S(2)}) collective-permute-start(bf16[96,1536]{1,0:T(8,128)(2,1)S(1)} %get-tuple-element.138), channel_id=1, source_target_pairs={{0,4},{1,5},{2,6},{3,7},{4,0},{5,1},{6,2},{7,3},{8,12},{9,13},{10,... | collective-permute-start | bytes 884744 | tf_op jit(solution)/shard_map/ppermute | solution.py:261
  729.4 97.5 %collective-permute-start.118 = (bf16[8,96,1152]{2,1,0:T(8,128)(2,1)S(1)}, bf16[8,96,1152]{2,1,0:T(8,128)(2,1)S(1)}, u32[]{:S(2)}, u32[]{:S(2)}) collective-permute-start(bf16[8,96,1152]{2,1,0:T(8,128)(2,1)S(1)} %dynamic-slice_bitcast_fusion), channel_id=1, source_target_pairs={{0,16},{8,24},{16,0},{24,8},{1,17},{9,25},{17,1},{25,9},{2,18},{10... | collective-permute-start | bytes 5308424 | tf_op jit(solution)/shard_map/ppermute | solution.py:261
  750.0 25.8 %collective-permute-start.83 = (bf16[96,1536]{1,0:T(8,128)(2,1)S(1)}, bf16[96,1536]{1,0:T(8,128)(2,1)S(1)}, u32[]{:S(2)}, u32[]{:S(2)}) collective-permute-start(bf16[96,1536]{1,0:T(8,128)(2,1)S(1)} %fusion.67), channel_id=1, source_target_pairs={{0,16},{8,24},{16,0},{24,8},{1,17},{9,25},{17,1},{25,9},{2,18},{10... | collective-permute-start | bytes 884744 | tf_op jit(solution)/shard_map/ppermute | solution.py:261
  750.7 25.5 %collective-permute-start.89 = (bf16[576,384]{1,0:T(8,128)(2,1)S(1)}, bf16[576,384]{1,0:T(8,128)(2,1)S(1)}, u32[]{:S(2)}, u32[]{:S(2)}) collective-permute-start(bf16[576,384]{1,0:T(8,128)(2,1)S(1)} %get-tuple-element.128), channel_id=1, source_target_pairs={{0,2},{1,3},{2,0},{3,1},{4,6},{5,7},{6,4},{7,5},{8,10},{9,11},{10,... | collective-permute-start | bytes 1327112 | tf_op jit(solution)/shard_map/ppermute | solution.py:261
  750.8 25.8 %collective-permute-start.91 = (bf16[576,384]{1,0:T(8,128)(2,1)S(1)}, bf16[576,384]{1,0:T(8,128)(2,1)S(1)}, u32[]{:S(2)}, u32[]{:S(2)}) collective-permute-start(bf16[576,384]{1,0:T(8,128)(2,1)S(1)} %get-tuple-element.129), channel_id=1, source_target_pairs={{0,6},{1,7},{2,4},{3,5},{4,2},{5,3},{6,0},{7,1},{8,14},{9,15},{10,... | collective-permute-start | bytes 1327112 | tf_op jit(solution)/shard_map/ppermute | solution.py:261
  752.2 39.5 %collective-permute-start.90 = (bf16[576,384]{1,0:T(8,128)(2,1)S(1)}, bf16[576,384]{1,0:T(8,128)(2,1)S(1)}, u32[]{:S(2)}, u32[]{:S(2)}) collective-permute-start(bf16[576,384]{1,0:T(8,128)(2,1)S(1)} %get-tuple-element.130), channel_id=1, source_target_pairs={{0,4},{1,5},{2,6},{3,7},{4,0},{5,1},{6,2},{7,3},{8,12},{9,13},{10,... | collective-permute-start | bytes 1327112 | tf_op jit(solution)/shard_map/ppermute | solution.py:261
  776.2 53.4 %collective-permute-start.110 = (bf16[8,96,1152]{2,1,0:T(8,128)(2,1)S(1)}, bf16[8,96,1152]{2,1,0:T(8,128)(2,1)S(1)}, u32[]{:S(2)}, u32[]{:S(2)}) collective-permute-start(bf16[8,96,1152]{2,1,0:T(8,128)(2,1)S(1)} %dynamic-slice_bitcast_fusion.1), channel_id=1, source_target_pairs={{0,16},{8,24},{16,0},{24,8},{1,17},{9,25},{17,1},{25,9},{2,18},{10... | collective-permute-start | bytes 5308424 | tf_op jit(solution)/shard_map/ppermute | solution.py:261
  792.0 34.7 %collective-permute-start.92 = (bf16[576,384]{1,0:T(8,128)(2,1)S(1)}, bf16[576,384]{1,0:T(8,128)(2,1)S(1)}, u32[]{:S(2)}, u32[]{:S(2)}) collective-permute-start(bf16[576,384]{1,0:T(8,128)(2,1)S(1)} %fusion.52), channel_id=1, source_target_pairs={{0,16},{8,24},{16,0},{24,8},{1,17},{9,25},{17,1},{25,9},{2,18},{10... | collective-permute-start | bytes 1327112 | tf_op jit(solution)/shard_map/ppermute | solution.py:261
  827.4 22.6 %collective-permute-start.119 = (bf16[4,96,1152]{2,1,0:T(8,128)(2,1)S(1)}, bf16[4,96,1152]{2,1,0:T(8,128)(2,1)S(1)}, u32[]{:S(2)}, u32[]{:S(2)}) collective-permute-start(bf16[4,96,1152]{2,1,0:T(8,128)(2,1)S(1)} %dynamic-slice_bitcast_fusion.5), channel_id=1, source_target_pairs={{0,1},{1,0},{2,3},{3,2},{4,5},{5,4},{6,7},{7,6},{8,9},{9,8},{10,11... | collective-permute-start | bytes 2654216 | tf_op jit(solution)/shard_map/ppermute | solution.py:261
  830.0 38.7 %collective-permute-start.111 = (bf16[4,96,1152]{2,1,0:T(8,128)(2,1)S(1)}, bf16[4,96,1152]{2,1,0:T(8,128)(2,1)S(1)}, u32[]{:S(2)}, u32[]{:S(2)}) collective-permute-start(bf16[4,96,1152]{2,1,0:T(8,128)(2,1)S(1)} %dynamic-slice_bitcast_fusion.6), channel_id=1, source_target_pairs={{0,1},{1,0},{2,3},{3,2},{4,5},{5,4},{6,7},{7,6},{8,9},{9,8},{10,11... | collective-permute-start | bytes 2654216 | tf_op jit(solution)/shard_map/ppermute | solution.py:261
  (258 other events, 2721.2 us)

commit v2 on v1

--- a/solution.py
+++ b/solution.py
@@ -725,6 +725,7 @@
     delta_toff = column_sum(delta_tside)
     lmix_sum = core_sum(place, pooled_low, delta_lside)
     delta_loff = column_sum(delta_lside)
+    mixer_pending = summed(place, (tmix_sum, lmix_sum), False)
     delta_second = delta_three + right_product(delta_tside, full_tmix)
     delta_pooled = delta_four + right_product(delta_lside, full_lmix)
 
@@ -765,7 +766,7 @@
     delta_two, delta_gain_two, delta_shift_two = pull_two(delta_second)
     delta_lowered = delta_two.astype(jnp.bfloat16)
     down_sum = core_sum(place, activated, delta_lowered)
-    down_pending = summed(place, (tmix_sum, lmix_sum, down_sum), False)
+    down_pending = summed(place, (down_sum,), True)
     delta_dbias = column_sum(delta_lowered)
     delta_activated = right_product(delta_lowered, full_down)
     delta_upper = (delta_activated * slope_upper).astype(jnp.bfloat16)
@@ -820,7 +821,8 @@
     (kernel_one_grad,) = shared(place, one_pending, delta_context)
     (kernel_two_grad,) = shared(place, two_pending, delta_context)
     (gin_grad,) = shared(place, gin_pending, delta_mixed)
-    tmix_grad, lmix_grad, down_grad = shared(place, down_pending, delta_mixed)
+    tmix_grad, lmix_grad = shared(place, mixer_pending, delta_context)
+    (down_grad,) = shared(place, down_pending, delta_mixed)
     (up_grad,) = shared(place, up_pending, delta_mixed)
     (output_grad,) = shared(place, output_pending, delta_mixed)
     (project_grad,) = shared(place, project_pending)

time: 914 us -> 958 us (1.048)
  waiting for transfers between devices: 442 us -> 467 us
  starting transfers between devices: 156 us -> 167 us
  local copies, waits for them, and re-layouts: 66.7 us -> 77.4 us
    ppermute x125 -> x132, waiting for transfers between devices: 442 us -> 467 us  [exchange(): return lax.ppermute(value, axis, pairs)]
    ppermute x125 -> x132, starting transfers between devices: 156 us -> 167 us  [exchange(): return lax.ppermute(value, axis, pairs)]
  transfers between devices with their start and end apart: 125 -> 132, of which waited for: 55 -> 58; matrix products, arithmetic and copies ran while one was open for 13% -> 13% of each run, Pallas kernels for 6% -> 6%
where the time goes in v2:
time: 958 us; the launch traced here: 948 us
  waiting for transfers between devices  467 us (49%)
  starting transfers between devices  167 us (17%)
  matrix products  108 us (11%)
  Pallas kernels  78.2 us (8%)
  local copies, waits for them, and re-layouts  77.4 us (8%)
  other arithmetic  45.8 us (5%)
    ppermute x132, waiting for transfers between devices, exchange(): return lax.ppermute(value, axis, pairs)  467 us
    ppermute x132, starting transfers between devices, exchange(): return lax.ppermute(value, axis, pairs)  167 us
    dot_general x20, matrix products, left_product(): lax.dot_general(left, right, (((0,), (0,)), ((), ())), preferred_element_...  56.6 us
    pallas_call x7, Pallas kernels, put_together(): pl.pallas_call(body, out_shape=[jax.ShapeDtypeStruct((blocks, count, 2 *...  40.5 us
    dot_general x10, matrix products, right_product(): lax.dot_general(left, right, (((1,), (1,)), ((), ())), preferred_element_...  25.4 us
    pallas_call x1, Pallas kernels, recurrent_forward(): pl.pallas_call(body, grid=(letter_slots,), in_specs=[pl.BlockSpec((1, row...  20.9 us
  transfers between devices with their start and end apart: 132, of which 58 were waited for; matrix products, arithmetic and copies ran while one was open for 13% of the time, Pallas kernels for 6%

profile of v2, /device:TPU:0, one launch (start us, length us, event | category | flops | bytes accessed | tf_op | source)
XLA Modules:
  0.0 948.2 jit_solution(11349256333818611269)
XLA Ops:
  2.7 4.1 collective-permute-start.27
  22.4 3.6 collective-permute-start.34
  30.4 11.2 %collective-permute-start.1 = (bf16[96,1152]{1,0:T(8,128)(2,1)S(1)}, bf16[96,1152]{1,0:T(8,128)(2,1)S(1)}, u32[]{:S(2)}, u32[]{:S(2)}) collective-permute-start(bf16[96,1152]{1,0:T(8,128)(2,1)S(1)} %get-tuple-element.214), channel_id=1, source_target_pairs={{0,4},{1,5},{2,6},{3,7},{4,0},{5,1},{6,2},{7,3},{8,12},{9,13},{10,... | collective-permute-start | bytes 663560 | tf_op jit(solution)/shard_map/ppermute | solution.py:261
  44.9 7.2 collective-permute-start.38
  53.2 15.0 %collective-permute-done.1 = bf16[96,1152]{1,0:T(8,128)(2,1)S(1)} collective-permute-done((bf16[96,1152]{1,0:T(8,128)(2,1)S(1)}, bf16[96,1152]{1,0:T(8,128)(2,1)S(1)}, u32[]{:S(2)}, u32[]{:S(2)}) %collective-permute-start.1) | collective-permute-done | bytes 221216 | tf_op jit(solution)/shard_map/ppermute | solution.py:261
  69.9 8.0 collective-permute-done.39
  78.9 12.7 %collective-permute-start.20 = (bf16[96,1536]{1,0:T(8,128)(2,1)S(1)}, bf16[96,1536]{1,0:T(8,128)(2,1)S(1)}, u32[]{:S(2)}, u32[]{:S(2)}) collective-permute-start(bf16[96,1536]{1,0:T(8,128)(2,1)S(1)} %constant_dynamic-slice_fusion.4), channel_id=1, source_target_pairs={{0,2},{1,3},{2,0},{3,1},{4,6},{5,7},{6,4},{7,5},{8,10},{9,11},{10,... | collective-permute-start | bytes 884744 | tf_op jit(solution)/shard_map/ppermute | solution.py:261
  91.7 4.3 collective-permute-done.49
  97.0 17.5 %collective-permute-start.14 = (bf16[480,384]{1,0:T(8,128)(2,1)S(1)}, bf16[480,384]{1,0:T(8,128)(2,1)S(1)}, u32[]{:S(2)}, u32[]{:S(2)}) collective-permute-start(bf16[480,384]{1,0:T(8,128)(2,1)S(1)} %get-tuple-element.197), channel_id=1, source_target_pairs={{0,2},{1,3},{2,0},{3,1},{4,6},{5,7},{6,4},{7,5},{8,10},{9,11},{10,... | collective-permute-start | bytes 1105928 | tf_op jit(solution)/shard_map/ppermute | solution.py:261
  115.6 5.6 collective-permute-done.21
  124.0 19.2 %collective-permute-done.15 = bf16[480,384]{1,0:T(8,128)(2,1)S(1)} collective-permute-done((bf16[480,384]{1,0:T(8,128)(2,1)S(1)}, bf16[480,384]{1,0:T(8,128)(2,1)S(1)}, u32[]{:S(2)}, u32[]{:S(2)}) %collective-permute-start.15) | collective-permute-done | bytes 368672 | tf_op jit(solution)/shard_map/ppermute | solution.py:261
  147.0 9.2 collective-permute-done.35.refs_1_
  158.0 9.4 collective-permute-done.29.refs_1_
  170.8 15.7 %collective-permute-done.3.refs_1_ = bf16[4,96,1152]{2,1,0:T(8,128)(2,1)} collective-permute-done((bf16[4,96,1152]{2,1,0:T(8,128)(2,1)S(1)}, bf16[4,96,1152]{2,1,0:T(8,128)(2,1)}, u32[]{:S(2)}, u32[]{:S(2)}) %collective-permute-start.3) | collective-permute-done | bytes 884768 | tf_op jit(solution)/shard_map/ppermute | solution.py:261
  192.9 12.4 %collective-permute-done.51.refs_1_ = bf16[4,96,1152]{2,1,0:T(8,128)(2,1)S(1)} collective-permute-done((bf16[4,96,1152]{2,1,0:T(8,128)(2,1)S(1)}, bf16[4,96,1152]{2,1,0:T(8,128)(2,1)S(1)}, u32[]{:S(2)}, u32[]{:S(2)}) %collective-permute-start.51) | collective-permute-done | bytes 884768 | tf_op jit(solution)/shard_map/ppermute | solution.py:261
  210.1 14.2 %collective-permute-done.41.refs_1_ = bf16[4,96,1152]{2,1,0:T(8,128)(2,1)S(1)} collective-permute-done((bf16[4,96,1152]{2,1,0:T(8,128)(2,1)S(1)}, bf16[4,96,1152]{2,1,0:T(8,128)(2,1)S(1)}, u32[]{:S(2)}, u32[]{:S(2)}) %collective-permute-start.41) | collective-permute-done | bytes 884768 | tf_op jit(solution)/shard_map/ppermute | solution.py:261
  229.8 47.3 %collective-permute-done.23.refs_1_ = bf16[4,96,1536]{2,1,0:T(8,128)(2,1)S(1)} collective-permute-done((bf16[4,96,1536]{2,1,0:T(8,128)(2,1)S(1)}, bf16[4,96,1536]{2,1,0:T(8,128)(2,1)S(1)}, u32[]{:S(2)}, u32[]{:S(2)}) %collective-permute-start.23) | collective-permute-done | bytes 1179680 | tf_op jit(solution)/shard_map/ppermute | solution.py:261
  279.3 4.2 copy.144
  290.3 16.4 %collective-permute-done.53.refs_3_ = bf16[4,96,1152]{2,1,0:T(8,128)(2,1)} collective-permute-done((bf16[4,96,1152]{2,1,0:T(8,128)(2,1)}, bf16[4,96,1152]{2,1,0:T(8,128)(2,1)}, u32[]{:S(2)}, u32[]{:S(2)}) %collective-permute-start.53) | collective-permute-done | bytes 884768 | tf_op jit(solution)/shard_map/ppermute | solution.py:261
  307.6 17.2 %collective-permute-done.43.refs_3_ = bf16[4,96,1152]{2,1,0:T(8,128)(2,1)} collective-permute-done((bf16[4,96,1152]{2,1,0:T(8,128)(2,1)}, bf16[4,96,1152]{2,1,0:T(8,128)(2,1)}, u32[]{:S(2)}, u32[]{:S(2)}) %collective-permute-start.43) | collective-permute-done | bytes 884768 | tf_op jit(solution)/shard_map/ppermute | solution.py:261
  334.4 3.5 put_together.11
  337.9 4.1 put_together.10
  342.0 5.2 put_together.9
  347.2 7.4 put_together.7
  359.5 20.9 %recurrent.1 = (bf16[8,256,1536]{2,1,0:T(8,128)(2,1)}, bf16[8,256,1536]{2,1,0:T(8,128)(2,1)}, bf16[8,256,384]{2,1,0:T(8,128)(2,1)}, bf16[8,256,384]{2,1,0:T(8,128)(2,1)}, f32[256,768]{1,0:T(8,128)}) custom-call(bf16[8,256,768]{2,1,0:T(8,128)(2,1)} %bitcast.421, bf16[8,256,768]{2,1,0:T(8,128)(2,1)} %bitcast.422, bf16[768,2304]{1,0:T(8,128)(2,1)} %bitcast.465, ...), custom_call_target="tpu_custom_call" | custom-call | tf_op jit(solution)/shard_map/recurrent/pallas_call | solution.py:117
  380.4 7.0 put_together.13
  387.5 7.0 put_together.12
  400.7 6.3 put_together.8
  409.4 6.3 multiply_convert_fusion.1
  448.8 16.8 %recurrent_back.1 = (bf16[8,256,1152]{2,1,0:T(8,128)(2,1)}, bf16[8,256,1152]{2,1,0:T(8,128)(2,1)}, bf16[8,256,1152]{2,1,0:T(8,128)(2,1)}, bf16[8,256,1152]{2,1,0...) custom-call(bf16[8,256,1536]{2,1,0:T(8,128)(2,1)} %get-tuple-element.65.gates_ahead, ...), custom_call_target="tpu_custom_call" | custom-call | tf_op jit(solution)/shard_map/recurrent_back/pallas_call | solution.py:224
  465.6 9.5 %fusion.6 = bf16[1152,768]{0,1:T(8,128)(2,1)} fusion(bf16[8,256,1152]{2,1,0:T(8,128)(2,1)} %get-tuple-element.69, bf16[8,256,768]{2,0,1:T(8,128)(2,1)} %bitcast.477), kind=kOutput, calls=%fused_computation.29 | convolution fusion | flops 3624763392 | bytes 9633792 | tf_op jit(solution)/shard_map/dot_general | solution.py:24
  475.2 6.2 fusion.7
  481.4 4.3 fusion.24
  485.8 5.7 convolution_add_fusion.2
  525.6 5.6 fusion.13
  562.7 6.0 broadcast_select_fusion
  570.4 3.3 collective-permute-done.69
  577.3 3.4 copy.143
  591.4 5.7 collective-permute-done.72
  601.7 3.8 collective-permute-done.75
  614.5 7.2 collective-permute-done.110
  624.2 4.2 collective-permute-done.102
  633.1 6.9 collective-permute-done.112
  640.7 6.1 collective-permute-done.104
  648.4 4.6 collective-permute-done.114
  671.3 15.7 %collective-permute-done.94 = bf16[8,48,1152]{2,1,0:T(8,128)(2,1)S(1)} collective-permute-done((bf16[8,48,1152]{2,1,0:T(8,128)(2,1)S(1)}, bf16[8,48,1152]{2,1,0:T(8,128)(2,1)S(1)}, u32[]{:S(2)}, u32[]{:S(2)}) %collective-permute-start.94) | collective-permute-done | bytes 884768 | tf_op jit(solution)/shard_map/ppermute | solution.py:261
  687.9 17.5 %collective-permute-done.59 = bf16[8,48,1152]{2,1,0:T(8,128)(2,1)S(1)} collective-permute-done((bf16[8,48,1152]{2,1,0:T(8,128)(2,1)S(1)}, bf16[8,48,1152]{2,1,0:T(8,128)(2,1)S(1)}, u32[]{:S(2)}, u32[]{:S(2)}) %collective-permute-start.59) | collective-permute-done | bytes 884768 | tf_op jit(solution)/shard_map/ppermute | solution.py:261
  707.9 9.4 collective-permute-done.60
  721.9 5.9 collective-permute-done.97
  730.0 3.9 collective-permute-done.62
  735.4 20.0 %collective-permute-done.99 = bf16[48,1152]{1,0:T(8,128)(2,1)S(1)} collective-permute-done((bf16[48,1152]{1,0:T(8,128)(2,1)S(1)}, bf16[48,1152]{1,0:T(8,128)(2,1)S(1)}, u32[]{:S(2)}, u32[]{:S(2)}) %collective-permute-start.99) | collective-permute-done | bytes 110624 | tf_op jit(solution)/shard_map/ppermute | solution.py:261
  756.8 3.4 collective-permute-done.64
  761.2 4.1 collective-permute-start.80
  776.3 5.2 collective-permute-done.82
  781.6 11.6 %collective-permute-done.81 = bf16[96,1536]{1,0:T(8,128)(2,1)S(1)} collective-permute-done((bf16[96,1536]{1,0:T(8,128)(2,1)S(1)}, bf16[96,1536]{1,0:T(8,128)(2,1)S(1)}, u32[]{:S(2)}, u32[]{:S(2)}) %collective-permute-start.81) | collective-permute-done | bytes 294944 | tf_op jit(solution)/shard_map/ppermute | solution.py:261
  796.4 24.6 %collective-permute-done.83 = bf16[96,1536]{1,0:T(8,128)(2,1)S(1)} collective-permute-done((bf16[96,1536]{1,0:T(8,128)(2,1)S(1)}, bf16[96,1536]{1,0:T(8,128)(2,1)S(1)}, u32[]{:S(2)}, u32[]{:S(2)}) %collective-permute-start.83) | collective-permute-done | bytes 294944 | tf_op jit(solution)/shard_map/ppermute | solution.py:261
  829.1 4.4 collective-permute-done.90
  833.5 4.9 collective-permute-done.89
  840.0 30.9 %collective-permute-done.91 = bf16[192,384]{1,0:T(8,128)(2,1)S(1)} collective-permute-done((bf16[192,384]{1,0:T(8,128)(2,1)S(1)}, bf16[192,384]{1,0:T(8,128)(2,1)S(1)}, u32[]{:S(2)}, u32[]{:S(2)}) %collective-permute-start.91) | collective-permute-done | bytes 147488 | tf_op jit(solution)/shard_map/ppermute | solution.py:261
  877.3 18.6 %collective-permute-done.126 = bf16[4,96,1152]{2,1,0:T(8,128)(2,1)S(1)} collective-permute-done((bf16[4,96,1152]{2,1,0:T(8,128)(2,1)S(1)}, bf16[4,96,1152]{2,1,0:T(8,128)(2,1)S(1)}, u32[]{:S(2)}, u32[]{:S(2)}) %collective-permute-start.126) | collective-permute-done | bytes 884768 | tf_op jit(solution)/shard_map/ppermute | solution.py:261
  900.4 13.7 %collective-permute-done.118 = bf16[4,96,1152]{2,1,0:T(8,128)(2,1)S(1)} collective-permute-done((bf16[4,96,1152]{2,1,0:T(8,128)(2,1)S(1)}, bf16[4,96,1152]{2,1,0:T(8,128)(2,1)S(1)}, u32[]{:S(2)}, u32[]{:S(2)}) %collective-permute-start.118) | collective-permute-done | bytes 884768 | tf_op jit(solution)/shard_map/ppermute | solution.py:261
  920.2 7.1 collective-permute-done.119
  929.6 7.2 collective-permute-done.120
  938.6 4.3 collective-permute-done.122
  (866 shorter events, 309.2 us)
Async XLA Ops:
  2.7 39.0 %collective-permute-start.27 = (bf16[192,384]{1,0:T(8,128)(2,1)}, bf16[192,384]{1,0:T(8,128)(2,1)S(1)}, u32[]{:S(2)}, u32[]{:S(2)}) collective-permute-start(bf16[192,384]{1,0:T(8,128)(2,1)} %get-tuple-element.222), channel_id=1, source_target_pairs={{0,4},{1,5},{2,6},{3,7},{4,0},{5,1},{6,2},{7,3},{8,12},{9,13},{10,... | collective-permute-start | bytes 442376 | tf_op jit(solution)/shard_map/ppermute | solution.py:261
  6.7 35.2 %collective-permute-start.26 = (bf16[192,384]{1,0:T(8,128)(2,1)}, bf16[192,384]{1,0:T(8,128)(2,1)}, u32[]{:S(2)}, u32[]{:S(2)}) collective-permute-start(bf16[192,384]{1,0:T(8,128)(2,1)} %get-tuple-element.222), channel_id=1, source_target_pairs={{0,2},{1,3},{2,0},{3,1},{4,6},{5,7},{6,4},{7,5},{8,10},{9,11},{10,... | collective-permute-start | bytes 442376 | tf_op jit(solution)/shard_map/ppermute | solution.py:261
  27.0 25.1 %collective-permute-start.2 = (bf16[96,1152]{1,0:T(8,128)(2,1)S(1)}, bf16[96,1152]{1,0:T(8,128)(2,1)S(1)}, u32[]{:S(2)}, u32[]{:S(2)}) collective-permute-start(bf16[96,1152]{1,0:T(8,128)(2,1)S(1)} %get-tuple-element.214), channel_id=1, source_target_pairs={{0,6},{1,7},{2,4},{3,5},{4,2},{5,3},{6,0},{7,1},{8,14},{9,15},{10,... | collective-permute-start | bytes 663560 | tf_op jit(solution)/shard_map/ppermute | solution.py:261
  30.4 37.7 %collective-permute-start.1 = (bf16[96,1152]{1,0:T(8,128)(2,1)S(1)}, bf16[96,1152]{1,0:T(8,128)(2,1)S(1)}, u32[]{:S(2)}, u32[]{:S(2)}) collective-permute-start(bf16[96,1152]{1,0:T(8,128)(2,1)S(1)} %get-tuple-element.214), channel_id=1, source_target_pairs={{0,4},{1,5},{2,6},{3,7},{4,0},{5,1},{6,2},{7,3},{8,12},{9,13},{10,... | collective-permute-start | bytes 663560 | tf_op jit(solution)/shard_map/ppermute | solution.py:261
  41.6 26.6 %collective-permute-start = (bf16[96,1152]{1,0:T(8,128)(2,1)S(1)}, bf16[96,1152]{1,0:T(8,128)(2,1)S(1)}, u32[]{:S(2)}, u32[]{:S(2)}) collective-permute-start(bf16[96,1152]{1,0:T(8,128)(2,1)S(1)} %get-tuple-element.214), channel_id=1, source_target_pairs={{0,2},{1,3},{2,0},{3,1},{4,6},{5,7},{6,4},{7,5},{8,10},{9,11},{10,... | collective-permute-start | bytes 663560 | tf_op jit(solution)/shard_map/ppermute | solution.py:261
  42.0 35.9 %collective-permute-start.39 = (bf16[96,1152]{1,0:T(8,128)(2,1)S(1)}, bf16[96,1152]{1,0:T(8,128)(2,1)S(1)}, u32[]{:S(2)}, u32[]{:S(2)}) collective-permute-start(bf16[96,1152]{1,0:T(8,128)(2,1)S(1)} %get-tuple-element.173), channel_id=1, source_target_pairs={{0,4},{1,5},{2,6},{3,7},{4,0},{5,1},{6,2},{7,3},{8,12},{9,13},{10,... | collective-permute-start | bytes 663560 | tf_op jit(solution)/shard_map/ppermute | solution.py:261
  44.9 34.0 %collective-permute-start.38 = (bf16[96,1152]{1,0:T(8,128)(2,1)S(1)}, bf16[96,1152]{1,0:T(8,128)(2,1)S(1)}, u32[]{:S(2)}, u32[]{:S(2)}) collective-permute-start(bf16[96,1152]{1,0:T(8,128)(2,1)S(1)} %get-tuple-element.173), channel_id=1, source_target_pairs={{0,2},{1,3},{2,0},{3,1},{4,6},{5,7},{6,4},{7,5},{8,10},{9,11},{10,... | collective-permute-start | bytes 663560 | tf_op jit(solution)/shard_map/ppermute | solution.py:261
  52.0 26.8 %collective-permute-start.40 = (bf16[96,1152]{1,0:T(8,128)(2,1)S(1)}, bf16[96,1152]{1,0:T(8,128)(2,1)S(1)}, u32[]{:S(2)}, u32[]{:S(2)}) collective-permute-start(bf16[96,1152]{1,0:T(8,128)(2,1)S(1)} %get-tuple-element.173), channel_id=1, source_target_pairs={{0,6},{1,7},{2,4},{3,5},{4,2},{5,3},{6,0},{7,1},{8,14},{9,15},{10,... | collective-permute-start | bytes 663560 | tf_op jit(solution)/shard_map/ppermute | solution.py:261
  68.2 27.8 %collective-permute-start.49 = (bf16[96,1152]{1,0:T(8,128)(2,1)S(1)}, bf16[96,1152]{1,0:T(8,128)(2,1)S(1)}, u32[]{:S(2)}, u32[]{:S(2)}) collective-permute-start(bf16[96,1152]{1,0:T(8,128)(2,1)S(1)} %get-tuple-element.174), channel_id=1, source_target_pairs={{0,4},{1,5},{2,6},{3,7},{4,0},{5,1},{6,2},{7,3},{8,12},{9,13},{10,... | collective-permute-start | bytes 663560 | tf_op jit(solution)/shard_map/ppermute | solution.py:261
  68.2 28.8 %collective-permute-start.48 = (bf16[96,1152]{1,0:T(8,128)(2,1)S(1)}, bf16[96,1152]{1,0:T(8,128)(2,1)S(1)}, u32[]{:S(2)}, u32[]{:S(2)}) collective-permute-start(bf16[96,1152]{1,0:T(8,128)(2,1)S(1)} %get-tuple-element.174), channel_id=1, source_target_pairs={{0,2},{1,3},{2,0},{3,1},{4,6},{5,7},{6,4},{7,5},{8,10},{9,11},{10,... | collective-permute-start | bytes 663560 | tf_op jit(solution)/shard_map/ppermute | solution.py:261
  78.8 42.3 %collective-permute-start.21 = (bf16[96,1536]{1,0:T(8,128)(2,1)S(1)}, bf16[96,1536]{1,0:T(8,128)(2,1)S(1)}, u32[]{:S(2)}, u32[]{:S(2)}) collective-permute-start(bf16[96,1536]{1,0:T(8,128)(2,1)S(1)} %constant_dynamic-slice_fusion.4), channel_id=1, source_target_pairs={{0,4},{1,5},{2,6},{3,7},{4,0},{5,1},{6,2},{7,3},{8,12},{9,13},{10,... | collective-permute-start | bytes 884744 | tf_op jit(solution)/shard_map/ppermute | solution.py:261
  78.9 43.3 %collective-permute-start.20 = (bf16[96,1536]{1,0:T(8,128)(2,1)S(1)}, bf16[96,1536]{1,0:T(8,128)(2,1)S(1)}, u32[]{:S(2)}, u32[]{:S(2)}) collective-permute-start(bf16[96,1536]{1,0:T(8,128)(2,1)S(1)} %constant_dynamic-slice_fusion.4), channel_id=1, source_target_pairs={{0,2},{1,3},{2,0},{3,1},{4,6},{5,7},{6,4},{7,5},{8,10},{9,11},{10,... | collective-permute-start | bytes 884744 | tf_op jit(solution)/shard_map/ppermute | solution.py:261
  95.9 27.5 %collective-permute-start.22 = (bf16[96,1536]{1,0:T(8,128)(2,1)S(1)}, bf16[96,1536]{1,0:T(8,128)(2,1)S(1)}, u32[]{:S(2)}, u32[]{:S(2)}) collective-permute-start(bf16[96,1536]{1,0:T(8,128)(2,1)S(1)} %constant_dynamic-slice_fusion.4), channel_id=1, source_target_pairs={{0,6},{1,7},{2,4},{3,5},{4,2},{5,3},{6,0},{7,1},{8,14},{9,15},{10,... | collective-permute-start | bytes 884744 | tf_op jit(solution)/shard_map/ppermute | solution.py:261
  97.0 46.2 %collective-permute-start.15 = (bf16[480,384]{1,0:T(8,128)(2,1)S(1)}, bf16[480,384]{1,0:T(8,128)(2,1)S(1)}, u32[]{:S(2)}, u32[]{:S(2)}) collective-permute-start(bf16[480,384]{1,0:T(8,128)(2,1)S(1)} %get-tuple-element.197), channel_id=1, source_target_pairs={{0,4},{1,5},{2,6},{3,7},{4,0},{5,1},{6,2},{7,3},{8,12},{9,13},{10,... | collective-permute-start | bytes 1105928 | tf_op jit(solution)/shard_map/ppermute | solution.py:261
  97.0 47.7 %collective-permute-start.14 = (bf16[480,384]{1,0:T(8,128)(2,1)S(1)}, bf16[480,384]{1,0:T(8,128)(2,1)S(1)}, u32[]{:S(2)}, u32[]{:S(2)}) collective-permute-start(bf16[480,384]{1,0:T(8,128)(2,1)S(1)} %get-tuple-element.197), channel_id=1, source_target_pairs={{0,2},{1,3},{2,0},{3,1},{4,6},{5,7},{6,4},{7,5},{8,10},{9,11},{10,... | collective-permute-start | bytes 1105928 | tf_op jit(solution)/shard_map/ppermute | solution.py:261
  121.2 24.2 %collective-permute-start.16 = (bf16[480,384]{1,0:T(8,128)(2,1)S(1)}, bf16[480,384]{1,0:T(8,128)(2,1)S(1)}, u32[]{:S(2)}, u32[]{:S(2)}) collective-permute-start(bf16[480,384]{1,0:T(8,128)(2,1)S(1)} %get-tuple-element.197), channel_id=1, source_target_pairs={{0,6},{1,7},{2,4},{3,5},{4,2},{5,3},{6,0},{7,1},{8,14},{9,15},{10,... | collective-permute-start | bytes 1105928 | tf_op jit(solution)/shard_map/ppermute | solution.py:261
  122.2 23.2 %collective-permute-start.36 = (bf16[4,48,1152]{2,1,0:T(8,128)(2,1)S(1)}, bf16[4,48,1152]{2,1,0:T(8,128)(2,1)S(1)}, u32[]{:S(2)}, u32[]{:S(2)}) collective-permute-start(bf16[4,48,1152]{2,1,0:T(8,128)(2,1)S(1)} %pad_maximum_fusion.11.refs_0_), channel_id=1, source_target_pairs={{0,8},{8,0},{16,24},{24,16},{1,9},{9,1},{17,25},{25,17},{2,10},{10... | collective-permute-start | bytes 1327112 | tf_op jit(solution)/shard_map/ppermute | solution.py:261
  123.4 32.8 %collective-permute-start.30 = (bf16[4,192,384]{2,1,0:T(8,128)(2,1)S(1)}, bf16[4,192,384]{2,1,0:T(8,128)(2,1)S(1)}, u32[]{:S(2)}, u32[]{:S(2)}) collective-permute-start(bf16[4,192,384]{2,1,0:T(8,128)(2,1)S(1)} %pad_maximum_fusion.9.refs_0_), channel_id=1, source_target_pairs={{0,8},{8,0},{16,24},{24,16},{1,9},{9,1},{17,25},{25,17},{2,10},{10... | collective-permute-start | bytes 1769480 | tf_op jit(solution)/shard_map/ppermute | solution.py:261
  144.7 22.7 %collective-permute-start.29 = (bf16[4,192,384]{2,1,0:T(8,128)(2,1)S(1)}, bf16[4,192,384]{2,1,0:T(8,128)(2,1)S(1)}, u32[]{:S(2)}, u32[]{:S(2)}) collective-permute-start(bf16[4,192,384]{2,1,0:T(8,128)(2,1)S(1)} %pad_maximum_fusion.9.refs_0_), channel_id=1, source_target_pairs={{0,1},{1,0},{2,3},{3,2},{4,5},{5,4},{6,7},{7,6},{8,9},{9,8},{10,11... | collective-permute-start | bytes 1769480 | tf_op jit(solution)/shard_map/ppermute | solution.py:261
  145.4 23.8 %collective-permute-start.6 = (bf16[4,96,1152]{2,1,0:T(8,128)(2,1)S(1)}, bf16[4,96,1152]{2,1,0:T(8,128)(2,1)S(1)}, u32[]{:S(2)}, u32[]{:S(2)}) collective-permute-start(bf16[4,96,1152]{2,1,0:T(8,128)(2,1)S(1)} %pad_maximum_fusion.5.refs_0_), channel_id=1, source_target_pairs={{0,8},{8,0},{16,24},{24,16},{1,9},{9,1},{17,25},{25,17},{2,10},{10... | collective-permute-start | bytes 2654216 | tf_op jit(solution)/shard_map/ppermute | solution.py:261
  145.5 25.3 %collective-permute-start.4 = (bf16[4,96,1152]{2,1,0:T(8,128)(2,1)S(1)}, bf16[4,96,1152]{2,1,0:T(8,128)(2,1)}, u32[]{:S(2)}, u32[]{:S(2)}) collective-permute-start(bf16[4,96,1152]{2,1,0:T(8,128)(2,1)S(1)} %pad_maximum_fusion.5.refs_0_), channel_id=1, source_target_pairs={{0,16},{8,24},{16,0},{24,8},{1,17},{9,25},{17,1},{25,9},{2,18},{10... | collective-permute-start | bytes 2654216 | tf_op jit(solution)/shard_map/ppermute | solution.py:261
  156.2 30.3 %collective-permute-start.3 = (bf16[4,96,1152]{2,1,0:T(8,128)(2,1)S(1)}, bf16[4,96,1152]{2,1,0:T(8,128)(2,1)}, u32[]{:S(2)}, u32[]{:S(2)}) collective-permute-start(bf16[4,96,1152]{2,1,0:T(8,128)(2,1)S(1)} %pad_maximum_fusion.5.refs_0_), channel_id=1, source_target_pairs={{0,1},{1,0},{2,3},{3,2},{4,5},{5,4},{6,7},{7,6},{8,9},{9,8},{10,11... | collective-permute-start | bytes 2654216 | tf_op jit(solution)/shard_map/ppermute | solution.py:261
  167.4 22.6 %collective-permute-start.52 = (bf16[4,96,1152]{2,1,0:T(8,128)(2,1)S(1)}, bf16[4,96,1152]{2,1,0:T(8,128)(2,1)S(1)}, u32[]{:S(2)}, u32[]{:S(2)}) collective-permute-start(bf16[4,96,1152]{2,1,0:T(8,128)(2,1)S(1)} %pad_maximum_fusion.7.refs_0_), channel_id=1, source_target_pairs={{0,16},{8,24},{16,0},{24,8},{1,17},{9,25},{17,1},{25,9},{2,18},{10... | collective-permute-start | bytes 2654216 | tf_op jit(solution)/shard_map/ppermute | solution.py:261
  169.2 36.2 %collective-permute-start.51 = (bf16[4,96,1152]{2,1,0:T(8,128)(2,1)S(1)}, bf16[4,96,1152]{2,1,0:T(8,128)(2,1)S(1)}, u32[]{:S(2)}, u32[]{:S(2)}) collective-permute-start(bf16[4,96,1152]{2,1,0:T(8,128)(2,1)S(1)} %pad_maximum_fusion.7.refs_0_), channel_id=1, source_target_pairs={{0,1},{1,0},{2,3},{3,2},{4,5},{5,4},{6,7},{7,6},{8,9},{9,8},{10,11... | collective-permute-start | bytes 2654216 | tf_op jit(solution)/shard_map/ppermute | solution.py:261
  170.8 36.1 %collective-permute-start.44 = (bf16[4,96,1152]{2,1,0:T(8,128)(2,1)S(1)}, bf16[4,96,1152]{2,1,0:T(8,128)(2,1)S(1)}, u32[]{:S(2)}, u32[]{:S(2)}) collective-permute-start(bf16[4,96,1152]{2,1,0:T(8,128)(2,1)S(1)} %pad_maximum_fusion.6.refs_0_), channel_id=1, source_target_pairs={{0,8},{8,0},{16,24},{24,16},{1,9},{9,1},{17,25},{25,17},{2,10},{10... | collective-permute-start | bytes 2654216 | tf_op jit(solution)/shard_map/ppermute | solution.py:261
  188.2 36.6 %collective-permute-start.24 = (bf16[4,96,1536]{2,1,0:T(8,128)(2,1)S(1)}, bf16[4,96,1536]{2,1,0:T(8,128)(2,1)S(1)}, u32[]{:S(2)}, u32[]{:S(2)}) collective-permute-start(bf16[4,96,1536]{2,1,0:T(8,128)(2,1)S(1)} %pad_maximum_fusion.3.refs_0_), channel_id=1, source_target_pairs={{0,8},{8,0},{16,24},{24,16},{1,9},{9,1},{17,25},{25,17},{2,10},{10... | collective-permute-start | bytes 3538952 | tf_op jit(solution)/shard_map/ppermute | solution.py:261
  190.0 34.3 %collective-permute-start.41 = (bf16[4,96,1152]{2,1,0:T(8,128)(2,1)S(1)}, bf16[4,96,1152]{2,1,0:T(8,128)(2,1)S(1)}, u32[]{:S(2)}, u32[]{:S(2)}) collective-permute-start(bf16[4,96,1152]{2,1,0:T(8,128)(2,1)S(1)} %pad_maximum_fusion.6.refs_0_), channel_id=1, source_target_pairs={{0,1},{1,0},{2,3},{3,2},{4,5},{5,4},{6,7},{7,6},{8,9},{9,8},{10,11... | collective-permute-start | bytes 2654216 | tf_op jit(solution)/shard_map/ppermute | solution.py:261
  205.3 78.1 %collective-permute-start.17 = (bf16[4,480,384]{2,1,0:T(8,128)(2,1)}, bf16[4,480,384]{2,1,0:T(8,128)(2,1)}, u32[]{:S(2)}, u32[]{:S(2)}) collective-permute-start(bf16[4,480,384]{2,1,0:T(8,128)(2,1)} %pad_maximum_fusion.1.refs_0_), channel_id=1, source_target_pairs={{0,1},{1,0},{2,3},{3,2},{4,5},{5,4},{6,7},{7,6},{8,9},{9,8},{10,11... | collective-permute-start | bytes 4423688 | tf_op jit(solution)/shard_map/ppermute | solution.py:261
  208.6 68.6 %collective-permute-start.23 = (bf16[4,96,1536]{2,1,0:T(8,128)(2,1)S(1)}, bf16[4,96,1536]{2,1,0:T(8,128)(2,1)S(1)}, u32[]{:S(2)}, u32[]{:S(2)}) collective-permute-start(bf16[4,96,1536]{2,1,0:T(8,128)(2,1)S(1)} %pad_maximum_fusion.3.refs_0_), channel_id=1, source_target_pairs={{0,1},{1,0},{2,3},{3,2},{4,5},{5,4},{6,7},{7,6},{8,9},{9,8},{10,11... | collective-permute-start | bytes 3538952 | tf_op jit(solution)/shard_map/ppermute | solution.py:261
  224.3 59.6 %collective-permute-start.8 = (bf16[4,96,1152]{2,1,0:T(8,128)(2,1)}, bf16[4,96,1152]{2,1,0:T(8,128)(2,1)}, u32[]{:S(2)}, u32[]{:S(2)}) collective-permute-start(bf16[4,96,1152]{2,1,0:T(8,128)(2,1)} %collective-permute-done.4.refs_2_), channel_id=1, source_target_pairs={{0,8},{8,0},{16,24},{24,16},{1,9},{9,1},{17,25},{25,17},{2,10},{10... | collective-permute-start | bytes 2654216 | tf_op jit(solution)/shard_map/ppermute | solution.py:261
  224.3 61.1 %collective-permute-start.7 = (bf16[4,96,1152]{2,1,0:T(8,128)(2,1)}, bf16[4,96,1152]{2,1,0:T(8,128)(2,1)}, u32[]{:S(2)}, u32[]{:S(2)}) collective-permute-start(bf16[4,96,1152]{2,1,0:T(8,128)(2,1)} %collective-permute-done.3.refs_1_), channel_id=1, source_target_pairs={{0,8},{8,0},{16,24},{24,16},{1,9},{9,1},{17,25},{25,17},{2,10},{10... | collective-permute-start | bytes 2654216 | tf_op jit(solution)/shard_map/ppermute | solution.py:261
  226.4 59.5 %collective-permute-start.5 = (bf16[4,96,1152]{2,1,0:T(8,128)(2,1)}, bf16[4,96,1152]{2,1,0:T(8,128)(2,1)}, u32[]{:S(2)}, u32[]{:S(2)}) collective-permute-start(bf16[4,96,1152]{2,1,0:T(8,128)(2,1)} %collective-permute-done.3.refs_1_), channel_id=1, source_target_pairs={{0,16},{8,24},{16,0},{24,8},{1,17},{9,25},{17,1},{25,9},{2,18},{10... | collective-permute-start | bytes 2654216 | tf_op jit(solution)/shard_map/ppermute | solution.py:261
  277.1 47.7 %collective-permute-start.25 = (bf16[4,96,1536]{2,1,0:T(8,128)(2,1)S(1)}, bf16[4,96,1536]{2,1,0:T(8,128)(2,1)S(1)}, u32[]{:S(2)}, u32[]{:S(2)}) collective-permute-start(bf16[4,96,1536]{2,1,0:T(8,128)(2,1)S(1)} %collective-permute-done.23.refs_1_), channel_id=1, source_target_pairs={{0,8},{8,0},{16,24},{24,16},{1,9},{9,1},{17,25},{25,17},{2,10},{10... | collective-permute-start | bytes 3538952 | tf_op jit(solution)/shard_map/ppermute | solution.py:261
  283.9 22.8 %collective-permute-start.53 = (bf16[4,96,1152]{2,1,0:T(8,128)(2,1)}, bf16[4,96,1152]{2,1,0:T(8,128)(2,1)}, u32[]{:S(2)}, u32[]{:S(2)}) collective-permute-start(bf16[4,96,1152]{2,1,0:T(8,128)(2,1)} %copy-done.88), channel_id=1, source_target_pairs={{0,16},{8,24},{16,0},{24,8},{1,17},{9,25},{17,1},{25,9},{2,18},{10... | collective-permute-start | bytes 2654216 | tf_op jit(solution)/shard_map/ppermute | solution.py:261
  285.4 39.4 %collective-permute-start.43 = (bf16[4,96,1152]{2,1,0:T(8,128)(2,1)}, bf16[4,96,1152]{2,1,0:T(8,128)(2,1)}, u32[]{:S(2)}, u32[]{:S(2)}) collective-permute-start(bf16[4,96,1152]{2,1,0:T(8,128)(2,1)} %copy-done.89), channel_id=1, source_target_pairs={{0,16},{8,24},{16,0},{24,8},{1,17},{9,25},{17,1},{25,9},{2,18},{10... | collective-permute-start | bytes 2654216 | tf_op jit(solution)/shard_map/ppermute | solution.py:261
  286.0 39.4 %collective-permute-start.9 = (bf16[4,96,1152]{2,1,0:T(8,128)(2,1)}, bf16[4,96,1152]{2,1,0:T(8,128)(2,1)S(1)}, u32[]{:S(2)}, u32[]{:S(2)}) collective-permute-start(bf16[4,96,1152]{2,1,0:T(8,128)(2,1)} %collective-permute-done.5.refs_3_), channel_id=1, source_target_pairs={{0,8},{8,0},{16,24},{24,16},{1,9},{9,1},{17,25},{25,17},{2,10},{10... | collective-permute-start | bytes 2654216 | tf_op jit(solution)/shard_map/ppermute | solution.py:261
  289.8 68.1 %collective-permute-start.55 = (bf16[4,96,1152]{2,1,0:T(8,128)(2,1)}, bf16[4,96,1152]{2,1,0:T(8,128)(2,1)}, u32[]{:S(2)}, u32[]{:S(2)}) collective-permute-start(bf16[4,96,1152]{2,1,0:T(8,128)(2,1)} %copy-done.88), channel_id=1, source_target_pairs={{0,8},{8,0},{16,24},{24,16},{1,9},{9,1},{17,25},{25,17},{2,10},{10... | collective-permute-start | bytes 2654216 | tf_op jit(solution)/shard_map/ppermute | solution.py:261
  306.8 51.6 %collective-permute-start.57 = (bf16[4,96,1152]{2,1,0:T(8,128)(2,1)}, bf16[4,96,1152]{2,1,0:T(8,128)(2,1)}, u32[]{:S(2)}, u32[]{:S(2)}) collective-permute-start(bf16[4,96,1152]{2,1,0:T(8,128)(2,1)} %collective-permute-done.53.refs_3_), channel_id=1, source_target_pairs={{0,8},{8,0},{16,24},{24,16},{1,9},{9,1},{17,25},{25,17},{2,10},{10... | collective-permute-start | bytes 2654216 | tf_op jit(solution)/shard_map/ppermute | solution.py:261
  324.9 62.6 %collective-permute-start.45 = (bf16[4,96,1152]{2,1,0:T(8,128)(2,1)}, bf16[4,96,1152]{2,1,0:T(8,128)(2,1)}, u32[]{:S(2)}, u32[]{:S(2)}) collective-permute-start(bf16[4,96,1152]{2,1,0:T(8,128)(2,1)} %copy-done.89), channel_id=1, source_target_pairs={{0,8},{8,0},{16,24},{24,16},{1,9},{9,1},{17,25},{25,17},{2,10},{10... | collective-permute-start | bytes 2654216 | tf_op jit(solution)/shard_map/ppermute | solution.py:261
  324.9 62.6 %collective-permute-start.46 = (bf16[4,96,1152]{2,1,0:T(8,128)(2,1)}, bf16[4,96,1152]{2,1,0:T(8,128)(2,1)}, u32[]{:S(2)}, u32[]{:S(2)}) collective-permute-start(bf16[4,96,1152]{2,1,0:T(8,128)(2,1)} %collective-permute-done.42.refs_2_), channel_id=1, source_target_pairs={{0,8},{8,0},{16,24},{24,16},{1,9},{9,1},{17,25},{25,17},{2,10},{10... | collective-permute-start | bytes 2654216 | tf_op jit(solution)/shard_map/ppermute | solution.py:261
  325.4 62.1 %collective-permute-start.47 = (bf16[4,96,1152]{2,1,0:T(8,128)(2,1)}, bf16[4,96,1152]{2,1,0:T(8,128)(2,1)}, u32[]{:S(2)}, u32[]{:S(2)}) collective-permute-start(bf16[4,96,1152]{2,1,0:T(8,128)(2,1)} %collective-permute-done.43.refs_3_), channel_id=1, source_target_pairs={{0,8},{8,0},{16,24},{24,16},{1,9},{9,1},{17,25},{25,17},{2,10},{10... | collective-permute-start | bytes 2654216 | tf_op jit(solution)/shard_map/ppermute | solution.py:261
  358.0 42.8 %collective-permute-start.18 = (bf16[4,480,384]{2,1,0:T(8,128)(2,1)}, bf16[4,480,384]{2,1,0:T(8,128)(2,1)}, u32[]{:S(2)}, u32[]{:S(2)}) collective-permute-start(bf16[4,480,384]{2,1,0:T(8,128)(2,1)} %pad_maximum_fusion.1.refs_0_), channel_id=1, source_target_pairs={{0,8},{8,0},{16,24},{24,16},{1,9},{9,1},{17,25},{25,17},{2,10},{10... | collective-permute-start | bytes 4423688 | tf_op jit(solution)/shard_map/ppermute | solution.py:261
  358.4 42.3 %collective-permute-start.19 = (bf16[4,480,384]{2,1,0:T(8,128)(2,1)}, bf16[4,480,384]{2,1,0:T(8,128)(2,1)}, u32[]{:S(2)}, u32[]{:S(2)}) collective-permute-start(bf16[4,480,384]{2,1,0:T(8,128)(2,1)} %collective-permute-done.17.refs_1_), channel_id=1, source_target_pairs={{0,8},{8,0},{16,24},{24,16},{1,9},{9,1},{17,25},{25,17},{2,10},{10... | collective-permute-start | bytes 4423688 | tf_op jit(solution)/shard_map/ppermute | solution.py:261
  525.3 62.9 %collective-permute-start.109 = (bf16[768,384]{1,0:T(8,128)(2,1)}, bf16[768,384]{1,0:T(8,128)(2,1)}, u32[]{:S(2)}, u32[]{:S(2)}) collective-permute-start(bf16[768,384]{1,0:T(8,128)(2,1)} %convolution_convert_fusion.5), channel_id=1, source_target_pairs={{0,8},{8,0},{16,24},{24,16},{1,9},{9,1},{17,25},{25,17},{2,10},{10... | collective-permute-start | bytes 1769480 | tf_op jit(solution)/shard_map/ppermute | solution.py:261
  560.1 29.5 %collective-permute-start.108 = (bf16[768,384]{1,0:T(8,128)(2,1)}, bf16[768,384]{1,0:T(8,128)(2,1)}, u32[]{:S(2)}, u32[]{:S(2)}) collective-permute-start(bf16[768,384]{1,0:T(8,128)(2,1)} %convolution_convert_fusion.6), channel_id=1, source_target_pairs={{0,8},{8,0},{16,24},{24,16},{1,9},{9,1},{17,25},{25,17},{2,10},{10... | collective-permute-start | bytes 1769480 | tf_op jit(solution)/shard_map/ppermute | solution.py:261
  560.1 209.9 %collective-permute-start.124 = (bf16[1536,1152]{1,0:T(8,128)(2,1)}, bf16[1536,1152]{1,0:T(8,128)(2,1)}, u32[]{:S(2)}, u32[]{:S(2)}) collective-permute-start(bf16[1536,1152]{1,0:T(8,128)(2,1)} %convolution_convert_fusion), channel_id=1, source_target_pairs={{0,8},{8,0},{16,24},{24,16},{1,9},{9,1},{17,25},{25,17},{2,10},{10... | collective-permute-start | bytes 10616840 | tf_op jit(solution)/shard_map/ppermute | solution.py:261
  568.7 40.8 %collective-permute-start.101 = (bf16[384,1152]{1,0:T(8,128)(2,1)}, bf16[384,1152]{1,0:T(8,128)(2,1)}, u32[]{:S(2)}, u32[]{:S(2)}) collective-permute-start(bf16[384,1152]{1,0:T(8,128)(2,1)} %get-tuple-element.271), channel_id=1, source_target_pairs={{0,8},{8,0},{16,24},{24,16},{1,9},{9,1},{17,25},{25,17},{2,10},{10... | collective-permute-start | bytes 2654216 | tf_op jit(solution)/shard_map/ppermute | solution.py:261
  601.7 60.4 %collective-permute-start.93 = (bf16[768,1152]{1,0:T(8,128)(2,1)S(1)}, bf16[768,1152]{1,0:T(8,128)(2,1)S(1)}, u32[]{:S(2)}, u32[]{:S(2)}) collective-permute-start(bf16[768,1152]{1,0:T(8,128)(2,1)S(1)} %copy-done.59), channel_id=1, source_target_pairs={{0,8},{8,0},{16,24},{24,16},{1,9},{9,1},{17,25},{25,17},{2,10},{10... | collective-permute-start | bytes 5308424 | tf_op jit(solution)/shard_map/ppermute | solution.py:261
  640.1 26.8 %collective-permute-start.78 = (bf16[768,1536]{1,0:T(8,128)(2,1)S(1)}, bf16[768,1536]{1,0:T(8,128)(2,1)S(1)}, u32[]{:S(2)}, u32[]{:S(2)}) collective-permute-start(bf16[768,1536]{1,0:T(8,128)(2,1)S(1)} %copy-done.58), channel_id=1, source_target_pairs={{0,8},{8,0},{16,24},{24,16},{1,9},{9,1},{17,25},{25,17},{2,10},{10... | collective-permute-start | bytes 7077896 | tf_op jit(solution)/shard_map/ppermute | solution.py:261
  640.2 29.1 %collective-permute-start.85 = (bf16[3072,384]{1,0:T(8,128)(2,1)S(1)}, bf16[3072,384]{1,0:T(8,128)(2,1)S(1)}, u32[]{:S(2)}, u32[]{:S(2)}) collective-permute-start(bf16[3072,384]{1,0:T(8,128)(2,1)S(1)} %copy-done.24), channel_id=1, source_target_pairs={{0,8},{8,0},{16,24},{24,16},{1,9},{9,1},{17,25},{25,17},{2,10},{10... | collective-permute-start | bytes 7077896 | tf_op jit(solution)/shard_map/ppermute | solution.py:261
  662.1 133.0 %collective-permute-start.116 = (bf16[1536,1152]{1,0:T(8,128)(2,1)S(1)}, bf16[1536,1152]{1,0:T(8,128)(2,1)S(1)}, u32[]{:S(2)}, u32[]{:S(2)}) collective-permute-start(bf16[1536,1152]{1,0:T(8,128)(2,1)S(1)} %copy-done.15), channel_id=1, source_target_pairs={{0,8},{8,0},{16,24},{24,16},{1,9},{9,1},{17,25},{25,17},{2,10},{10... | collective-permute-start | bytes 10616840 | tf_op jit(solution)/shard_map/ppermute | solution.py:261
  664.5 22.5 %collective-permute-start.94 = (bf16[8,48,1152]{2,1,0:T(8,128)(2,1)S(1)}, bf16[8,48,1152]{2,1,0:T(8,128)(2,1)S(1)}, u32[]{:S(2)}, u32[]{:S(2)}) collective-permute-start(bf16[8,48,1152]{2,1,0:T(8,128)(2,1)S(1)} %dynamic-slice_bitcast_fusion.6), channel_id=1, source_target_pairs={{0,16},{8,24},{16,0},{24,8},{1,17},{9,25},{17,1},{25,9},{2,18},{10... | collective-permute-start | bytes 2654216 | tf_op jit(solution)/shard_map/ppermute | solution.py:261
  666.9 38.5 %collective-permute-start.59 = (bf16[8,48,1152]{2,1,0:T(8,128)(2,1)S(1)}, bf16[8,48,1152]{2,1,0:T(8,128)(2,1)S(1)}, u32[]{:S(2)}, u32[]{:S(2)}) collective-permute-start(bf16[8,48,1152]{2,1,0:T(8,128)(2,1)S(1)} %dynamic-slice_bitcast_fusion.7), channel_id=1, source_target_pairs={{0,16},{8,24},{16,0},{24,8},{1,17},{9,25},{17,1},{25,9},{2,18},{10... | collective-permute-start | bytes 2654216 | tf_op jit(solution)/shard_map/ppermute | solution.py:261
  727.9 32.3 %collective-permute-start.79 = (bf16[4,96,1536]{2,1,0:T(8,128)(2,1)S(1)}, bf16[4,96,1536]{2,1,0:T(8,128)(2,1)S(1)}, u32[]{:S(2)}, u32[]{:S(2)}) collective-permute-start(bf16[4,96,1536]{2,1,0:T(8,128)(2,1)S(1)} %dynamic-slice_bitcast_fusion.3), channel_id=1, source_target_pairs={{0,1},{1,0},{2,3},{3,2},{4,5},{5,4},{6,7},{7,6},{8,9},{9,8},{10,11... | collective-permute-start | bytes 3538952 | tf_op jit(solution)/shard_map/ppermute | solution.py:261
  728.5 32.8 %collective-permute-start.86 = (bf16[8,192,384]{2,1,0:T(8,128)(2,1)S(1)}, bf16[8,192,384]{2,1,0:T(8,128)(2,1)S(1)}, u32[]{:S(2)}, u32[]{:S(2)}) collective-permute-start(bf16[8,192,384]{2,1,0:T(8,128)(2,1)S(1)} %dynamic-slice_bitcast_fusion.2), channel_id=1, source_target_pairs={{0,16},{8,24},{16,0},{24,8},{1,17},{9,25},{17,1},{25,9},{2,18},{10... | collective-permute-start | bytes 3538952 | tf_op jit(solution)/shard_map/ppermute | solution.py:261
  769.0 24.2 %collective-permute-start.81 = (bf16[96,1536]{1,0:T(8,128)(2,1)S(1)}, bf16[96,1536]{1,0:T(8,128)(2,1)S(1)}, u32[]{:S(2)}, u32[]{:S(2)}) collective-permute-start(bf16[96,1536]{1,0:T(8,128)(2,1)S(1)} %get-tuple-element.135), channel_id=1, source_target_pairs={{0,4},{1,5},{2,6},{3,7},{4,0},{5,1},{6,2},{7,3},{8,12},{9,13},{10,... | collective-permute-start | bytes 884744 | tf_op jit(solution)/shard_map/ppermute | solution.py:261
  770.0 51.1 %collective-permute-start.87 = (bf16[4,192,384]{2,1,0:T(8,128)(2,1)S(1)}, bf16[4,192,384]{2,1,0:T(8,128)(2,1)S(1)}, u32[]{:S(2)}, u32[]{:S(2)}) collective-permute-start(bf16[4,192,384]{2,1,0:T(8,128)(2,1)S(1)} %dynamic-slice_bitcast_fusion.8), channel_id=1, source_target_pairs={{0,1},{1,0},{2,3},{3,2},{4,5},{5,4},{6,7},{7,6},{8,9},{9,8},{10,11... | collective-permute-start | bytes 1769480 | tf_op jit(solution)/shard_map/ppermute | solution.py:261
  774.9 97.9 %collective-permute-start.125 = (bf16[8,96,1152]{2,1,0:T(8,128)(2,1)S(1)}, bf16[8,96,1152]{2,1,0:T(8,128)(2,1)S(1)}, u32[]{:S(2)}, u32[]{:S(2)}) collective-permute-start(bf16[8,96,1152]{2,1,0:T(8,128)(2,1)S(1)} %dynamic-slice_bitcast_fusion), channel_id=1, source_target_pairs={{0,16},{8,24},{16,0},{24,8},{1,17},{9,25},{17,1},{25,9},{2,18},{10... | collective-permute-start | bytes 5308424 | tf_op jit(solution)/shard_map/ppermute | solution.py:261
  793.3 27.6 %collective-permute-start.83 = (bf16[96,1536]{1,0:T(8,128)(2,1)S(1)}, bf16[96,1536]{1,0:T(8,128)(2,1)S(1)}, u32[]{:S(2)}, u32[]{:S(2)}) collective-permute-start(bf16[96,1536]{1,0:T(8,128)(2,1)S(1)} %fusion.66), channel_id=1, source_target_pairs={{0,16},{8,24},{16,0},{24,8},{1,17},{9,25},{17,1},{25,9},{2,18},{10... | collective-permute-start | bytes 884744 | tf_op jit(solution)/shard_map/ppermute | solution.py:261
  827.6 47.0 %collective-permute-start.117 = (bf16[8,96,1152]{2,1,0:T(8,128)(2,1)S(1)}, bf16[8,96,1152]{2,1,0:T(8,128)(2,1)S(1)}, u32[]{:S(2)}, u32[]{:S(2)}) collective-permute-start(bf16[8,96,1152]{2,1,0:T(8,128)(2,1)S(1)} %dynamic-slice_bitcast_fusion.1), channel_id=1, source_target_pairs={{0,16},{8,24},{16,0},{24,8},{1,17},{9,25},{17,1},{25,9},{2,18},{10... | collective-permute-start | bytes 5308424 | tf_op jit(solution)/shard_map/ppermute | solution.py:261
  838.5 32.5 %collective-permute-start.91 = (bf16[192,384]{1,0:T(8,128)(2,1)S(1)}, bf16[192,384]{1,0:T(8,128)(2,1)S(1)}, u32[]{:S(2)}, u32[]{:S(2)}) collective-permute-start(bf16[192,384]{1,0:T(8,128)(2,1)S(1)} %fusion.93), channel_id=1, source_target_pairs={{0,16},{8,24},{16,0},{24,8},{1,17},{9,25},{17,1},{25,9},{2,18},{10... | collective-permute-start | bytes 442376 | tf_op jit(solution)/shard_map/ppermute | solution.py:261
  873.3 22.6 %collective-permute-start.126 = (bf16[4,96,1152]{2,1,0:T(8,128)(2,1)S(1)}, bf16[4,96,1152]{2,1,0:T(8,128)(2,1)S(1)}, u32[]{:S(2)}, u32[]{:S(2)}) collective-permute-start(bf16[4,96,1152]{2,1,0:T(8,128)(2,1)S(1)} %dynamic-slice_bitcast_fusion.4), channel_id=1, source_target_pairs={{0,1},{1,0},{2,3},{3,2},{4,5},{5,4},{6,7},{7,6},{8,9},{9,8},{10,11... | collective-permute-start | bytes 2654216 | tf_op jit(solution)/shard_map/ppermute | solution.py:261
  875.4 38.6 %collective-permute-start.118 = (bf16[4,96,1152]{2,1,0:T(8,128)(2,1)S(1)}, bf16[4,96,1152]{2,1,0:T(8,128)(2,1)S(1)}, u32[]{:S(2)}, u32[]{:S(2)}) collective-permute-start(bf16[4,96,1152]{2,1,0:T(8,128)(2,1)S(1)} %dynamic-slice_bitcast_fusion.5), channel_id=1, source_target_pairs={{0,1},{1,0},{2,3},{3,2},{4,5},{5,4},{6,7},{7,6},{8,9},{9,8},{10,11... | collective-permute-start | bytes 2654216 | tf_op jit(solution)/shard_map/ppermute | solution.py:261
  896.2 22.3 %collective-permute-start.127 = (bf16[96,1152]{1,0:T(8,128)(2,1)S(1)}, bf16[96,1152]{1,0:T(8,128)(2,1)S(1)}, u32[]{:S(2)}, u32[]{:S(2)}) collective-permute-start(bf16[96,1152]{1,0:T(8,128)(2,1)S(1)} %get-tuple-element.146), channel_id=1, source_target_pairs={{0,2},{1,3},{2,0},{3,1},{4,6},{5,7},{6,4},{7,5},{8,10},{9,11},{10,... | collective-permute-start | bytes 663560 | tf_op jit(solution)/shard_map/ppermute | solution.py:261
  (249 other events, 2769.0 us)
